TPU v7x, 32 devices: a whole 2x2x4 slice. The times are simulated.
32 devices in a mesh: fsdp: 8 (over y, x, core), ctx: 4 (over z).
Axes of the slice: x: 2, y: 2, z: 4, core: 2. Of those that a mesh axis runs over, the one named last changes fastest.
Arguments:
- hidden_in: bfloat16 [8, 512, 1024], P('fsdp', 'ctx'), may hold values from -6 to 6
- encoder_states: bfloat16 [8, 2048, 1024], P('fsdp', 'ctx'), may hold values from -6 to 6
- segment_ids: int32 [8, 512], P('fsdp'), may hold values from 0 to 3, never falling along the last dimension, each value on 1 to 256 neighbouring positions
- encoder_docs: int32 [8, 2048], P('fsdp'), may hold values from 0 to 3, as said below
- self_query: bfloat16 [1024, 1024], P('fsdp'), may hold values from -0.046875 to 0.046875
- self_key: bfloat16 [1024, 1024], P('fsdp'), may hold values from -0.1875 to 0.1875
- self_value: bfloat16 [1024, 1024], P('fsdp'), may hold values from -0.1875 to 0.1875
- self_out: bfloat16 [1024, 1024], P('fsdp'), may hold values from -3 to 3
- cross_query: bfloat16 [1024, 1024], P('fsdp'), may hold values from -0.046875 to 0.046875
- cross_key: bfloat16 [1024, 1024], P('fsdp'), may hold values from -0.1875 to 0.1875
- cross_value: bfloat16 [1024, 1024], P('fsdp'), may hold values from -0.1875 to 0.1875
- cross_out: bfloat16 [1024, 1024], P('fsdp'), may hold values from -3 to 3
- feed_gate: bfloat16 [1024, 2816], P('fsdp'), may hold values from -0.1875 to 0.1875
- feed_up: bfloat16 [1024, 2816], P('fsdp'), may hold values from -0.1875 to 0.1875
- feed_down: bfloat16 [2816, 1024], P('fsdp'), may hold values from -0.109375 to 0.109375
- norm_self: bfloat16 [1024], P('fsdp'), may hold values from 0.25 to 1.75
- norm_cross: bfloat16 [1024], P('fsdp'), may hold values from 0.25 to 1.75
- norm_feed: bfloat16 [1024], P('fsdp'), may hold values from 0.25 to 1.75
- bias_table: bfloat16 [512], P('fsdp'), may hold values from -4 to 4
- out_grad: bfloat16 [8, 512, 1024], P('fsdp', 'ctx'), may hold values from -6 to 6
Outputs:
- layer_out: bfloat16 [8, 512, 1024], P('fsdp', 'ctx')
- hidden_grad: float32 [8, 512, 1024], P('fsdp', 'ctx')
- encoder_grad: float32 [8, 2048, 1024], P('fsdp', 'ctx')
- grad_self_query: float32 [1024, 1024], P('fsdp')
- grad_self_key: float32 [1024, 1024], P('fsdp')
- grad_self_value: float32 [1024, 1024], P('fsdp')
- grad_self_out: float32 [1024, 1024], P('fsdp')
- grad_cross_query: float32 [1024, 1024], P('fsdp')
- grad_cross_key: float32 [1024, 1024], P('fsdp')
- grad_cross_value: float32 [1024, 1024], P('fsdp')
- grad_cross_out: float32 [1024, 1024], P('fsdp')
- grad_feed_gate: float32 [1024, 2816], P('fsdp')
- grad_feed_up: float32 [1024, 2816], P('fsdp')
- grad_feed_down: float32 [2816, 1024], P('fsdp')
- grad_norm_self: float32 [1024], P('fsdp')
- grad_norm_cross: float32 [1024], P('fsdp')
- grad_norm_feed: float32 [1024], P('fsdp')
- grad_bias_table: float32 [512], P('fsdp')
Inputs may be any that keep to these rules, and one draw needn't show every extreme that they name: `segment_ids`: within a sequence the ids never fall; each of the 4 documents has 1 to 256 tokens, and one has exactly 256. `encoder_docs`: in each sequence the encoder states form 4 aligned blocks of 512, one block for each document id, in an order that differs by sequence.
All inputs are finite; a program needn't handle non-finite values.
Results may differ from a plain program's by a relative error of at most 0.025.
The roundings to bfloat16 on the way count: a program that leaves them out, or rounds other values in their place, can miss the bound.
Values may be sent and summed in bfloat16 or wider, within the bound.
A program may use at most 192 MiB of HBM per device.

v0:
```python
import math

import jax
import jax.numpy as jnp
from jax import lax
from jax.sharding import PartitionSpec as P

H = 16
HD = 64
BUCKETS = 32


bucket_edges = (19, 21, 24, 27, 31, 35, 40, 46, 52, 59, 67, 77, 87, 99, 113)
epsilon = 1e-06
masked_value = -1e30
highest = lax.Precision.HIGHEST


def normalize(values, gain_vector):
    inverse_root = lax.rsqrt(jnp.mean(values * values, axis=-1, keepdims=True) + epsilon)
    return values * inverse_root * gain_vector


def norm_back(values, gain_vector, grad_normed):
    unused, pullback = jax.vjp(normalize, values, gain_vector)
    return pullback(grad_normed)


def product(left_side, right_side):
    return jnp.dot(left_side, right_side, preferred_element_type=jnp.float32)


def product_left(left_side, right_side):
    return lax.dot_general(
        left_side, right_side, (((0,), (0,)), ((), ())), preferred_element_type=jnp.float32
    )


def product_right(left_side, right_side):
    return lax.dot_general(
        left_side, right_side, (((1,), (1,)), ((), ())), preferred_element_type=jnp.float32
    )


def bucket_onehot(distance):
    bucket_index = jnp.minimum(distance, 16)
    for threshold in bucket_edges:
        bucket_index = bucket_index + (distance >= threshold).astype(jnp.int32)
    return (bucket_index[:, :, None] == jnp.arange(BUCKETS, dtype=jnp.int32)).astype(jnp.bfloat16)


def split_blocks(rows_all):
    total_rows = rows_all.shape[0]
    block_rows = math.gcd(total_rows, 512)
    return (block_rows, rows_all.reshape(total_rows // block_rows, block_rows, H, HD))


def block_logits(query_heads, key_part, allowed, distance, table_rows):
    scores = jnp.einsum("qhd,khd->hqk", query_heads, key_part, preferred_element_type=jnp.float32)
    onehot = None
    if table_rows is not None:
        onehot = bucket_onehot(distance)
        scores = scores + jnp.einsum(
            "qkb,hb->hqk", onehot, table_rows, preferred_element_type=jnp.float32
        )
    return (jnp.where(allowed[None], scores, masked_value), onehot)


def attention_forward(query_heads, key_rows, value_rows, mask_of, table_rows):
    block_rows, key_blocks = split_blocks(key_rows)
    unused, value_blocks = split_blocks(value_rows)
    numbers = jnp.arange(key_blocks.shape[0], dtype=jnp.int32)
    query_count = query_heads.shape[0]

    def total_step(carried, element):
        number, key_part = element
        allowed, distance = mask_of(number, block_rows)

        def total_live_branch(state):
            running, summed = state
            scores, unused_hot = block_logits(query_heads, key_part, allowed, distance, table_rows)
            newest = jnp.maximum(running, jnp.max(scores, axis=-1))
            exp_terms = jnp.where(allowed[None], jnp.exp(scores - newest[..., None]), 0.0)
            return (newest, summed * jnp.exp(running - newest) + jnp.sum(exp_terms, axis=-1))

        return (lax.cond(jnp.any(allowed), total_live_branch, lambda state: state, carried), None)

    start_state = (
        jnp.full((H, query_count), masked_value, jnp.float32),
        jnp.zeros((H, query_count), jnp.float32),
    )
    (running, summed), unused_out = lax.scan(total_step, start_state, (numbers, key_blocks))
    logsum = running + jnp.log(summed)

    def output_step(carried, element):
        number, key_part, value_part = element
        allowed, distance = mask_of(number, block_rows)

        def output_live_branch(state):
            scores, unused_hot = block_logits(query_heads, key_part, allowed, distance, table_rows)
            weights = jnp.where(allowed[None], jnp.exp(scores - logsum[..., None]), 0.0).astype(
                jnp.bfloat16
            )
            return state + jnp.einsum(
                "hqk,khd->qhd", weights, value_part, preferred_element_type=jnp.float32
            )

        return (lax.cond(jnp.any(allowed), output_live_branch, lambda state: state, carried), None)

    output, unused_out = lax.scan(
        output_step,
        jnp.zeros((query_count, H, HD), jnp.float32),
        (numbers, key_blocks, value_blocks),
    )
    return (output, logsum)


def attention_delta(query_heads, key_rows, value_rows, grad_heads, logsum, mask_of, table_rows):
    block_rows, key_blocks = split_blocks(key_rows)
    unused, value_blocks = split_blocks(value_rows)
    numbers = jnp.arange(key_blocks.shape[0], dtype=jnp.int32)
    query_count = query_heads.shape[0]

    def delta_step(carried, element):
        number, key_part, value_part = element
        allowed, distance = mask_of(number, block_rows)

        def delta_live_branch(state):
            scores, unused_hot = block_logits(query_heads, key_part, allowed, distance, table_rows)
            weights = jnp.where(allowed[None], jnp.exp(scores - logsum[..., None]), 0.0)
            grad_weights = jnp.einsum(
                "qhd,khd->hqk", grad_heads, value_part, preferred_element_type=jnp.float32
            )
            return state + jnp.sum(weights * grad_weights, axis=-1)

        return (lax.cond(jnp.any(allowed), delta_live_branch, lambda state: state, carried), None)

    row_delta, unused_out = lax.scan(
        delta_step, jnp.zeros((H, query_count), jnp.float32), (numbers, key_blocks, value_blocks)
    )
    return row_delta


def attention_backward(
    query_heads, key_rows, value_rows, grad_heads, logsum, row_delta, mask_of, table_rows
):
    block_rows, key_blocks = split_blocks(key_rows)
    unused, value_blocks = split_blocks(value_rows)
    numbers = jnp.arange(key_blocks.shape[0], dtype=jnp.int32)
    query_count = query_heads.shape[0]
    part_shape = (block_rows, H, HD)

    def grad_step(carried, element):
        number, key_part, value_part = element
        allowed, distance = mask_of(number, block_rows)

        def grad_live_branch(state):
            grad_query, grad_table = state
            scores, onehot = block_logits(query_heads, key_part, allowed, distance, table_rows)
            weights = jnp.where(allowed[None], jnp.exp(scores - logsum[..., None]), 0.0)
            grad_weights = jnp.einsum(
                "qhd,khd->hqk", grad_heads, value_part, preferred_element_type=jnp.float32
            )
            grad_scores = weights * (grad_weights - row_delta[..., None])
            rounded = grad_scores.astype(jnp.bfloat16)
            grad_query = grad_query + jnp.einsum(
                "hqk,khd->qhd", rounded, key_part, preferred_element_type=jnp.float32
            )
            if table_rows is not None:
                grad_table = grad_table + jnp.einsum(
                    "hqk,qkb->hb", grad_scores, onehot.astype(jnp.float32), precision=highest
                )
            grad_key_part = jnp.einsum(
                "hqk,qhd->khd", rounded, query_heads, preferred_element_type=jnp.float32
            )
            grad_value_part = jnp.einsum(
                "hqk,qhd->khd",
                weights.astype(jnp.bfloat16),
                grad_heads,
                preferred_element_type=jnp.float32,
            )
            return ((grad_query, grad_table), (grad_key_part, grad_value_part))

        def dead_branch(state):
            return (state, (jnp.zeros(part_shape, jnp.float32), jnp.zeros(part_shape, jnp.float32)))

        return lax.cond(jnp.any(allowed), grad_live_branch, dead_branch, carried)

    table_shape = (H, BUCKETS) if table_rows is not None else (1, 1)
    start_state = (
        jnp.zeros((query_count, H, HD), jnp.float32),
        jnp.zeros(table_shape, jnp.float32),
    )
    (grad_query, grad_table), key_parts = lax.scan(
        grad_step, start_state, (numbers, key_blocks, value_blocks)
    )
    total_rows = key_rows.shape[0]
    return (
        grad_query,
        grad_table,
        key_parts[0].reshape(total_rows, H * HD),
        key_parts[1].reshape(total_rows, H * HD),
    )


def on_device(
    hidden_in,
    encoder_states,
    segment_ids,
    encoder_docs,
    self_query,
    self_key,
    self_value,
    self_out,
    cross_query,
    cross_key,
    cross_value,
    cross_out,
    feed_gate,
    feed_up,
    feed_down,
    norm_self,
    norm_cross,
    norm_feed,
    bias_table,
    out_grad,
):
    gathered = (
        lax.all_gather(self_query, "fsdp", axis=0, tiled=True),
        lax.all_gather(self_key, "fsdp", axis=0, tiled=True),
        lax.all_gather(self_value, "fsdp", axis=0, tiled=True),
        lax.all_gather(self_out, "fsdp", axis=0, tiled=True),
        lax.all_gather(cross_query, "fsdp", axis=0, tiled=True),
        lax.all_gather(cross_key, "fsdp", axis=0, tiled=True),
        lax.all_gather(cross_value, "fsdp", axis=0, tiled=True),
        lax.all_gather(cross_out, "fsdp", axis=0, tiled=True),
        lax.all_gather(feed_gate, "fsdp", axis=0, tiled=True),
        lax.all_gather(feed_up, "fsdp", axis=0, tiled=True),
        lax.all_gather(feed_down, "fsdp", axis=0, tiled=True),
        lax.all_gather(norm_self, "fsdp", axis=0, tiled=True),
        lax.all_gather(norm_cross, "fsdp", axis=0, tiled=True),
        lax.all_gather(norm_feed, "fsdp", axis=0, tiled=True),
        lax.all_gather(bias_table, "fsdp", axis=0, tiled=True),
    )
    tokens = hidden_in[0]
    encoded = encoder_states[0]
    segments = segment_ids[0]
    documents = encoder_docs[0]
    tok_rows = tokens.shape[0]
    first_row = lax.axis_index("ctx") * tok_rows
    query_pos = first_row + jnp.arange(tok_rows, dtype=jnp.int32)
    query_seg = lax.dynamic_slice_in_dim(segments, first_row, tok_rows, 0)

    def self_mask(number, block_rows):
        key_pos = number * block_rows + jnp.arange(block_rows, dtype=jnp.int32)
        key_seg = lax.dynamic_slice_in_dim(segments, number * block_rows, block_rows, 0)
        distance = query_pos[:, None] - key_pos[None, :]
        allowed = (distance >= 0) & (query_seg[:, None] == key_seg[None, :])
        return (allowed, jnp.maximum(distance, 0))

    def cross_mask(number, block_rows):
        key_doc = lax.dynamic_slice_in_dim(documents, number * block_rows, block_rows, 0)
        return (query_seg[:, None] == key_doc[None, :], None)

    inputs = tokens.astype(jnp.float32)
    self_normed = normalize(inputs, gathered[11].astype(jnp.float32)).astype(jnp.bfloat16)
    queries = product(self_normed, gathered[0]).astype(jnp.bfloat16)
    key_local = product(self_normed, gathered[1]).astype(jnp.bfloat16)
    value_local = product(self_normed, gathered[2]).astype(jnp.bfloat16)
    key_rows, value_rows = (
        lax.all_gather(key_local, "ctx", axis=0, tiled=True),
        lax.all_gather(value_local, "ctx", axis=0, tiled=True),
    )
    table_rows = gathered[14].reshape(H, BUCKETS)
    query_heads = queries.reshape(tok_rows, H, HD)
    key_heads = key_rows.reshape(-1, H, HD)
    value_heads = value_rows.reshape(-1, H, HD)
    self_heads, self_logsum = attention_forward(
        query_heads, key_heads, value_heads, self_mask, table_rows
    )
    self_attended = self_heads.reshape(tok_rows, H * HD).astype(jnp.bfloat16)
    after_self = inputs + product(self_attended, gathered[3])
    cross_normed = normalize(after_self, gathered[12].astype(jnp.float32)).astype(jnp.bfloat16)
    cross_queries = product(cross_normed, gathered[4]).astype(jnp.bfloat16)
    cross_key_local = product(encoded, gathered[5]).astype(jnp.bfloat16)
    cross_value_local = product(encoded, gathered[6]).astype(jnp.bfloat16)
    cross_keys, cross_values = (
        lax.all_gather(cross_key_local, "ctx", axis=0, tiled=True),
        lax.all_gather(cross_value_local, "ctx", axis=0, tiled=True),
    )
    cross_query_heads = cross_queries.reshape(tok_rows, H, HD)
    cross_key_heads = cross_keys.reshape(-1, H, HD)
    cross_value_heads = cross_values.reshape(-1, H, HD)
    cross_heads, cross_logsum = attention_forward(
        cross_query_heads, cross_key_heads, cross_value_heads, cross_mask, None
    )
    cross_attended = cross_heads.reshape(tok_rows, H * HD).astype(jnp.bfloat16)
    after_cross = after_self + product(cross_attended, gathered[7])
    feed_normed = normalize(after_cross, gathered[13].astype(jnp.float32)).astype(jnp.bfloat16)
    gate_value = product(feed_normed, gathered[8])
    up_value = product(feed_normed, gathered[9])
    hidden_units = (jax.nn.gelu(gate_value, approximate=True) * up_value).astype(jnp.bfloat16)
    layer_out = (after_cross + product(hidden_units, gathered[10])).astype(jnp.bfloat16)
    grad_after = out_grad[0].astype(jnp.float32)
    grad_round = grad_after.astype(jnp.bfloat16)
    grad_feed_down = product_left(hidden_units, grad_round)
    grad_hidden = product_right(grad_round, gathered[10])
    unused, pullback = jax.vjp(
        lambda gate_in, up_in: jax.nn.gelu(gate_in, approximate=True) * up_in, gate_value, up_value
    )
    grad_gate, grad_up = pullback(grad_hidden)
    gate_round = grad_gate.astype(jnp.bfloat16)
    up_round = grad_up.astype(jnp.bfloat16)
    grad_feed_gate = product_left(feed_normed, gate_round)
    grad_feed_up = product_left(feed_normed, up_round)
    grad_feed_normed = product_right(gate_round, gathered[8]) + product_right(up_round, gathered[9])
    grad_cross_side, grad_norm_feed = norm_back(
        after_cross, gathered[13].astype(jnp.float32), grad_feed_normed
    )
    grad_after_cross = grad_after + grad_cross_side
    cross_round = grad_after_cross.astype(jnp.bfloat16)
    grad_cross_out = product_left(cross_attended, cross_round)
    grad_cross_heads = (
        product_right(cross_round, gathered[7]).astype(jnp.bfloat16).reshape(tok_rows, H, HD)
    )
    cross_delta = attention_delta(
        cross_query_heads,
        cross_key_heads,
        cross_value_heads,
        grad_cross_heads,
        cross_logsum,
        cross_mask,
        None,
    )
    grad_cross_q, unused_table, grad_cross_k, grad_cross_v = attention_backward(
        cross_query_heads,
        cross_key_heads,
        cross_value_heads,
        grad_cross_heads,
        cross_logsum,
        cross_delta,
        cross_mask,
        None,
    )
    cross_key_grad, cross_value_grad = (
        lax.psum_scatter(
            grad_cross_k.astype(jnp.bfloat16), "ctx", scatter_dimension=0, tiled=True
        ).astype(jnp.float32),
        lax.psum_scatter(
            grad_cross_v.astype(jnp.bfloat16), "ctx", scatter_dimension=0, tiled=True
        ).astype(jnp.float32),
    )
    cross_key_round = cross_key_grad.astype(jnp.bfloat16)
    cross_value_round = cross_value_grad.astype(jnp.bfloat16)
    grad_cross_key = product_left(encoded, cross_key_round)
    grad_cross_value = product_left(encoded, cross_value_round)
    encoder_grad = product_right(cross_key_round, gathered[5]) + product_right(
        cross_value_round, gathered[6]
    )
    cross_query_round = grad_cross_q.reshape(tok_rows, H * HD).astype(jnp.bfloat16)
    grad_cross_query = product_left(cross_normed, cross_query_round)
    grad_cross_normed = product_right(cross_query_round, gathered[4])
    grad_self_side, grad_norm_cross = norm_back(
        after_self, gathered[12].astype(jnp.float32), grad_cross_normed
    )
    grad_after_self = grad_after_cross + grad_self_side
    self_round = grad_after_self.astype(jnp.bfloat16)
    grad_self_out = product_left(self_attended, self_round)
    grad_self_flat = product_right(self_round, gathered[3]).astype(jnp.bfloat16)
    grad_self_heads = grad_self_flat.reshape(tok_rows, H, HD)
    back_table = gathered[14].reshape(H, BUCKETS)
    self_delta = attention_delta(
        query_heads, key_heads, value_heads, grad_self_heads, self_logsum, self_mask, back_table
    )
    grad_self_q, grad_table, grad_self_k, grad_self_v = attention_backward(
        query_heads,
        key_heads,
        value_heads,
        grad_self_heads,
        self_logsum,
        self_delta,
        self_mask,
        back_table,
    )
    self_key_grad, self_value_grad = (
        lax.psum_scatter(
            grad_self_k.astype(jnp.bfloat16), "ctx", scatter_dimension=0, tiled=True
        ).astype(jnp.float32),
        lax.psum_scatter(
            grad_self_v.astype(jnp.bfloat16), "ctx", scatter_dimension=0, tiled=True
        ).astype(jnp.float32),
    )
    self_key_round = self_key_grad.astype(jnp.bfloat16)
    self_value_round = self_value_grad.astype(jnp.bfloat16)
    self_query_round = grad_self_q.reshape(tok_rows, H * HD).astype(jnp.bfloat16)
    grad_self_query = product_left(self_normed, self_query_round)
    grad_self_key = product_left(self_normed, self_key_round)
    grad_self_value = product_left(self_normed, self_value_round)
    grad_self_normed = (
        product_right(self_query_round, gathered[0])
        + product_right(self_key_round, gathered[1])
        + product_right(self_value_round, gathered[2])
    )
    grad_input_side, grad_norm_self = norm_back(
        inputs, gathered[11].astype(jnp.float32), grad_self_normed
    )
    hidden_grad = grad_after_self + grad_input_side
    grad_bias_table = grad_table.reshape(H * BUCKETS)
    pieces = (
        lax.psum_scatter(
            grad_self_query.astype(jnp.bfloat16), "fsdp", scatter_dimension=0, tiled=True
        ).astype(jnp.float32),
        lax.psum_scatter(
            grad_self_key.astype(jnp.bfloat16), "fsdp", scatter_dimension=0, tiled=True
        ).astype(jnp.float32),
        lax.psum_scatter(
            grad_self_value.astype(jnp.bfloat16), "fsdp", scatter_dimension=0, tiled=True
        ).astype(jnp.float32),
        lax.psum_scatter(
            grad_self_out.astype(jnp.bfloat16), "fsdp", scatter_dimension=0, tiled=True
        ).astype(jnp.float32),
        lax.psum_scatter(
            grad_cross_query.astype(jnp.bfloat16), "fsdp", scatter_dimension=0, tiled=True
        ).astype(jnp.float32),
        lax.psum_scatter(
            grad_cross_key.astype(jnp.bfloat16), "fsdp", scatter_dimension=0, tiled=True
        ).astype(jnp.float32),
        lax.psum_scatter(
            grad_cross_value.astype(jnp.bfloat16), "fsdp", scatter_dimension=0, tiled=True
        ).astype(jnp.float32),
        lax.psum_scatter(
            grad_cross_out.astype(jnp.bfloat16), "fsdp", scatter_dimension=0, tiled=True
        ).astype(jnp.float32),
        lax.psum_scatter(
            grad_feed_gate.astype(jnp.bfloat16), "fsdp", scatter_dimension=0, tiled=True
        ).astype(jnp.float32),
        lax.psum_scatter(
            grad_feed_up.astype(jnp.bfloat16), "fsdp", scatter_dimension=0, tiled=True
        ).astype(jnp.float32),
        lax.psum_scatter(
            grad_feed_down.astype(jnp.bfloat16), "fsdp", scatter_dimension=0, tiled=True
        ).astype(jnp.float32),
        lax.psum_scatter(
            grad_norm_self.astype(jnp.bfloat16), "fsdp", scatter_dimension=0, tiled=True
        ).astype(jnp.float32),
        lax.psum_scatter(
            grad_norm_cross.astype(jnp.bfloat16), "fsdp", scatter_dimension=0, tiled=True
        ).astype(jnp.float32),
        lax.psum_scatter(
            grad_norm_feed.astype(jnp.bfloat16), "fsdp", scatter_dimension=0, tiled=True
        ).astype(jnp.float32),
        lax.psum_scatter(
            grad_bias_table.astype(jnp.bfloat16), "fsdp", scatter_dimension=0, tiled=True
        ).astype(jnp.float32),
    )
    owned = (
        lax.psum(pieces[0].astype(jnp.bfloat16), "ctx").astype(jnp.float32),
        lax.psum(pieces[1].astype(jnp.bfloat16), "ctx").astype(jnp.float32),
        lax.psum(pieces[2].astype(jnp.bfloat16), "ctx").astype(jnp.float32),
        lax.psum(pieces[3].astype(jnp.bfloat16), "ctx").astype(jnp.float32),
        lax.psum(pieces[4].astype(jnp.bfloat16), "ctx").astype(jnp.float32),
        lax.psum(pieces[5].astype(jnp.bfloat16), "ctx").astype(jnp.float32),
        lax.psum(pieces[6].astype(jnp.bfloat16), "ctx").astype(jnp.float32),
        lax.psum(pieces[7].astype(jnp.bfloat16), "ctx").astype(jnp.float32),
        lax.psum(pieces[8].astype(jnp.bfloat16), "ctx").astype(jnp.float32),
        lax.psum(pieces[9].astype(jnp.bfloat16), "ctx").astype(jnp.float32),
        lax.psum(pieces[10].astype(jnp.bfloat16), "ctx").astype(jnp.float32),
        lax.psum(pieces[11].astype(jnp.bfloat16), "ctx").astype(jnp.float32),
        lax.psum(pieces[12].astype(jnp.bfloat16), "ctx").astype(jnp.float32),
        lax.psum(pieces[13].astype(jnp.bfloat16), "ctx").astype(jnp.float32),
        lax.psum(pieces[14].astype(jnp.bfloat16), "ctx").astype(jnp.float32),
    )
    return (
        layer_out[None],
        hidden_grad[None],
        encoder_grad[None],
        owned[0],
        owned[1],
        owned[2],
        owned[3],
        owned[4],
        owned[5],
        owned[6],
        owned[7],
        owned[8],
        owned[9],
        owned[10],
        owned[11],
        owned[12],
        owned[13],
        owned[14],
    )


def solution(mesh):
    in_specs = (
        P("fsdp", "ctx", None),
        P("fsdp", "ctx", None),
        P("fsdp", None),
        P("fsdp", None),
        P("fsdp", None),
        P("fsdp", None),
        P("fsdp", None),
        P("fsdp", None),
        P("fsdp", None),
        P("fsdp", None),
        P("fsdp", None),
        P("fsdp", None),
        P("fsdp", None),
        P("fsdp", None),
        P("fsdp", None),
        P("fsdp"),
        P("fsdp"),
        P("fsdp"),
        P("fsdp"),
        P("fsdp", "ctx", None),
    )
    out_specs = (
        P("fsdp", "ctx", None),
        P("fsdp", "ctx", None),
        P("fsdp", "ctx", None),
        P("fsdp", None),
        P("fsdp", None),
        P("fsdp", None),
        P("fsdp", None),
        P("fsdp", None),
        P("fsdp", None),
        P("fsdp", None),
        P("fsdp", None),
        P("fsdp", None),
        P("fsdp", None),
        P("fsdp", None),
        P("fsdp"),
        P("fsdp"),
        P("fsdp"),
        P("fsdp"),
    )
    return jax.shard_map(
        on_device, mesh=mesh, in_specs=in_specs, out_specs=out_specs, check_vma=False
    )
```

profile of v0, /device:TPU:0, one launch (start us, length us, event | category | flops | bytes accessed | tf_op | source)
XLA Modules:
  0.0 1653.0 jit_solution(9977105895890452251)
XLA Ops:
  43.4 26.7 %all-gather.25.cloned.1.call-done = bf16[1024,1024]{1,0:T(8,128)(2,1)} async-done(((bf16[128,1024]{1,0:T(8,128)(2,1)}), bf16[1024,1024]{1,0:T(8,128)(2,1)}) %all-gather.25.cloned.1.call-update) | async-done | bytes 2097168 | tf_op jit(solution)/shard_map/all_gather | solution.py:231
  74.5 25.4 %all-gather.31.cloned.1.call-done = bf16[1024,1024]{1,0:T(8,128)(2,1)} async-done(((bf16[128,1024]{1,0:T(8,128)(2,1)}), bf16[1024,1024]{1,0:T(8,128)(2,1)}) %all-gather.31.cloned.1.call-update) | async-done | bytes 2097168 | tf_op jit(solution)/shard_map/all_gather | solution.py:234
  103.8 25.6 %all-gather.37.cloned.1.call-done = bf16[1024,1024]{1,0:T(8,128)(2,1)} async-done(((bf16[128,1024]{1,0:T(8,128)(2,1)}), bf16[1024,1024]{1,0:T(8,128)(2,1)}) %all-gather.37.cloned.1.call-update) | async-done | bytes 2097168 | tf_op jit(solution)/shard_map/all_gather | solution.py:235
  249.8 27.5 %all-gather.35.cloned.1.call-done = bf16[1024,1024]{1,0:T(8,128)(2,1)} async-done(((bf16[128,1024]{1,0:T(8,128)(2,1)}), bf16[1024,1024]{1,0:T(8,128)(2,1)}) %all-gather.35.cloned.1.call-update) | async-done | bytes 2097168 | tf_op jit(solution)/shard_map/all_gather | solution.py:233
  279.5 80.5 %all-gather.33.cloned.1.call-done = bf16[2048,1024]{1,0:T(8,128)(2,1)} async-done(((bf16[512,1024]{1,0:T(8,128)(2,1)}), bf16[2048,1024]{1,0:T(8,128)(2,1)}) %all-gather.33.cloned.1.call-update) | async-done | bytes 4194320 | tf_op jit(solution)/shard_map/all_gather | solution.py:288
  381.5 59.9 %all-gather.39.cloned.1.call-done = bf16[2048,1024]{1,0:T(8,128)(2,1)} async-done(((bf16[512,1024]{1,0:T(8,128)(2,1)}), bf16[2048,1024]{1,0:T(8,128)(2,1)}) %all-gather.39.cloned.1.call-update) | async-done | bytes 4194320 | tf_op jit(solution)/shard_map/all_gather | solution.py:289
  519.2 40.3 %all-gather.45.cloned.1.call-done = bf16[1024,2816]{1,0:T(8,128)(2,1)} async-done(((bf16[128,2816]{1,0:T(8,128)(2,1)}), bf16[1024,2816]{1,0:T(8,128)(2,1)}) %all-gather.45.cloned.1.call-update) | async-done | bytes 5767184 | tf_op jit(solution)/shard_map/all_gather | solution.py:238
  564.2 40.3 %all-gather.47.cloned.1.call-done = bf16[2816,1024]{1,0:T(8,128)(2,1)} async-done(((bf16[352,1024]{1,0:T(8,128)(2,1)}), bf16[2816,1024]{1,0:T(8,128)(2,1)}) %all-gather.47.cloned.1.call-update) | async-done | bytes 5767184 | tf_op jit(solution)/shard_map/all_gather | solution.py:239
  640.9 31.1 %while.24 = (s32[]{:T(128)}, f32[128,16,64]{0,2,1:T(8,128)}, bf16[4,512,16,64]{1,3,2,0:T(8,128)(2,1)}, bf16[4,512,16,64]{1,3,2,0:T(8,128)(2,1)}, s32[128]{0:T(12...) while((s32[]{:T(128)}, f32[128,16,64]{0,2,1:T(8,128)}, ...), condition=%wide.region_33.34_spmd, body=%wide.region_29.33_spmd.sunk | while | flops 681836544 | bytes 34931852 | solution.py:194
  717.7 35.2 %conditional.11 = (f32[128,16,64]{0,2,1:T(8,128)}, f32[16,32]{1,0:T(8,128)S(1)}, bf16[512,16,64]{0,2,1:T(8,128)(2,1)}, bf16[512,16,64]{0,2,1:T(8,128)(2,1)}) conditional(s32[]{:T(128)} %convert_element_type.506, (f32[128,16,64]{0,2,1:T(8,128)}, f32[16,32]{1,0:T(8,128)S(1)}) %tuple.133, (pred[128,512]{0,1:T(8,128)(4,1)S(1)}, ...), branch_computations={%region_38.39_spmd, %region_39.40_spmd} | conditional | flops 1157628416 | bytes 139679040 | solution.py:187
  757.6 28.7 %reduce-scatter.24.cloned.1.call-done = bf16[512,1024]{0,1:T(8,128)(2,1)} async-done(((bf16[2048,1024]{0,1:T(8,128)(2,1)}), bf16[512,1024]{0,1:T(8,128)(2,1)}) %reduce-scatter.24.cloned.1.call-update) | async-done | bytes 1048592 | tf_op jit(solution)/shard_map/reduce_scatter | solution.py:346
  794.1 71.6 %reduce-scatter.26.cloned.1.call-done = bf16[512,1024]{0,1:T(8,128)(2,1)} async-done(((bf16[2048,1024]{0,1:T(8,128)(2,1)}), bf16[512,1024]{0,1:T(8,128)(2,1)}) %reduce-scatter.26.cloned.1.call-update) | async-done | bytes 1048592 | tf_op jit(solution)/shard_map/reduce_scatter | solution.py:349
  899.5 25.5 %reduce-scatter.48.cloned.1.call-done = bf16[128,1024]{1,0:T(8,128)(2,1)} async-done(((bf16[512,1024]{1,0:T(8,128)(2,1)}), bf16[128,1024]{1,0:T(8,128)(2,1)}) %reduce-scatter.48.cloned.1.call-update) | async-done | bytes 262160
  969.6 42.6 %reduce-scatter.52.cloned.1.call-done = bf16[128,1024]{1,0:T(8,128)(2,1)} async-done(((bf16[1024,1024]{1,0:T(8,128)(2,1)}), bf16[128,1024]{1,0:T(8,128)(2,1)}) %reduce-scatter.52.cloned.1.call-update) | async-done | bytes 262160
  1014.0 43.2 %reduce-scatter.28.cloned.1.call-done = bf16[128,1024]{1,0:T(8,128)(2,1)} async-done(((bf16[1024,1024]{1,0:T(8,128)(2,1)}), bf16[128,1024]{1,0:T(8,128)(2,1)}) %reduce-scatter.28.cloned.1.call-update) | async-done | bytes 262160 | tf_op jit(solution)/shard_map/reduce_scatter | solution.py:410
  1057.2 44.4 %reduce-scatter.34.cloned.1.call-done = bf16[128,1024]{1,0:T(8,128)(2,1)} async-done(((bf16[1024,1024]{1,0:T(8,128)(2,1)}), bf16[128,1024]{1,0:T(8,128)(2,1)}) %reduce-scatter.34.cloned.1.call-update) | async-done | bytes 262160 | tf_op jit(solution)/shard_map/reduce_scatter | solution.py:419
  1101.6 44.3 %reduce-scatter.36.cloned.1.call-done = bf16[128,1024]{1,0:T(8,128)(2,1)} async-done(((bf16[1024,1024]{1,0:T(8,128)(2,1)}), bf16[128,1024]{1,0:T(8,128)(2,1)}) %reduce-scatter.36.cloned.1.call-update) | async-done | bytes 262160 | tf_op jit(solution)/shard_map/reduce_scatter | solution.py:422
  1145.9 44.4 %reduce-scatter.38.cloned.1.call-done = bf16[128,1024]{1,0:T(8,128)(2,1)} async-done(((bf16[1024,1024]{1,0:T(8,128)(2,1)}), bf16[128,1024]{1,0:T(8,128)(2,1)}) %reduce-scatter.38.cloned.1.call-update) | async-done | bytes 262160 | tf_op jit(solution)/shard_map/reduce_scatter | solution.py:431
  1190.3 44.3 %reduce-scatter.30.cloned.1.call-done = bf16[128,1024]{1,0:T(8,128)(2,1)} async-done(((bf16[1024,1024]{1,0:T(8,128)(2,1)}), bf16[128,1024]{1,0:T(8,128)(2,1)}) %reduce-scatter.30.cloned.1.call-update) | async-done | bytes 262160 | tf_op jit(solution)/shard_map/reduce_scatter | solution.py:413
  1234.6 44.3 %reduce-scatter.32.cloned.1.call-done = bf16[128,1024]{1,0:T(8,128)(2,1)} async-done(((bf16[1024,1024]{1,0:T(8,128)(2,1)}), bf16[128,1024]{1,0:T(8,128)(2,1)}) %reduce-scatter.32.cloned.1.call-update) | async-done | bytes 262160 | tf_op jit(solution)/shard_map/reduce_scatter | solution.py:416
  1278.8 62.5 %reduce-scatter.40.cloned.1.call-done = bf16[128,2816]{1,0:T(8,128)(2,1)} async-done(((bf16[1024,2816]{1,0:T(8,128)(2,1)}), bf16[128,2816]{1,0:T(8,128)(2,1)}) %reduce-scatter.40.cloned.1.call-update) | async-done | bytes 720912 | tf_op jit(solution)/shard_map/reduce_scatter | solution.py:434
  1341.3 62.5 %reduce-scatter.42.cloned.1.call-done = bf16[128,2816]{1,0:T(8,128)(2,1)} async-done(((bf16[1024,2816]{1,0:T(8,128)(2,1)}), bf16[128,2816]{1,0:T(8,128)(2,1)}) %reduce-scatter.42.cloned.1.call-update) | async-done | bytes 720912 | tf_op jit(solution)/shard_map/reduce_scatter | solution.py:437
  1403.8 62.3 %reduce-scatter.44.cloned.1.call-done = bf16[352,1024]{1,0:T(8,128)(2,1)} async-done(((bf16[2816,1024]{1,0:T(8,128)(2,1)}), bf16[352,1024]{1,0:T(8,128)(2,1)}) %reduce-scatter.44.cloned.1.call-update) | async-done | bytes 720912 | tf_op jit(solution)/shard_map/reduce_scatter | solution.py:440
  1511.6 116.9 %all-reduce.10.cloned.1.call-done = (bf16[128,1024]{0,1:T(8,128)(2,1)}, bf16[128,1024]{0,1:T(8,128)(2,1)}, bf16[128,1024]{1,0:T(8,128)(2,1)}, bf16[128,1024]{1,0...) async-done(((bf16[128,1024]{0,1:T(8,128)(2,1)}, ...) | async-done | bytes 4259856 | tf_op jit(solution)/shard_map/psum | solution.py:462
  (510 shorter events, 665.2 us)
Async XLA Ops:
  10.6 178.4 %all-gather.23.cloned.1.call-start = ((), (), s32[]{:S(2)}) async-start(), calls=%async_computation.17 | async-start | bytes 1310720 | tf_op jit(solution)/shard_map/all_gather | solution.py:271
  43.4 175.1 %all-gather.27.cloned.1.call-start = ((), (), s32[]{:S(2)}) async-start(), calls=%async_computation.19 | async-start | bytes 1310720 | tf_op jit(solution)/shard_map/all_gather | solution.py:272
  73.7 203.6 %all-gather.35.cloned.1.call-start = ((), (), s32[]{:S(2)}) async-start(), calls=%async_computation.23 | async-start | bytes 2359296 | tf_op jit(solution)/shard_map/all_gather | solution.py:233
  74.4 285.6 %all-gather.33.cloned.1.call-start = ((), (), s32[]{:S(2)}) async-start(), calls=%async_computation.22 | async-start | bytes 5242880 | tf_op jit(solution)/shard_map/all_gather | solution.py:288
  103.8 337.7 %all-gather.39.cloned.1.call-start = ((), (), s32[]{:S(2)}) async-start(), calls=%async_computation.25 | async-start | bytes 5242880 | tf_op jit(solution)/shard_map/all_gather | solution.py:289
  133.2 363.8 %all-gather.41.cloned.1.call-start = ((), (), s32[]{:S(2)}) async-start(), calls=%async_computation.26 | async-start | bytes 2359296 | tf_op jit(solution)/shard_map/all_gather | solution.py:236
  133.8 380.8 %all-gather.43.cloned.1.call-start = ((), (), s32[]{:S(2)}) async-start(), calls=%async_computation.27 | async-start | bytes 6488064 | tf_op jit(solution)/shard_map/all_gather | solution.py:237
  134.6 425.0 %all-gather.45.cloned.1.call-start = ((), (), s32[]{:S(2)}) async-start(), calls=%async_computation.28 | async-start | bytes 6488064 | tf_op jit(solution)/shard_map/all_gather | solution.py:238
  135.1 469.3 %all-gather.47.cloned.1.call-start = ((), (), s32[]{:S(2)}) async-start(), calls=%async_computation.29 | async-start | bytes 6488064 | tf_op jit(solution)/shard_map/all_gather | solution.py:239
  135.7 650.6 %reduce-scatter.24.cloned.1.call-start = ((), (), s32[]{:S(2)}) async-start(), calls=%async_computation.30 | async-start | bytes 5242880 | tf_op jit(solution)/shard_map/reduce_scatter | solution.py:346
  681.1 184.7 %reduce-scatter.26.cloned.1.call-start = ((), (), s32[]{:S(2)}) async-start(), calls=%async_computation.31 | async-start | bytes 5242880 | tf_op jit(solution)/shard_map/reduce_scatter | solution.py:349
  690.4 205.9 %reduce-scatter.46.cloned.1.call-start = ((), (), s32[]{:S(2)}) async-start(), calls=%async_computation.41 | async-start | bytes 1310720
  757.5 210.2 %reduce-scatter.50.cloned.1.call-start = ((), (), s32[]{:S(2)}) async-start(), calls=%async_computation.43 | async-start | bytes 2359296
  794.1 218.1 %reduce-scatter.52.cloned.1.call-start = ((), (), s32[]{:S(2)}) async-start(), calls=%async_computation.44 | async-start | bytes 2359296
  873.6 183.6 %reduce-scatter.28.cloned.1.call-start = ((), (), s32[]{:S(2)}) async-start(), calls=%async_computation.32 | async-start | bytes 2359296 | tf_op jit(solution)/shard_map/reduce_scatter | solution.py:410
  877.4 224.2 %reduce-scatter.34.cloned.1.call-start = ((), (), s32[]{:S(2)}) async-start(), calls=%async_computation.35 | async-start | bytes 2359296 | tf_op jit(solution)/shard_map/reduce_scatter | solution.py:419
  880.5 265.4 %reduce-scatter.36.cloned.1.call-start = ((), (), s32[]{:S(2)}) async-start(), calls=%async_computation.36 | async-start | bytes 2359296 | tf_op jit(solution)/shard_map/reduce_scatter | solution.py:422
  882.7 307.6 %reduce-scatter.38.cloned.1.call-start = ((), (), s32[]{:S(2)}) async-start(), calls=%async_computation.37 | async-start | bytes 2359296 | tf_op jit(solution)/shard_map/reduce_scatter | solution.py:431
  884.8 349.7 %reduce-scatter.30.cloned.1.call-start = ((), (), s32[]{:S(2)}) async-start(), calls=%async_computation.33 | async-start | bytes 2359296 | tf_op jit(solution)/shard_map/reduce_scatter | solution.py:413
  899.5 379.4 %reduce-scatter.32.cloned.1.call-start = ((), (), s32[]{:S(2)}) async-start(), calls=%async_computation.34 | async-start | bytes 2359296 | tf_op jit(solution)/shard_map/reduce_scatter | solution.py:416
  928.1 413.3 %reduce-scatter.40.cloned.1.call-start = ((), (), s32[]{:S(2)}) async-start(), calls=%async_computation.38 | async-start | bytes 6488064 | tf_op jit(solution)/shard_map/reduce_scatter | solution.py:434
  932.3 471.5 %reduce-scatter.42.cloned.1.call-start = ((), (), s32[]{:S(2)}) async-start(), calls=%async_computation.39 | async-start | bytes 6488064 | tf_op jit(solution)/shard_map/reduce_scatter | solution.py:437
  937.6 528.6 %reduce-scatter.44.cloned.1.call-start = ((), (), s32[]{:S(2)}) async-start(), calls=%async_computation.40 | async-start | bytes 6488064 | tf_op jit(solution)/shard_map/reduce_scatter | solution.py:440
  943.0 685.6 %all-reduce.10.cloned.1.call-start = ((), (), s32[]{:S(2)}) async-start(), calls=%async_computation.45 | async-start | bytes 8519680 | tf_op jit(solution)/shard_map/psum | solution.py:462
  (103 other events, 4166.8 us)
Sparse Core Ops, SparseCore 0:
  9.9 30.4 all-gather.20
  42.3 27.7 all-gather.24
  131.1 27.8 all-gather.18
  161.0 27.9 all-gather.22
  279.3 80.7 all-gather.32
  362.2 79.2 all-gather.38
  471.4 43.1 all-gather.42
  516.3 43.1 all-gather.44
  561.3 43.1 all-gather.46
  681.2 105.0 reduce-scatter.23
  788.4 77.2 reduce-scatter.25
  868.5 27.7 reduce-scatter.45
  928.1 39.6 reduce-scatter.49
  971.1 41.0 reduce-scatter.51
  1016.1 41.0 reduce-scatter.27
  1060.5 41.0 reduce-scatter.33
  1104.8 41.0 reduce-scatter.35
  1149.2 41.0 reduce-scatter.37
  1193.4 41.0 reduce-scatter.29
  1237.7 41.0 reduce-scatter.31
  1282.3 59.0 reduce-scatter.39
  1344.8 59.0 reduce-scatter.41
  1407.1 59.0 reduce-scatter.43
  1470.7 157.8 all-reduce.9
  (7 shorter events, 189.5 us)
where the time goes:
time: 1660 us; the launch traced here: 1650 us
  waiting for transfers between devices  1190 us (72%)
  matrix products  176 us (11%)
  local copies, waits for them, and re-layouts  139 us (8%)
  blocking collectives  66.1 us (4%)
  other arithmetic  42 us (3%)
  loops' own time  23.9 us (1%)
  between operations  18.2 us (1%)
    psum x1, waiting for transfers between devices, on_device(): lax.psum(pieces[5].astype(jnp.bfloat16), 'ctx').astype(jnp.float32)  117 us
    unnamed x35, waiting for transfers between devices  111 us
    all_gather x1, waiting for transfers between devices, on_device(): lax.all_gather(cross_key_local, 'ctx', axis=0, tiled=True)  80.5 us
    reduce_scatter x1, waiting for transfers between devices, on_device(): lax.psum_scatter(grad_cross_v.astype(jnp.bfloat16), 'ctx', scatter_dimens...  71.6 us
    reduce_scatter x1, waiting for transfers between devices, on_device(): lax.psum_scatter(grad_feed_up.astype(jnp.bfloat16), 'fsdp', scatter_dimen...  62.5 us
    reduce_scatter x1, waiting for transfers between devices, on_device(): lax.psum_scatter(grad_feed_gate.astype(jnp.bfloat16), 'fsdp', scatter_dim...  62.5 us
    reduce_scatter x1, waiting for transfers between devices, on_device(): lax.psum_scatter(grad_feed_down.astype(jnp.bfloat16), 'fsdp', scatter_dim...  62.3 us
    all_gather x1, waiting for transfers between devices, on_device(): lax.all_gather(cross_value_local, 'ctx', axis=0, tiled=True)  59.9 us
  transfers between devices with their start and end apart: 31, of which 29 were waited for; matrix products, arithmetic and copies ran while one was open for 16% of the time, Pallas kernels for 0%

commit v1 on v0

--- a/solution.py
+++ b/solution.py
@@ -1,13 +1,18 @@
+import functools
 import math
 
 import jax
 import jax.numpy as jnp
 from jax import lax
+from jax.experimental import pallas as pl
+from jax.experimental.pallas import tpu as pltpu
 from jax.sharding import PartitionSpec as P
 
 H = 16
 HD = 64
 BUCKETS = 32
+DOCS = 4
+MESH = pl.DeviceIdType.MESH
 
 
 bucket_edges = (19, 21, 24, 27, 31, 35, 40, 46, 52, 59, 67, 77, 87, 99, 113)
@@ -492,6 +497,734 @@
     )
 
 
+def place():
+    rank = lax.axis_index("fsdp")
+    core = lax.rem(rank, 2)
+    along_x = lax.rem(lax.div(rank, 2), 2)
+    along_y = lax.div(rank, 4)
+    return (rank, core, along_x, along_y, lax.axis_index("ctx"))
+
+
+def greet(partners):
+    barrier = pltpu.get_barrier_semaphore()
+    for partner in partners:
+        pl.semaphore_signal(barrier, inc=1, device_id=partner, device_id_type=MESH)
+    pl.semaphore_wait(barrier, len(partners))
+
+
+def remote(source, target, send_sem, recv_sem, device):
+    return pltpu.make_async_remote_copy(
+        src_ref=source,
+        dst_ref=target,
+        send_sem=send_sem,
+        recv_sem=recv_sem,
+        device_id=device,
+        device_id_type=MESH,
+    )
+
+
+class Gather:
+    def __init__(self, owns, fulls, send_sems, recv_sems, local_sems):
+        rank, core, along_x, along_y, depth = place()
+        self.owns, self.fulls = owns, fulls
+        self.send_sems, self.recv_sems, self.local_sems = send_sems, recv_sems, local_sems
+        self.rank = rank
+        self.by_x = rank + 2 - 4 * along_x
+        self.by_y = rank + 4 - 8 * along_y
+        self.diag = self.by_x + 4 - 8 * along_y
+        self.to_x = (self.by_x, depth)
+        self.to_y = (self.by_y, depth)
+        self.to_core = (rank + 1 - 2 * core, depth)
+        self.shift = 1 - 2 * core
+
+    def rows(self, number, slot, half):
+        full = self.fulls[number]
+        if half is None:
+            return full.at[slot]
+        size = full.shape[1] // 2
+        return full.at[slot, pl.ds(half * size, size)]
+
+    def copy(self, number, kind, slot, half, device, own=False):
+        target = self.rows(number, slot, half)
+        return remote(
+            self.owns[number] if own else target,
+            target,
+            self.send_sems.at[number, kind],
+            self.recv_sems.at[number, kind],
+            device,
+        )
+
+    def sent(self, number, kind):
+        slot, half, device = (
+            (self.rank, None, self.to_x),
+            (self.rank, None, self.to_y),
+            (self.rank, None, self.to_core),
+            (self.by_x, 0, self.to_y),
+            (self.by_y, 1, self.to_x),
+            (self.by_x, None, self.to_core),
+            (self.by_y, None, self.to_core),
+            (self.diag, 0, self.to_core),
+            (self.diag, 1, self.to_core),
+        )[kind]
+        return self.copy(number, kind, slot, half, device, kind < 3)
+
+    def landed(self, number, kind):
+        shift = self.shift
+        slot, half, device = (
+            (self.by_x, None, self.to_x),
+            (self.by_y, None, self.to_y),
+            (self.rank + shift, None, self.to_core),
+            (self.diag, 0, self.to_y),
+            (self.diag, 1, self.to_x),
+            (self.by_x + shift, None, self.to_core),
+            (self.by_y + shift, None, self.to_core),
+            (self.diag + shift, 0, self.to_core),
+            (self.diag + shift, 1, self.to_core),
+        )[kind]
+        return self.copy(number, kind, slot, half, device)
+
+    def local(self, number):
+        return pltpu.make_async_copy(
+            self.owns[number], self.fulls[number].at[self.rank], self.local_sems.at[number]
+        )
+
+    def issue(self, number):
+        for kind in range(3):
+            self.sent(number, kind).start()
+        self.local(number).start()
+
+    def relay(self, number):
+        self.landed(number, 0).wait_recv()
+        self.sent(number, 3).start()
+        self.landed(number, 1).wait_recv()
+        self.sent(number, 4).start()
+        self.sent(number, 5).start()
+        self.sent(number, 6).start()
+
+    def spread(self, number):
+        self.landed(number, 3).wait_recv()
+        self.sent(number, 7).start()
+        self.landed(number, 4).wait_recv()
+        self.sent(number, 8).start()
+
+    def finish(self, number):
+        for kind in (2, 5, 6, 7, 8):
+            self.landed(number, kind).wait_recv()
+        for kind in range(9):
+            self.sent(number, kind).wait_send()
+        self.local(number).wait()
+
+
+def column_partners(rank, depth):
+    return [(rank, lax.rem(depth + step, DOCS)) for step in range(1, DOCS)]
+
+
+def gather_kernel(count, *refs):
+    owns, (tokens, cotangent) = refs[:count], refs[count : count + 2]
+    refs = refs[count + 2 :]
+    fulls, (all_tokens, all_cotangent) = refs[:count], refs[count : count + 2]
+    send_sems, recv_sems, local_sems, line_send, line_recv, line_local = refs[count + 2 :]
+    rank, core, along_x, along_y, depth = place()
+    gather = Gather(owns, fulls, send_sems, recv_sems, local_sems)
+    column = column_partners(rank, depth)
+    greet([gather.to_x, gather.to_y, gather.to_core] + column)
+    pairs = ((tokens, all_tokens), (cotangent, all_cotangent))
+    line = []
+    for number, (own, whole) in enumerate(pairs):
+        pltpu.make_async_copy(own, whole.at[depth], line_local.at[number]).start()
+        for step, partner in enumerate(column):
+            send = remote(
+                own, whole.at[depth], line_send.at[number, step], line_recv.at[number, step], partner
+            )
+            send.start()
+            origin = lax.rem(depth + DOCS - 1 - step, DOCS)
+            receive = remote(
+                own, whole.at[origin], line_send.at[number, step], line_recv.at[number, step], partner
+            )
+            line.append((send, receive))
+    for step in range(count + 3):
+        if step < count:
+            gather.issue(step)
+        if 0 <= step - 1 < count:
+            gather.relay(step - 1)
+        if 0 <= step - 2 < count:
+            gather.spread(step - 2)
+        if 0 <= step - 3 < count:
+            gather.finish(step - 3)
+    for number, (own, whole) in enumerate(pairs):
+        pltpu.make_async_copy(own, whole.at[depth], line_local.at[number]).wait()
+    for send, receive in line:
+        receive.wait_recv()
+        send.wait_send()
+
+
+def gather_call(shards, tokens, cotangent):
+    count = len(shards)
+    vmem = pl.BlockSpec(memory_space=pltpu.VMEM)
+    anywhere = pl.BlockSpec(memory_space=pl.ANY)
+    shapes = [jax.ShapeDtypeStruct((8,) + s.shape, s.dtype) for s in shards]
+    shapes += [jax.ShapeDtypeStruct((DOCS,) + s.shape, s.dtype) for s in (tokens, cotangent)]
+    return pl.pallas_call(
+        functools.partial(gather_kernel, count),
+        out_shape=shapes,
+        in_specs=[vmem] * (count + 2),
+        out_specs=[anywhere] * (count + 2),
+        scratch_shapes=[
+            pltpu.SemaphoreType.DMA((count, 9)),
+            pltpu.SemaphoreType.DMA((count, 9)),
+            pltpu.SemaphoreType.DMA((count,)),
+            pltpu.SemaphoreType.DMA((2, DOCS - 1)),
+            pltpu.SemaphoreType.DMA((2, DOCS - 1)),
+            pltpu.SemaphoreType.DMA((2,)),
+        ],
+        compiler_params=pltpu.CompilerParams(collective_id=1, has_side_effects=True),
+        name="gather_all",
+    )(*shards, tokens, cotangent)
+
+
+def add_rows(target, source):
+    rows = target.shape[-2]
+    step = math.gcd(rows, 32)
+
+    def one(index, unused):
+        at = pl.ds(index * step, step)
+        target[at, :] = target[at, :] + source[at, :]
+        return unused
+
+    lax.fori_loop(0, rows // step, one, 0)
+
+
+class Reduce:
+    def __init__(self, grads, outs, buffers, load, send_sems, recv_sems, local_sems):
+        rank, core, along_x, along_y, depth = place()
+        self.grads, self.outs, self.buffers, self.load = grads, outs, buffers, load
+        self.send_sems, self.recv_sems, self.local_sems = send_sems, recv_sems, local_sems
+        self.core, self.along_x, self.along_y = core, along_x, along_y
+        self.block = 2 * along_y + along_x
+        self.to_x = (rank + 2 - 4 * along_x, depth)
+        self.to_y = (rank + 4 - 8 * along_y, depth)
+        self.to_core = (rank + 1 - 2 * core, depth)
+        self.inner = (depth == 1) | (depth == 2)
+        self.to_line = (rank, depth + 1 - 2 * lax.rem(depth, 2))
+        self.to_middle = (rank, 3 - depth)
+        self.partners = [self.to_x, self.to_y, self.to_core, self.to_line, self.to_middle]
+
+    def copy(self, number, kind, source, target, device):
+        return remote(
+            source,
+            target,
+            self.send_sems.at[number, kind],
+            self.recv_sems.at[number, kind],
+            device,
+        )
+
+    def halves(self, number):
+        size = self.grads[number].shape[1] // 2
+        return (pl.ds(0, size), pl.ds(size, size))
+
+    def core_copies(self, number):
+        grad, both = self.grads[number], self.buffers[number][0]
+        return [
+            self.copy(number, q, grad.at[2 * q + 1 - self.core], both.at[q], self.to_core)
+            for q in range(4)
+        ]
+
+    def loads(self, number):
+        grad = self.grads[number]
+        return [
+            pltpu.make_async_copy(
+                grad.at[2 * q + self.core], self.load[number].at[q], self.local_sems.at[number, q]
+            )
+            for q in range(4)
+        ]
+
+    def first_copies(self, number):
+        both, from_x, from_y = self.buffers[number][:3]
+        low, high = self.halves(number)
+        copies = []
+        for other in range(2):
+            copies.append(
+                self.copy(
+                    number,
+                    4 + other,
+                    both.at[2 * other + 1 - self.along_x, low],
+                    from_x.at[other],
+                    self.to_x,
+                )
+            )
+        for other in range(2):
+            copies.append(
+                self.copy(
+                    number,
+                    6 + other,
+                    both.at[2 * (1 - self.along_y) + other, high],
+                    from_y.at[other],
+                    self.to_y,
+                )
+            )
+        return copies
+
+    def second_copies(self, number):
+        both, unused_x, unused_y, late_x, late_y = self.buffers[number][:5]
+        low, high = self.halves(number)
+        return [
+            self.copy(
+                number,
+                8,
+                both.at[2 * (1 - self.along_y) + self.along_x, low],
+                late_y,
+                self.to_y,
+            ),
+            self.copy(
+                number,
+                9,
+                both.at[2 * self.along_y + 1 - self.along_x, high],
+                late_x,
+                self.to_x,
+            ),
+        ]
+
+    def line_copy(self, number):
+        return self.copy(
+            number,
+            10,
+            self.buffers[number][0].at[self.block],
+            self.buffers[number][5],
+            self.to_line,
+        )
+
+    def middle_copy(self, number):
+        return self.copy(
+            number,
+            11,
+            self.buffers[number][0].at[self.block],
+            self.buffers[number][6],
+            self.to_middle,
+        )
+
+    def return_copy(self, number):
+        return self.copy(
+            number,
+            10,
+            self.buffers[number][5],
+            self.buffers[number][5],
+            self.to_line,
+        )
+
+    def write(self, number):
+        return pltpu.make_async_copy(
+            self.buffers[number][5], self.outs[number], self.local_sems.at[number, 4]
+        )
+
+    def stage(self, number, level):
+        both, from_x, from_y, late_x, late_y, on_line, on_middle = self.buffers[number]
+        low, high = self.halves(number)
+        if level == 0:
+            for copy in self.core_copies(number) + self.loads(number):
+                copy.start()
+        elif level == 1:
+            for q, (copy, load) in enumerate(zip(self.core_copies(number), self.loads(number))):
+                copy.wait_recv()
+                load.wait()
+                add_rows(both.at[q], self.load[number].at[q])
+            for copy in self.first_copies(number):
+                copy.start()
+        elif level == 2:
+            copies = self.first_copies(number)
+            for other in range(2):
+                copies[other].wait_recv()
+                copies[other].wait_send()
+                add_rows(both.at[2 * other + self.along_x, low], from_x.at[other])
+            for other in range(2):
+                copies[2 + other].wait_recv()
+                copies[2 + other].wait_send()
+                add_rows(both.at[2 * self.along_y + other, high], from_y.at[other])
+            for copy in self.second_copies(number):
+                copy.start()
+        elif level == 3:
+            to_y, to_x = self.second_copies(number)
+            to_y.wait_recv()
+            add_rows(both.at[self.block, low], late_y)
+            to_x.wait_recv()
+            add_rows(both.at[self.block, high], late_x)
+            to_y.wait_send()
+            to_x.wait_send()
+
+            @pl.when(jnp.logical_not(self.inner))
+            def _():
+                self.line_copy(number).start()
+        elif level == 4:
+
+            @pl.when(self.inner)
+            def _():
+                self.line_copy(number).wait_recv()
+                add_rows(both.at[self.block], on_line)
+                self.middle_copy(number).start()
+        elif level == 5:
+
+            @pl.when(self.inner)
+            def _():
+                middle = self.middle_copy(number)
+                middle.wait_recv()
+                rows = on_line.shape[0]
+                step = math.gcd(rows, 32)
+
+                def one(index, unused):
+                    at = pl.ds(index * step, step)
+                    on_line[at, :] = both[self.block, at, :] + on_middle[at, :]
+                    return unused
+
+                lax.fori_loop(0, rows // step, one, 0)
+                middle.wait_send()
+                self.return_copy(number).start()
+        else:
+            line = self.line_copy(number)
+
+            @pl.when(jnp.logical_not(self.inner))
+            def _():
+                line.wait_send()
+                line.wait_recv()
+
+            @pl.when(self.inner)
+            def _():
+                self.return_copy(number).wait_send()
+
+            for copy in self.core_copies(number):
+                copy.wait_send()
+            self.write(number).start()
+
+    levels = 7
+
+
+def buffer_shapes(rows, width, dtype):
+    return [
+        pltpu.VMEM((4, rows, width), dtype),
+        pltpu.VMEM((2, rows // 2, width), dtype),
+        pltpu.VMEM((2, rows // 2, width), dtype),
+        pltpu.VMEM((rows // 2, width), dtype),
+        pltpu.VMEM((rows // 2, width), dtype),
+        pltpu.VMEM((rows, width), dtype),
+        pltpu.VMEM((rows, width), dtype),
+    ]
+
+
+def reduce_kernel(count, shared, *refs):
+    grads, backs = refs[:count], refs[count : count + 2]
+    refs = refs[count + 2 :]
+    outs, back_outs = refs[:count], refs[count : count + 2]
+    refs = refs[count + 2 :]
+    buffers = [refs[7 * i : 7 * i + 7] for i in range(count)]
+    refs = refs[7 * count :]
+    loads = [refs[shared[i]] for i in range(count)]
+    refs = refs[max(shared) + 1 :]
+    landing, send_sems, recv_sems, local_sems, line_send, line_recv = refs
+    rank, core, along_x, along_y, depth = place()
+    reduce = Reduce(grads, outs, buffers, loads, send_sems, recv_sems, local_sems)
+    column = column_partners(rank, depth)
+    greet([reduce.to_x, reduce.to_y, reduce.to_core] + column)
+    line = []
+    for number, back in enumerate(backs):
+        for step, (unused, partner) in enumerate(column):
+            send = remote(
+                back.at[partner],
+                landing.at[number, step],
+                line_send.at[number, step],
+                line_recv.at[number, step],
+                (rank, partner),
+            )
+            send.start()
+            line.append(send)
+    for step in range(count + reduce.levels - 1):
+        for level in range(reduce.levels):
+            if 0 <= step - level < count:
+                reduce.stage(step - level, level)
+    for copy in line:
+        copy.wait_recv()
+        copy.wait_send()
+    rows = backs[0].shape[1]
+    chunk = math.gcd(rows, 32)
+    for number, back in enumerate(backs):
+
+        def one(index, unused):
+            at = pl.ds(index * chunk, chunk)
+            total = back[depth, at, :].astype(jnp.float32)
+            for step in range(DOCS - 1):
+                total = total + landing[number, step, at, :].astype(jnp.float32)
+            back_outs[number][at, :] = total.astype(jnp.bfloat16)
+            return unused
+
+        lax.fori_loop(0, rows // chunk, one, 0)
+    for number in range(count):
+        reduce.write(number).wait()
+
+
+def reduce_call(grads, backs):
+    count = len(grads)
+    vmem = pl.BlockSpec(memory_space=pltpu.VMEM)
+    anywhere = pl.BlockSpec(memory_space=pl.ANY)
+    scratch, load_shapes, shared = [], [], []
+    for grad in grads:
+        scratch += buffer_shapes(grad.shape[1], grad.shape[2], grad.dtype)
+        shape = ((4,) + grad.shape[1:], grad.dtype)
+        held = [i for i, s in enumerate(load_shapes) if s == shape]
+        if len(held) < 2:
+            shared.append(len(load_shapes))
+            load_shapes.append(shape)
+        else:
+            turns = [i for i in shared if load_shapes[i] == shape]
+            shared.append(held[0] if turns[-1] == held[1] else held[1])
+    scratch += [pltpu.VMEM(*shape) for shape in load_shapes]
+    return pl.pallas_call(
+        functools.partial(reduce_kernel, count, shared),
+        out_shape=[jax.ShapeDtypeStruct(g.shape[1:], g.dtype) for g in grads]
+        + [jax.ShapeDtypeStruct(b.shape[1:], b.dtype) for b in backs],
+        in_specs=[anywhere] * count + [vmem] * 2,
+        out_specs=[anywhere] * count + [vmem] * 2,
+        scratch_shapes=scratch
+        + [
+            pltpu.VMEM((2, DOCS - 1) + backs[0].shape[1:], jnp.bfloat16),
+            pltpu.SemaphoreType.DMA((count, 12)),
+            pltpu.SemaphoreType.DMA((count, 12)),
+            pltpu.SemaphoreType.DMA((count, 5)),
+            pltpu.SemaphoreType.DMA((2, DOCS - 1)),
+            pltpu.SemaphoreType.DMA((2, DOCS - 1)),
+        ],
+        compiler_params=pltpu.CompilerParams(
+            collective_id=2, has_side_effects=True, vmem_limit_bytes=60 * 2**20
+        ),
+        name="reduce_all",
+    )(*grads, *backs)
+
+
+def pack_small(norms, table):
+    rows = [n.astype(jnp.float32) for n in norms]
+    rows.append(jnp.pad(table.astype(jnp.float32), (0, 128 - table.shape[0])))
+    return jnp.pad(jnp.stack(rows), ((0, 12), (0, 0)))
+
+
+def by_document(
+    hidden_in,
+    encoder_states,
+    segment_ids,
+    encoder_docs,
+    self_query,
+    self_key,
+    self_value,
+    self_out,
+    cross_query,
+    cross_key,
+    cross_value,
+    cross_out,
+    feed_gate,
+    feed_up,
+    feed_down,
+    norm_self,
+    norm_cross,
+    norm_feed,
+    bias_table,
+    out_grad,
+):
+    width = hidden_in.shape[2]
+    total = segment_ids.shape[1]
+    most = total // 2
+    encoded = encoder_states[0]
+    small = pack_small((norm_self, norm_cross, norm_feed), bias_table)
+    gathered = gather_call(
+        (
+            small,
+            cross_key,
+            cross_value,
+            self_query,
+            self_key,
+            self_value,
+            self_out,
+            cross_query,
+            cross_out,
+            feed_gate,
+            feed_up,
+            feed_down,
+        ),
+        hidden_in[0],
+        out_grad[0],
+    )
+    smalls = gathered[0]
+    w_ck, w_cv, w_sq, w_sk, w_sv, w_so, w_cq, w_co, w_fg, w_fu, w_fd = (
+        w.reshape(-1, w.shape[2]) for w in gathered[1:12]
+    )
+    all_tokens = gathered[12].reshape(total, width)
+    all_cotangent = gathered[13].reshape(total, width)
+    gain_self, gain_cross, gain_feed = (smalls[:, i].reshape(-1) for i in range(3))
+    table = smalls[:, 3, : bias_table.shape[0]].reshape(H, BUCKETS).astype(jnp.bfloat16)
+
+    document = lax.dynamic_slice_in_dim(
+        encoder_docs[0], lax.axis_index("ctx") * encoded.shape[0], 1, 0
+    )
+    segments = segment_ids[0]
+    start = jnp.sum((segments < document).astype(jnp.int32))
+    length = jnp.sum((segments == document).astype(jnp.int32))
+    row = lax.broadcasted_iota(jnp.int32, (most, total), 0)
+    column = lax.broadcasted_iota(jnp.int32, (most, total), 1)
+    chosen = ((row + start == column) & (row < length)).astype(jnp.bfloat16)
+
+    inputs = product(chosen, all_tokens)
+    grad_after = product(chosen, all_cotangent)
+    grad_round = grad_after.astype(jnp.bfloat16)
+
+    position = jnp.arange(most, dtype=jnp.int32)
+    distance = position[:, None] - position[None, :]
+    causal = (distance >= 0)[None]
+    onehot = bucket_onehot(jnp.maximum(distance, 0))
+
+    def heads(values):
+        return values.reshape(values.shape[0], H, HD)
+
+    def flat(values):
+        return values.reshape(values.shape[0], H * HD).astype(jnp.bfloat16)
+
+    def attend(q, k, v, bias, allowed):
+        scores = jnp.einsum("qhd,khd->hqk", q, k, preferred_element_type=jnp.float32)
+        if bias is not None:
+            scores = jnp.where(allowed, scores + bias, masked_value)
+        p = jax.nn.softmax(scores, axis=-1)
+        out = jnp.einsum(
+            "hqk,khd->qhd", p.astype(jnp.bfloat16), v, preferred_element_type=jnp.float32
+        )
+        return (p, out)
+
+    def attend_back(q, k, v, p, grad):
+        grad_p = jnp.einsum("qhd,khd->hqk", grad, v, preferred_element_type=jnp.float32)
+        grad_s = p * (grad_p - jnp.sum(p * grad_p, axis=-1, keepdims=True))
+        rounded = grad_s.astype(jnp.bfloat16)
+        grad_q = jnp.einsum("hqk,khd->qhd", rounded, k, preferred_element_type=jnp.float32)
+        grad_k = jnp.einsum("hqk,qhd->khd", rounded, q, preferred_element_type=jnp.float32)
+        grad_v = jnp.einsum(
+            "hqk,qhd->khd", p.astype(jnp.bfloat16), grad, preferred_element_type=jnp.float32
+        )
+        return (grad_s, flat(grad_q), flat(grad_k), flat(grad_v))
+
+    self_normed = normalize(inputs, gain_self).astype(jnp.bfloat16)
+    queries = heads(product(self_normed, w_sq).astype(jnp.bfloat16))
+    keys = heads(product(self_normed, w_sk).astype(jnp.bfloat16))
+    values = heads(product(self_normed, w_sv).astype(jnp.bfloat16))
+    bias = jnp.einsum("qkb,hb->hqk", onehot, table, preferred_element_type=jnp.float32)
+    self_p, self_heads = attend(queries, keys, values, bias, causal)
+    self_attended = flat(self_heads)
+    after_self = inputs + product(self_attended, w_so)
+    cross_normed = normalize(after_self, gain_cross).astype(jnp.bfloat16)
+    cross_q = heads(product(cross_normed, w_cq).astype(jnp.bfloat16))
+    cross_k = heads(product(encoded, w_ck).astype(jnp.bfloat16))
+    cross_v = heads(product(encoded, w_cv).astype(jnp.bfloat16))
+    cross_p, cross_heads = attend(cross_q, cross_k, cross_v, None, None)
+    cross_attended = flat(cross_heads)
+    after_cross = after_self + product(cross_attended, w_co)
+    feed_normed = normalize(after_cross, gain_feed).astype(jnp.bfloat16)
+    gate_value = product(feed_normed, w_fg)
+    up_value = product(feed_normed, w_fu)
+
+    def gated(gate_in, up_in):
+        return jax.nn.gelu(gate_in, approximate=True) * up_in
+
+    hidden_units, pullback = jax.vjp(gated, gate_value, up_value)
+    hidden_units = hidden_units.astype(jnp.bfloat16)
+    layer_out = (after_cross + product(hidden_units, w_fd)).astype(jnp.bfloat16)
+
+    grad_fd = product_left(hidden_units, grad_round)
+    grad_gate, grad_up = pullback(product_right(grad_round, w_fd))
+    gate_round = grad_gate.astype(jnp.bfloat16)
+    up_round = grad_up.astype(jnp.bfloat16)
+    grad_fg = product_left(feed_normed, gate_round)
+    grad_fu = product_left(feed_normed, up_round)
+    grad_normed = product_right(gate_round, w_fg) + product_right(up_round, w_fu)
+    side, grad_gain_feed = norm_back(after_cross, gain_feed, grad_normed)
+    grad_after_cross = grad_after + side
+    cross_round = grad_after_cross.astype(jnp.bfloat16)
+    grad_co = product_left(cross_attended, cross_round)
+    grad_heads = heads(product_right(cross_round, w_co).astype(jnp.bfloat16))
+    unused, grad_q, grad_k, grad_v = attend_back(cross_q, cross_k, cross_v, cross_p, grad_heads)
+    grad_ck = product_left(encoded, grad_k)
+    grad_cv = product_left(encoded, grad_v)
+    encoder_grad = product_right(grad_k, w_ck) + product_right(grad_v, w_cv)
+    grad_cq = product_left(cross_normed, grad_q)
+    side, grad_gain_cross = norm_back(after_self, gain_cross, product_right(grad_q, w_cq))
+    grad_after_self = grad_after_cross + side
+    self_round = grad_after_self.astype(jnp.bfloat16)
+    grad_so = product_left(self_attended, self_round)
+    grad_heads = heads(product_right(self_round, w_so).astype(jnp.bfloat16))
+    grad_s, grad_q, grad_k, grad_v = attend_back(queries, keys, values, self_p, grad_heads)
+    grad_table = jnp.einsum(
+        "hqk,qkb->hb", grad_s, onehot.astype(jnp.float32), precision=highest
+    )
+    grad_sq = product_left(self_normed, grad_q)
+    grad_sk = product_left(self_normed, grad_k)
+    grad_sv = product_left(self_normed, grad_v)
+    grad_normed = (
+        product_right(grad_q, w_sq) + product_right(grad_k, w_sk) + product_right(grad_v, w_sv)
+    )
+    side, grad_gain_self = norm_back(inputs, gain_self, grad_normed)
+    hidden_grad = (grad_after_self + side).astype(jnp.bfloat16)
+
+    def back(values):
+        return product_left(chosen, values).astype(jnp.bfloat16).reshape(DOCS, -1, width)
+
+    table_rows = jnp.pad(grad_table.reshape(8, -1), ((0, 0), (0, 64)))
+    small_grads = jnp.stack(
+        [g.reshape(8, 128) for g in (grad_gain_self, grad_gain_cross, grad_gain_feed)]
+        + [table_rows],
+        axis=1,
+    )
+    small_grads = jnp.pad(small_grads, ((0, 0), (0, 12), (0, 0)))
+
+    def shards(grad):
+        return grad.astype(jnp.bfloat16).reshape(8, -1, grad.shape[1])
+
+    names = (
+        grad_fd,
+        grad_fg,
+        grad_fu,
+        grad_co,
+        grad_ck,
+        grad_cv,
+        grad_cq,
+        grad_so,
+        grad_sq,
+        grad_sk,
+        grad_sv,
+    )
+    reduced = reduce_call(
+        tuple(shards(g) for g in names) + (small_grads,), (back(layer_out), back(hidden_grad))
+    )
+    fd, fg, fu, co, ck, cv, cq, so, sq, sk, sv = (r.astype(jnp.float32) for r in reduced[:11])
+    smalls = reduced[11]
+    return (
+        reduced[12][None],
+        reduced[13].astype(jnp.float32)[None],
+        encoder_grad[None],
+        sq,
+        sk,
+        sv,
+        so,
+        cq,
+        ck,
+        cv,
+        co,
+        fg,
+        fu,
+        fd,
+        smalls[0],
+        smalls[1],
+        smalls[2],
+        smalls[3, : bias_table.shape[0]],
+    )
+
+
+def layer(sizes, *args):
+    encoder_states, encoder_docs = args[1], args[3]
+    whole_document = encoder_states.shape[1] * DOCS == encoder_docs.shape[1]
+    if whole_document and sizes["fsdp"] == 8 and sizes["ctx"] == DOCS:
+        return by_document(*args)
+    return on_device(*args)
+
+
 def solution(mesh):
     in_specs = (
         P("fsdp", "ctx", None),
@@ -536,5 +1269,5 @@
         P("fsdp"),
     )
     return jax.shard_map(
-        on_device, mesh=mesh, in_specs=in_specs, out_specs=out_specs, check_vma=False
-    )
+        functools.partial(layer, dict(mesh.shape)), mesh=mesh, in_specs=in_specs, out_specs=out_specs, check_vma=False
+    )

time: 1660 us -> 582 us (0.35)
  waiting for transfers between devices: 1190 us -> 0 us
  Pallas kernels: 0 us -> 347 us
  local copies, waits for them, and re-layouts: 139 us -> 43.9 us
  blocking collectives: 66.1 us -> 0 us
  loops' own time: 23.9 us -> 0 us
  matrix products: 176 us -> 158 us
    reduce_scatter x11 -> x0, waiting for transfers between devices: 553 us -> none  [the longest x1 71.6 us: on_device(): lax.psum_scatter(grad_cross_v.astype(jnp.bfloat16), 'ctx', scatter_dimens...]
    all_gather x15 -> x0, waiting for transfers between devices: 404 us -> none  [the longest x1 80.5 us: on_device(): lax.all_gather(cross_key_local, 'ctx', axis=0, tiled=True)]
    pallas_call x0 -> x2, Pallas kernels: none -> 347 us  [the longest x1 196 us: reduce_call(): pl.pallas_call(functools.partial(reduce_kernel, count, shared), out_shape...]
    psum x1 -> x0, waiting for transfers between devices: 117 us -> none  [on_device(): lax.psum(pieces[5].astype(jnp.bfloat16), 'ctx').astype(jnp.float32)]
    unnamed x35 -> x0, waiting for transfers between devices: 111 us -> none
    all_gather x3 -> x0, blocking collectives: 27.1 us -> none  [the longest x1 10.4 us: on_device(): lax.all_gather(norm_self, 'fsdp', axis=0, tiled=True)]
    unnamed x2 -> x0, blocking collectives: 26.8 us -> none
    another operation x16 -> x1, local copies, waits for them, and re-layouts: 27.4 us -> 0.75 us  [pack_small(): return jnp.pad(jnp.stack(rows), ((0, 12), (0, 0)))]
  transfers between devices with their start and end apart: 31 -> 0, of which waited for: 29 -> 0; matrix products, arithmetic and copies ran while one was open for 16% -> 0% of each run, Pallas kernels for 0% -> 0%
where the time goes in v1:
time: 582 us; the launch traced here: 576 us
  Pallas kernels  347 us (60%)
  matrix products  158 us (27%)
  local copies, waits for them, and re-layouts  43.9 us (8%)
  other arithmetic  25.7 us (4%)
    pallas_call x1, Pallas kernels, reduce_call(): pl.pallas_call(functools.partial(reduce_kernel, count, shared), out_shape...  196 us
    pallas_call x1, Pallas kernels, gather_call(): pl.pallas_call(functools.partial(gather_kernel, count), out_shape=shapes,...  151 us
    dot_general x13, matrix products, product_left(): lax.dot_general(left_side, right_side, (((0,), (0,)), ((), ())), preferre...  40 us
    dot_general x11, matrix products, product_right(): lax.dot_general(left_side, right_side, (((1,), (1,)), ((), ())), preferre...  31.8 us
    dot_general x12, matrix products, product(): return jnp.dot(left_side, right_side, preferred_element_type=jnp.float32)  29.6 us
    convert_element_type x11, other arithmetic, by_document(): r.astype(jnp.float32)  12.8 us
    eq x1, local copies, waits for them, and re-layouts, bucket_onehot(): bucket_index[:, :, None] == jnp.arange(BUCKETS, dtype=jnp.int32)  11.8 us

profile of v1, /device:TPU:0, one launch (start us, length us, event | category | flops | bytes accessed | tf_op | source)
XLA Modules:
  0.0 576.1 jit_solution(3350005067471100408)
XLA Ops:
  2.7 151.0 %gather_all.1 = (f32[8,16,128]{2,1,0:T(8,128)}, bf16[8,128,1024]{2,1,0:T(8,128)(2,1)}, bf16[8,128,1024]{2,1,0:T(8,128)(2,1)}, bf16[8,128,1024]{2,1,0:T(8,128)(2,...) custom-call(f32[16,128]{1,0:T(8,128)} %fusion.89.refs_0_, ...), custom_call_target="tpu_custom_call" | custom-call | tf_op jit(solution)/shard_map/gather_all/pallas_call | solution.py:667
  169.0 11.8 %copy.60 = pred[256,256,32]{1,2,0:T(32,128)(4,1)S(1)} copy(pred[256,256,32]{0,2,1:T(32,128)(4,1)S(1)} %iota_compare_fusion) | data formatting | bytes 4194304 | tf_op jit(solution)/shard_map/eq | solution.py:54
  183.8 5.8 %copy.61 = f32[16,256,256]{1,2,0:T(8,128)} copy(f32[16,256,256]{2,0,1:T(8,128)} %fusion.107) | data formatting | bytes 8388608 | tf_op jit(solution)/shard_map/qkb,hb->hqk/dot_general | solution.py:1109
  197.2 5.5 convolution_convert_fusion.23
  209.0 3.9 convolution_convert_fusion.14
  212.9 6.8 %fusion.106 = (f32[16,256]{1,0:T(8,128)S(1)}, f32[16,256,512]{2,1,0:T(8,128)}) fusion(bf16[256,16,64]{0,2,1:T(8,128)(2,1)} %bitcast.216, bf16[512,16,64]{0,2,1:T(8,128)(2,1)} %bitcast.221), kind=kOutput, calls=%fused_computation.176 | convolution fusion | flops 272630272 | bytes 9977856 | tf_op jit(solution)/shard_map/sub | solution.py:1088
  219.7 3.9 convolution_convert_fusion.15
  223.6 6.1 %fusion.19 = bf16[16,64,256]{2,1,0:T(8,128)(2,1)} fusion(bf16[512,16,64]{0,2,1:T(8,128)(2,1)} %bitcast.288, f32[16,256]{1,0:T(8,128)S(1)} %get-tuple-element.97, bf16[256,16,64]{0,2,1:T(8,128)(2,1)} %bitcast.217, bf16[512,16,64]{0,2,1:T(8,128)(2,1)} %bitcast.222), kind=kOutput, calls=%fused_computation.58 | convolution fusion | flops 543429120 | bytes 3162112 | tf_op jit(solution)/shard_map/hqk,khd->qhd/dot_general | solution.py:1089
  232.6 4.7 fusion.109
  237.4 3.3 fusion.108
  241.3 6.6 %multiply_convert_fusion.1 = (bf16[256,2816]{1,0:T(8,128)(2,1)S(1)}, bf16[256,2816]{1,0:T(8,128)(2,1)S(1)}, bf16[256,2816]{1,0:T(8,128)(2,1)}) fusion(f32[256,2816]{1,0:T(8,128)} %fusion.108, f32[256,2816]{1,0:T(8,128)S(1)} %fusion.109, bf16[2816,1024]{1,0:T(8,128)(2,1)S(1)} %bitcast.273, f32[256,1024]{1,0:T(8,128)S(1)} %fusion.46), kind=kOutput, calls=%fused_computation.25 | convolution fusion | flops 1495400448 | bytes 16908288 | tf_op jit(solution)/shard_map/dot_general | solution.py:45
  247.8 5.4 fusion.110
  260.7 6.1 %multiply_reduce_fusion = (f32[16,256]{1,0:T(8,128)S(1)}, f32[16,256,512]{2,1,0:T(8,128)S(1)}) fusion(f32[16,256,512]{2,1,0:T(8,128)} %get-tuple-element.98, f32[16,256]{1,0:T(8,128)S(1)} %get-tuple-element.97, bf16[256,16,64]{0,2,1:T(8,128)(2,1)} %bitcast.248, bf16[512,16,64]{0,2,1:T(8,128)(2,1)} %bitcast.289), kind=kOutput, calls=%fused_computation.3 | convolution fusion | flops 274722816 | bytes 18382848 | tf_op jit(solution)/shard_map/qhd,khd->hqk/dot_general | solution.py:1095
  274.6 5.8 %fusion.15 = bf16[16,64,512]{2,1,0:T(8,128)(2,1)} fusion(bf16[256,16,64]{0,2,1:T(8,128)(2,1)} %bitcast.249, f32[16,256]{1,0:T(8,128)S(1)} %get-tuple-element.97, bf16[256,16,64]{0,2,1:T(8,128)(2,1)} %bitcast.218, bf16[512,16,64]{0,2,1:T(8,128)(2,1)} %bitcast.223), kind=kOutput, calls=%fused_computation.45 | convolution fusion | flops 543691264 | bytes 3162112 | tf_op jit(solution)/shard_map/hqk,qhd->khd/dot_general | solution.py:1100
  280.3 5.3 add_bitcast_fusion
  293.4 3.5 multiply_reduce_fusion.1
  306.0 5.5 convolution_convert_fusion.17
  316.3 6.2 %convolution_convert_fusion.12 = bf16[512,1024]{1,0:T(8,128)(2,1)} fusion(f32[256,1024]{1,0:T(8,128)} %copy-done.14, bf16[256,2816]{1,0:T(8,128)(2,1)} %get-tuple-element.84, bf16[2816,1024]{1,0:T(8,128)(2,1)} %bitcast.270, s32[256]{0:T(256)S(1)} %iota_add_fusion, pred[256]{0:T(512)(128)(4,1)S(1)} %iota_compare_fusion.4), kind=kOutput, calls=%fused_computation.47 | convolution fusion | flops 1746141184 | bytes 9307392 | tf_op jit(solution)/shard_map/dot_general | solution.py:39
  322.5 8.0 %fusion.22 = f32[16,32]{1,0:T(8,128)S(1)} fusion(f32[16,256,256]{1,2,0:T(8,128)} %copy-done.1, s32[256,256]{0,1:T(8,128)S(1)} %convert_add_fusion), kind=kOutput, calls=%fused_computation.70 | convolution fusion | flops 404750336 | bytes 4458496 | tf_op jit(solution)/shard_map/hqk,qkb->hb/dot_general | solution.py:1154
  333.4 3.5 convolution_convert_fusion.4
  350.7 4.3 convolution_convert_fusion
  355.0 4.2 convolution_convert_fusion.1
  359.2 4.2 convolution_convert_fusion.2
  363.4 195.6 %reduce_all.1 = (bf16[352,1024]{1,0:T(8,128)(2,1)}, bf16[128,2816]{1,0:T(8,128)(2,1)}, bf16[128,2816]{1,0:T(8,128)(2,1)}, bf16[128,1024]{1,0:T(8,128)(2,1)}, bf1...) custom-call(bf16[8,352,1024]{2,1,0:T(8,128)(2,1)} %bitcast.189, ...), custom_call_target="tpu_custom_call" | custom-call | tf_op jit(solution)/shard_map/reduce_all/pallas_call | solution.py:977
  (227 shorter events, 107.8 us)
Async XLA Ops:
  0.7 208.4 %copy-start = (bf16[1,512,1024]{2,1,0:T(8,128)(2,1)S(1)}, bf16[1,512,1024]{2,1,0:T(8,128)(2,1)}, u32[]{:S(2)}) copy-start(bf16[1,512,1024]{2,1,0:T(8,128)(2,1)} %param.21) | copy-start | bytes 3145732
  0.7 154.5 %copy-start.61 = (s32[1,512]{1,0:T(1,128)S(1)}, s32[1,512]{1,0:T(1,128)}, u32[]{:S(2)}) copy-start(s32[1,512]{1,0:T(1,128)} %param.22) | copy-start | bytes 6148
  153.8 6.9 %copy-start.38 = (bf16[8,128,1024]{2,1,0:T(8,128)(2,1)S(1)}, bf16[8,128,1024]{2,1,0:T(8,128)(2,1)}, u32[]{:S(2)}) copy-start(bf16[8,128,1024]{2,1,0:T(8,128)(2,1)} %get-tuple-element.50) | copy-start | bytes 6291460
  160.6 35.6 %copy-start.19 = (bf16[256,1024]{1,0:T(8,128)(2,1)}, bf16[256,1024]{1,0:T(8,128)(2,1)S(1)}, u32[]{:S(2)}) copy-start(bf16[256,1024]{1,0:T(8,128)(2,1)S(1)} %multiply_convert_fusion.5) | copy-start | bytes 1572868
  166.7 23.0 %copy-start.24 = (bf16[256,1024]{0,1:T(8,128)(2,1)}, bf16[256,1024]{0,1:T(8,128)(2,1)S(1)}, u32[]{:S(2)}) copy-start(bf16[256,1024]{0,1:T(8,128)(2,1)S(1)} %copy.58) | copy-start | bytes 1572868
  229.7 7.7 %slice-start.6 = ((s8[5767168]{0:T(1024)(128)(4,1)}), s8[4194304]{0:T(1024)(128)(4,1)S(1)}, s32[]{:S(2)}) async-start(s8[5767168]{0:T(1024)(128)(4,1)} %bitcast.279), calls=%async_computation.6 | async-start | bytes 8388608
  232.4 22.8 %copy-start.14 = (f32[256,1024]{1,0:T(8,128)}, f32[256,1024]{1,0:T(8,128)S(1)}, u32[]{:S(2)}) copy-start(f32[256,1024]{1,0:T(8,128)S(1)} %get-tuple-element.100) | copy-start | bytes 3145732
  232.6 8.6 %slice-start.2 = ((s8[5767168]{0:T(1024)(128)(4,1)}), s8[4194304]{0:T(1024)(128)(4,1)S(1)}, s32[]{:S(2)}) async-start(s8[5767168]{0:T(1024)(128)(4,1)} %bitcast.271), calls=%async_computation.2 | async-start | bytes 8388608
  237.4 15.8 %slice-start.4 = ((s8[5767168]{0:T(1024)(128)(4,1)}), s8[4194304]{0:T(1024)(128)(4,1)S(1)}, s32[]{:S(2)}) async-start(s8[5767168]{0:T(1024)(128)(4,1)} %bitcast.275), calls=%async_computation.4 | async-start | bytes 8388608
  241.2 14.0 %copy-start.12 = (f32[256,1024]{1,0:T(8,128)}, f32[256,1024]{1,0:T(8,128)S(1)}, u32[]{:S(2)}) copy-start(f32[256,1024]{1,0:T(8,128)S(1)} %fusion.46) | copy-start | bytes 3145732
  241.3 12.0 %slice-start.5 = ((s8[5767168]{0:T(1024)(128)(4,1)}), s8[1572864]{0:T(1024)(128)(4,1)S(1)}, s32[]{:S(2)}) async-start(s8[5767168]{0:T(1024)(128)(4,1)} %bitcast.275), calls=%async_computation.5 | async-start | bytes 3145728
  260.7 6.1 %slice-start = ((s8[8388608]{0:T(1024)(128)(4,1)}), s8[4194304]{0:T(1024)(128)(4,1)S(1)}, s32[]{:S(2)}) async-start(s8[8388608]{0:T(1024)(128)(4,1)} %bitcast.190), calls=%async_computation | async-start | bytes 8388608
  260.7 6.3 %slice-start.1 = ((s8[8388608]{0:T(1024)(128)(4,1)}), s8[4194304]{0:T(1024)(128)(4,1)S(1)}, s32[]{:S(2)}) async-start(s8[8388608]{0:T(1024)(128)(4,1)} %bitcast.190), calls=%async_computation.1 | async-start | bytes 8388608
  322.5 8.8 %copy-start.20 = (bf16[256,1024]{1,0:T(8,128)(2,1)S(1)}, bf16[256,1024]{1,0:T(8,128)(2,1)}, u32[]{:S(2)}) copy-start(bf16[256,1024]{1,0:T(8,128)(2,1)} %copy-done.19) | copy-start | bytes 1572868
  322.5 8.8 %copy-start.41 = (bf16[16,64,256]{2,1,0:T(8,128)(2,1)S(1)}, bf16[16,64,256]{2,1,0:T(8,128)(2,1)}, u32[]{:S(2)}) copy-start(bf16[16,64,256]{2,1,0:T(8,128)(2,1)} %convolution_convert_fusion.17) | copy-start | bytes 1572868
  331.3 5.6 copy-start.21
  331.3 5.6 copy-start.28
  333.4 5.6 copy-start.10
  333.4 5.6 copy-start.35
  559.0 6.1 %copy-start.59 = (bf16[128,1024]{1,0:T(8,128)(2,1)S(1)}, bf16[128,1024]{1,0:T(8,128)(2,1)}, u32[]{:S(2)}) copy-start(bf16[128,1024]{1,0:T(8,128)(2,1)} %get-tuple-element.61) | copy-start | bytes 786436
  561.4 6.2 %copy-start.56 = (bf16[128,1024]{1,0:T(8,128)(2,1)S(1)}, bf16[128,1024]{1,0:T(8,128)(2,1)}, u32[]{:S(2)}) copy-start(bf16[128,1024]{1,0:T(8,128)(2,1)} %get-tuple-element.64) | copy-start | bytes 786436
  565.0 5.9 %copy-start.52 = (bf16[128,1024]{1,0:T(8,128)(2,1)S(1)}, bf16[128,1024]{1,0:T(8,128)(2,1)}, u32[]{:S(2)}) copy-start(bf16[128,1024]{1,0:T(8,128)(2,1)} %get-tuple-element.68) | copy-start | bytes 786436
  565.9 5.9 %copy-start.51 = (bf16[128,1024]{1,0:T(8,128)(2,1)S(1)}, bf16[128,1024]{1,0:T(8,128)(2,1)}, u32[]{:S(2)}) copy-start(bf16[128,1024]{1,0:T(8,128)(2,1)} %get-tuple-element.69) | copy-start | bytes 786436
  566.7 8.4 %copy-start.60 = (bf16[128,1024]{1,0:T(8,128)(2,1)S(1)}, bf16[128,1024]{1,0:T(8,128)(2,1)}, u32[]{:S(2)}) copy-start(bf16[128,1024]{1,0:T(8,128)(2,1)} %get-tuple-element.60) | copy-start | bytes 786436
  (48 other events, 156.1 us)

commit v2 on v1

--- a/solution.py
+++ b/solution.py
@@ -47,11 +47,15 @@
     )
 
 
-def bucket_onehot(distance):
+def bucket_of(distance):
     bucket_index = jnp.minimum(distance, 16)
     for threshold in bucket_edges:
         bucket_index = bucket_index + (distance >= threshold).astype(jnp.int32)
-    return (bucket_index[:, :, None] == jnp.arange(BUCKETS, dtype=jnp.int32)).astype(jnp.bfloat16)
+    return bucket_index
+
+
+def bucket_onehot(distance):
+    return (bucket_of(distance)[:, :, None] == jnp.arange(BUCKETS, dtype=jnp.int32)).astype(jnp.bfloat16)
 
 
 def split_blocks(rows_all):
@@ -538,11 +542,12 @@
         self.shift = 1 - 2 * core
 
     def rows(self, number, slot, half):
-        full = self.fulls[number]
+        size = self.owns[number].shape[0]
+        start = pl.multiple_of(slot * size, size)
         if half is None:
-            return full.at[slot]
-        size = full.shape[1] // 2
-        return full.at[slot, pl.ds(half * size, size)]
+            return self.fulls[number].at[pl.ds(start, size)]
+        size = size // 2
+        return self.fulls[number].at[pl.ds(pl.multiple_of(start + half * size, size), size)]
 
     def copy(self, number, kind, slot, half, device, own=False):
         target = self.rows(number, slot, half)
@@ -585,7 +590,7 @@
 
     def local(self, number):
         return pltpu.make_async_copy(
-            self.owns[number], self.fulls[number].at[self.rank], self.local_sems.at[number]
+            self.owns[number], self.rows(number, self.rank, None), self.local_sems.at[number]
         )
 
     def issue(self, number):
@@ -619,67 +624,320 @@
     return [(rank, lax.rem(depth + step, DOCS)) for step in range(1, DOCS)]
 
 
-def gather_kernel(count, *refs):
-    owns, (tokens, cotangent) = refs[:count], refs[count : count + 2]
-    refs = refs[count + 2 :]
-    fulls, (all_tokens, all_cotangent) = refs[:count], refs[count : count + 2]
-    send_sems, recv_sems, local_sems, line_send, line_recv, line_local = refs[count + 2 :]
+def tile(index, size=256):
+    return pl.ds(pl.multiple_of(index * size, size), size)
+
+
+def each(count, body):
+    def one(index, unused):
+        body(index)
+        return unused
+
+    lax.fori_loop(0, count, one, 0)
+
+
+def by_columns(left, right, write):
+    def one(index):
+        at = tile(index)
+        write(at, product(left[...], right[:, at]))
+
+    each(right.shape[1] // 256, one)
+
+
+def store_as(target):
+    def write(at, value):
+        target[:, at] = value.astype(target.dtype)
+
+    return write
+
+
+def rms_rows(values, gain, normed):
+    def one(index):
+        at = tile(index, 32)
+        v = values[at, :]
+        root = lax.rsqrt(jnp.mean(v * v, axis=-1, keepdims=True) + epsilon)
+        normed[at, :] = (v * root * gain).astype(jnp.bfloat16)
+
+    each(values.shape[0] // 32, one)
+
+
+def half_masks():
+    lane = lax.broadcasted_iota(jnp.int32, (1, 2 * HD), 1)
+    low = (lane < HD).astype(jnp.float32)
+    return (low.astype(jnp.bfloat16), (1.0 - low).astype(jnp.bfloat16))
+
+
+def causal_bias(smalls, spread, pair, half):
+    row = smalls[tile(pair, 16), :][3:4]
+    size = spread.shape[2]
+    row = jnp.broadcast_to(row, (8, 128)).astype(jnp.bfloat16)
+    line = product(row, spread[half])[0:1]
+    bias = pltpu.roll(jnp.broadcast_to(line, (size, size)), 0, 1, stride=1, stride_axis=0)
+    here = lax.broadcasted_iota(jnp.int32, (size, size), 0)
+    there = lax.broadcasted_iota(jnp.int32, (size, size), 1)
+    return jnp.where(there <= here, bias, masked_value)
+
+
+def softmax_rows(scores):
+    terms = jnp.exp(scores - jnp.max(scores, axis=-1, keepdims=True))
+    return terms * (1.0 / jnp.sum(terms, axis=-1, keepdims=True))
+
+
+def attend_heads(queries, keys, values, out, bias_of):
+    masks = half_masks()
+
+    def pair(index):
+        at = tile(index, 2 * HD)
+        q, k, v = queries[:, at], keys[:, at], values[:, at]
+        total = jnp.zeros(q.shape, jnp.float32)
+        for half in range(2):
+            scores = product_right(q * masks[half], k)
+            if bias_of is not None:
+                scores = scores + bias_of(index, half)
+            weights = softmax_rows(scores).astype(jnp.bfloat16)
+            total = total + product(weights, v * masks[half])
+        out[:, at] = total.astype(jnp.bfloat16)
+
+    each(H // 2, pair)
+
+
+def column_partners(rank, depth):
+    return [(rank, lax.rem(depth + step, DOCS)) for step in range(1, DOCS)]
+
+
+class Kept:
+    inputs, normed, q, k, u, o1, after, normed2, cq = range(9)
+    ck, cv, o2, after2, normed3, w, slope, gelu, cot = range(9, 18)
+    normed_t, q_t, o1_t, normed2_t, cq_t, o2_t, normed3_t, states_t = range(18, 26)
+    count = 26
+    wide = (14, 15, 16)
+    exact = (0, 6, 12, 15, 16)
+    states = (9, 10)
+    flipped = tuple(range(18, 26))
+    inside = (1, 5, 7, 11, 13)
+
+
+def forward_kernel(count, *refs):
+    owns, refs = refs[:count], refs[count:]
+    (tokens, cotangent, chosen, encoded, spread), refs = refs[:5], refs[5:]
+    fulls, refs = refs[:count], refs[count:]
+    n = Kept.count
+    outs, refs = refs[:n], refs[n:]
+    grad_out, refs = refs[0], refs[1:]
+    keep, refs = refs[:n], refs[n:]
+    (
+        grad_fd,
+        smalls,
+        gains,
+        all_tokens,
+        all_cotangent,
+        square,
+        wide,
+        send_sems,
+        recv_sems,
+        local_sems,
+        line_send,
+        line_recv,
+        line_local,
+        load_sems,
+        save_sems,
+    ) = refs
     rank, core, along_x, along_y, depth = place()
     gather = Gather(owns, fulls, send_sems, recv_sems, local_sems)
     column = column_partners(rank, depth)
     greet([gather.to_x, gather.to_y, gather.to_core] + column)
-    pairs = ((tokens, all_tokens), (cotangent, all_cotangent))
-    line = []
-    for number, (own, whole) in enumerate(pairs):
-        pltpu.make_async_copy(own, whole.at[depth], line_local.at[number]).start()
+
+    def line_copies(number):
+        own, whole = ((tokens, all_tokens), (cotangent, all_cotangent))[number]
+        rows = own.shape[0]
+        at = whole.at[pl.ds(pl.multiple_of(depth * rows, rows), rows)]
+        here = pltpu.make_async_copy(own, at, line_local.at[number])
+        sends, receives = [], []
         for step, partner in enumerate(column):
-            send = remote(
-                own, whole.at[depth], line_send.at[number, step], line_recv.at[number, step], partner
+            sems = (line_send.at[number, step], line_recv.at[number, step])
+            sends.append(remote(own, at, sems[0], sems[1], partner))
+            origin = lax.rem(depth + DOCS - 1 - step, DOCS)
+            landing = whole.at[pl.ds(pl.multiple_of(origin * rows, rows), rows)]
+            receives.append(remote(own, landing, sems[0], sems[1], partner))
+        return (here, sends, receives)
+
+    def line_finish(number):
+        here, sends, receives = line_copies(number)
+        here.wait()
+        for copy in receives:
+            copy.wait_recv()
+        for copy in sends:
+            copy.wait_send()
+
+    for number in range(2):
+        here, sends, unused = line_copies(number)
+        here.start()
+        for copy in sends:
+            copy.start()
+
+    def flip(source, name):
+        turn(source, keep[name])
+        save(name)
+
+    def save(name):
+        if name in Kept.inside:
+            return
+        pltpu.make_async_copy(keep[name], outs[name], save_sems.at[name]).start()
+
+    def load(number, buffer):
+        copy = pltpu.make_async_copy(fulls[number], buffer, load_sems.at[number])
+        copy.start()
+        copy.wait()
+
+    def project(left, number, name):
+        load(number, square)
+        by_columns(left, square, store_as(keep[name]))
+        save(name)
+
+    def residual(before, left, number, name, gain, normed, turned):
+        load(number, square)
+
+        def write(at, value):
+            keep[name][:, at] = keep[before][:, at] + value
+
+        by_columns(keep[left], square, write)
+        save(name)
+        rms_rows(keep[name], gains[gain : gain + 1, :], keep[normed])
+        flip(keep[normed], turned)
+
+    def start():
+        load(0, smalls)
+        for slot in range(8):
+            gains[0:3, 128 * slot : 128 * slot + 128] = smalls[16 * slot : 16 * slot + 3, :]
+        line_finish(0)
+        by_columns(chosen, all_tokens, store_as(keep[Kept.inputs]))
+        save(Kept.inputs)
+        rms_rows(keep[Kept.inputs], gains[0:1, :], keep[Kept.normed])
+        flip(keep[Kept.normed], Kept.normed_t)
+        flip(encoded, Kept.states_t)
+
+    def keys():
+        flip(keep[Kept.q], Kept.q_t)
+        project(keep[Kept.normed], 4, Kept.k)
+
+    def self_heads():
+        project(keep[Kept.normed], 5, Kept.u)
+        attend_heads(
+            keep[Kept.q], keep[Kept.k], keep[Kept.u], keep[Kept.o1], functools.partial(causal_bias, smalls, spread)
+        )
+        flip(keep[Kept.o1], Kept.o1_t)
+
+    def cross_heads():
+        project(keep[Kept.normed2], 7, Kept.cq)
+        flip(keep[Kept.cq], Kept.cq_t)
+        attend_heads(keep[Kept.cq], keep[Kept.ck], keep[Kept.cv], keep[Kept.o2], None)
+        flip(keep[Kept.o2], Kept.o2_t)
+        line_finish(1)
+        by_columns(chosen, all_cotangent, store_as(keep[Kept.cot]))
+        save(Kept.cot)
+
+    def gate():
+        load(9, wide)
+        by_columns(keep[Kept.normed3], wide, store_as(keep[Kept.slope]))
+
+    def up():
+        load(10, wide)
+        scale = math.sqrt(2.0 / math.pi)
+
+        def write(at, b):
+            a = keep[Kept.slope][:, at]
+            t = jnp.tanh(scale * (a + 0.044715 * (a * a * a)))
+            gelu = 0.5 * a * (1.0 + t)
+            slope = 0.5 * (1.0 + t) + 0.5 * a * (1.0 - t * t) * scale * (
+                1.0 + 3 * 0.044715 * (a * a)
             )
-            send.start()
-            origin = lax.rem(depth + DOCS - 1 - step, DOCS)
-            receive = remote(
-                own, whole.at[origin], line_send.at[number, step], line_recv.at[number, step], partner
-            )
-            line.append((send, receive))
-    for step in range(count + 3):
+            keep[Kept.gelu][:, at] = gelu
+            keep[Kept.slope][:, at] = slope * b
+            w = (gelu * b).astype(jnp.bfloat16)
+            keep[Kept.w][:, at] = w
+            grad_fd[at, :] = product_left(w, keep[Kept.cot][...]).astype(jnp.bfloat16)
+
+        by_columns(keep[Kept.normed3], wide, write)
+        for name in (Kept.gelu, Kept.slope, Kept.w):
+            save(name)
+        pltpu.make_async_copy(grad_fd, grad_out, save_sems.at[n]).start()
+
+    compute = (
+        start,
+        lambda: project(encoded, 1, Kept.ck),
+        lambda: project(encoded, 2, Kept.cv),
+        lambda: project(keep[Kept.normed], 3, Kept.q),
+        keys,
+        self_heads,
+        lambda: residual(Kept.inputs, Kept.o1, 6, Kept.after, 1, Kept.normed2, Kept.normed2_t),
+        cross_heads,
+        lambda: residual(Kept.after, Kept.o2, 8, Kept.after2, 2, Kept.normed3, Kept.normed3_t),
+        gate,
+        up,
+        lambda: None,
+    )
+    for step in range(count + 4):
         if step < count:
             gather.issue(step)
-        if 0 <= step - 1 < count:
-            gather.relay(step - 1)
         if 0 <= step - 2 < count:
-            gather.spread(step - 2)
+            gather.relay(step - 2)
         if 0 <= step - 3 < count:
-            gather.finish(step - 3)
-    for number, (own, whole) in enumerate(pairs):
-        pltpu.make_async_copy(own, whole.at[depth], line_local.at[number]).wait()
-    for send, receive in line:
-        receive.wait_recv()
-        send.wait_send()
-
-
-def gather_call(shards, tokens, cotangent):
+            gather.spread(step - 3)
+        if 0 <= step - 4 < count:
+            gather.finish(step - 4)
+            compute[step - 4]()
+    for name in range(n):
+        if name not in Kept.inside:
+            pltpu.make_async_copy(keep[name], outs[name], save_sems.at[name]).wait()
+    pltpu.make_async_copy(grad_fd, grad_out, save_sems.at[n]).wait()
+
+
+def forward_call(shards, tokens, cotangent, chosen, encoded, spread):
     count = len(shards)
     vmem = pl.BlockSpec(memory_space=pltpu.VMEM)
     anywhere = pl.BlockSpec(memory_space=pl.ANY)
-    shapes = [jax.ShapeDtypeStruct((8,) + s.shape, s.dtype) for s in shards]
-    shapes += [jax.ShapeDtypeStruct((DOCS,) + s.shape, s.dtype) for s in (tokens, cotangent)]
+    most, total = chosen.shape
+    shapes = [jax.ShapeDtypeStruct((8 * s.shape[0], s.shape[1]), s.dtype) for s in shards]
+    saved = []
+    for name in range(Kept.count):
+        if name in Kept.flipped:
+            rows = encoded.shape[0] if name == Kept.states_t else most
+            saved.append(((shards[1].shape[1], rows), jnp.bfloat16))
+            continue
+        rows = encoded.shape[0] if name in Kept.states else most
+        width = shards[9].shape[1] if name in Kept.wide else shards[1].shape[1]
+        saved.append(((rows, width), jnp.float32 if name in Kept.exact else jnp.bfloat16))
+    shapes += [jax.ShapeDtypeStruct(*s) for s in saved]
+    down = shapes[count - 1]
+    square = shards[1].shape[1]
     return pl.pallas_call(
-        functools.partial(gather_kernel, count),
-        out_shape=shapes,
-        in_specs=[vmem] * (count + 2),
-        out_specs=[anywhere] * (count + 2),
-        scratch_shapes=[
+        functools.partial(forward_kernel, count),
+        out_shape=shapes + [down],
+        in_specs=[vmem] * (count + 5),
+        out_specs=[anywhere] * (len(shapes) + 1),
+        scratch_shapes=[pltpu.VMEM(*s) for s in saved]
+        + [
+            pltpu.VMEM(down.shape, down.dtype),
+            pltpu.VMEM(shapes[0].shape, jnp.float32),
+            pltpu.VMEM((8, square), jnp.float32),
+            pltpu.VMEM((total, square), jnp.bfloat16),
+            pltpu.VMEM((total, square), jnp.bfloat16),
+            pltpu.VMEM((square, square), jnp.bfloat16),
+            pltpu.VMEM((square, shards[9].shape[1]), jnp.bfloat16),
             pltpu.SemaphoreType.DMA((count, 9)),
             pltpu.SemaphoreType.DMA((count, 9)),
             pltpu.SemaphoreType.DMA((count,)),
             pltpu.SemaphoreType.DMA((2, DOCS - 1)),
             pltpu.SemaphoreType.DMA((2, DOCS - 1)),
             pltpu.SemaphoreType.DMA((2,)),
+            pltpu.SemaphoreType.DMA((count,)),
+            pltpu.SemaphoreType.DMA((len(saved) + 1,)),
         ],
-        compiler_params=pltpu.CompilerParams(collective_id=1, has_side_effects=True),
-        name="gather_all",
-    )(*shards, tokens, cotangent)
+        compiler_params=pltpu.CompilerParams(
+            collective_id=1, has_side_effects=True, vmem_limit_bytes=60 * 2**20
+        ),
+        name="forward",
+    )(*shards, tokens, cotangent, chosen, encoded, spread)
 
 
 def add_rows(target, source):
@@ -695,9 +953,9 @@
 
 
 class Reduce:
-    def __init__(self, grads, outs, buffers, load, send_sems, recv_sems, local_sems):
+    def __init__(self, pieces, buffers, load, send_sems, recv_sems, local_sems):
         rank, core, along_x, along_y, depth = place()
-        self.grads, self.outs, self.buffers, self.load = grads, outs, buffers, load
+        self.pieces, self.buffers, self.load = pieces, buffers, load
         self.send_sems, self.recv_sems, self.local_sems = send_sems, recv_sems, local_sems
         self.core, self.along_x, self.along_y = core, along_x, along_y
         self.block = 2 * along_y + along_x
@@ -719,24 +977,22 @@
         )
 
     def halves(self, number):
-        size = self.grads[number].shape[1] // 2
+        size = self.pieces[number].rows // 2
         return (pl.ds(0, size), pl.ds(size, size))
 
     def core_copies(self, number):
-        grad, both = self.grads[number], self.buffers[number][0]
+        piece, both = self.pieces[number], self.buffers[number][0]
         return [
-            self.copy(number, q, grad.at[2 * q + 1 - self.core], both.at[q], self.to_core)
+            self.copy(number, q, piece.slot(2 * q + 1 - self.core), both.at[q], self.to_core)
             for q in range(4)
         ]
 
-    def loads(self, number):
-        grad = self.grads[number]
-        return [
-            pltpu.make_async_copy(
-                grad.at[2 * q + self.core], self.load[number].at[q], self.local_sems.at[number, q]
-            )
-            for q in range(4)
-        ]
+    def own_load(self, number, q):
+        return pltpu.make_async_copy(
+            self.pieces[number].slot(2 * q + self.core),
+            self.load[number].at[q % 2],
+            self.local_sems.at[number, q],
+        )
 
     def first_copies(self, number):
         both, from_x, from_y = self.buffers[number][:3]
@@ -813,20 +1069,26 @@
 
     def write(self, number):
         return pltpu.make_async_copy(
-            self.buffers[number][5], self.outs[number], self.local_sems.at[number, 4]
+            self.buffers[number][5],
+            self.pieces[number].out.at[:, self.pieces[number].columns],
+            self.local_sems.at[number, 4],
         )
 
     def stage(self, number, level):
         both, from_x, from_y, late_x, late_y, on_line, on_middle = self.buffers[number]
         low, high = self.halves(number)
         if level == 0:
-            for copy in self.core_copies(number) + self.loads(number):
+            for copy in self.core_copies(number):
                 copy.start()
+            self.own_load(number, 0).start()
+            self.own_load(number, 1).start()
         elif level == 1:
-            for q, (copy, load) in enumerate(zip(self.core_copies(number), self.loads(number))):
+            for q, copy in enumerate(self.core_copies(number)):
                 copy.wait_recv()
-                load.wait()
-                add_rows(both.at[q], self.load[number].at[q])
+                self.own_load(number, q).wait()
+                add_rows(both.at[q], self.load[number].at[q % 2])
+                if q < 2:
+                    self.own_load(number, q + 2).start()
             for copy in self.first_copies(number):
                 copy.start()
         elif level == 2:
@@ -908,92 +1170,563 @@
     ]
 
 
-def reduce_kernel(count, shared, *refs):
-    grads, backs = refs[:count], refs[count : count + 2]
-    refs = refs[count + 2 :]
-    outs, back_outs = refs[:count], refs[count : count + 2]
-    refs = refs[count + 2 :]
-    buffers = [refs[7 * i : 7 * i + 7] for i in range(count)]
-    refs = refs[7 * count :]
+class Piece:
+    def __init__(self, grad, out, start, width):
+        self.grad, self.out = grad, out
+        self.columns = pl.ds(start, width)
+        self.rows, self.width = grad.shape[1], width
+
+    def slot(self, index):
+        return self.grad.at[index, :, self.columns]
+
+
+def pieces_of(width):
+    return [(start, min(1024, width - start)) for start in range(0, width, 1024)]
+
+
+def rms_back(values, cotangent, gain, carry, out, gain_grad):
+    def one(index):
+        at = tile(index, 32)
+        v, gz = values[at, :], cotangent[at, :]
+        root = lax.rsqrt(jnp.mean(v * v, axis=-1, keepdims=True) + epsilon)
+        scaled = gain * gz
+        inner = jnp.mean(scaled * v, axis=-1, keepdims=True)
+        gain_grad[...] += jnp.sum(gz * v * root, axis=0, keepdims=True)
+        result = carry[at, :].astype(jnp.float32) + root * scaled - v * (root * root * root * inner)
+        out[at, :] = result.astype(out.dtype)
+
+    gain_grad[...] = jnp.zeros_like(gain_grad)
+    each(values.shape[0] // 32, one)
+
+
+def diagonal_sums(grad):
+    size = grad.shape[1]
+    total = grad[0:8]
+    for group in range(1, grad.shape[0] // 8):
+        part = grad[8 * group : 8 * group + 8]
+        total = total + pltpu.roll(part, size - 8 * group, 1)
+    row = lax.broadcasted_iota(jnp.int32, total.shape, 0)
+    line = jnp.where(row == 0, total, 0.0)
+    for step in range(1, 8):
+        line = line + jnp.where(row == step, pltpu.roll(total, size - step, 1), 0.0)
+    return jnp.sum(line, axis=0, keepdims=True)
+
+
+def attend_back_heads(
+    first, last, queries, flipped, keys, values, grad, grad_flipped, grad_q, grad_k, grad_v, bias_of, bias_grad
+):
+    masks = half_masks()
+    row = lax.broadcasted_iota(jnp.int32, (2 * HD, 1), 0)
+    low = (row < HD).astype(jnp.float32)
+    sides = (low.astype(jnp.bfloat16), (1.0 - low).astype(jnp.bfloat16))
+
+    def pair(index):
+        at = tile(index + first, 2 * HD)
+        q, k, v, g = queries[:, at], keys[:, at], values[:, at], grad[:, at]
+        qt, gt = flipped[at, :], grad_flipped[at, :]
+        total_q = jnp.zeros(q.shape, jnp.float32)
+        total_k = jnp.zeros((2 * HD, k.shape[0]), jnp.float32)
+        total_v = jnp.zeros((2 * HD, k.shape[0]), jnp.float32)
+        for half in range(2):
+            scores = product_right(q * masks[half], k)
+            if bias_of is not None:
+                scores = scores + bias_of(index + first, half)
+            weights = softmax_rows(scores)
+            grad_w = product_right(g * masks[half], v)
+            inner = jnp.sum(weights * grad_w, axis=-1, keepdims=True)
+            grad_s = weights * (grad_w - inner)
+            if bias_grad is not None:
+                bias_grad(index + first, half, grad_s)
+            rounded = grad_s.astype(jnp.bfloat16)
+            total_q = total_q + product(rounded, k * masks[half])
+            total_k = total_k + product(qt * sides[half], rounded)
+            total_v = total_v + product(gt * sides[half], weights.astype(jnp.bfloat16))
+        grad_q[:, at] = total_q.astype(jnp.bfloat16)
+        grad_k[at, :] = total_k.astype(jnp.bfloat16)
+        grad_v[at, :] = total_v.astype(jnp.bfloat16)
+
+    each(last - first, pair)
+
+
+def turn(source, target):
+    step = min(256, source.shape[0])
+
+    def one(index):
+        at = tile(index, step)
+        target[:, at] = source[at, :].T
+
+    each(source.shape[0] // step, one)
+
+
+class Given:
+    inputs, normed_t, q, q_t, k, u, o1_t, after, normed2_t = range(9)
+    cq, cq_t, ck, cv, o2_t, after2, normed3_t, w, slope, gelu, cot = range(9, 20)
+    states_t, chosen_t, spread, smalls = range(20, 24)
+    w_ck, w_cv, w_sq, w_sk, w_sv, w_so, w_cq, w_co, w_fg, w_fu, w_fd = range(24, 35)
+    grad_fd = 35
+    count = 36
+
+
+def backward_kernel(names, shared, *refs):
+    given, refs = refs[: Given.count], refs[Given.count :]
+    n = len(names)
+    grads, refs = (given[Given.grad_fd],) + refs[: n - 1], refs[n - 1 :]
+    outs, refs = refs[:n], refs[n:]
+    (encoder_out, layer_out, hidden_out), refs = refs[:3], refs[3:]
+    pieces = []
+    for grad, out in zip(grads, outs):
+        for start, width in pieces_of(grad.shape[2]) if grad.shape[1] < 256 else thirds(grad.shape[2]):
+            pieces.append(Piece(grad, out, start, width))
+    order = piece_order(len(pieces))
+    pieces = [pieces[i] for i in order]
+    count = len(pieces)
+    buffers, refs = [refs[7 * i : 7 * i + 7] for i in range(count)], refs[7 * count :]
     loads = [refs[shared[i]] for i in range(count)]
     refs = refs[max(shared) + 1 :]
-    landing, send_sems, recv_sems, local_sems, line_send, line_recv = refs
+    (
+        one_w,
+        two_w,
+        three_w,
+        backs,
+        stage,
+        state_stage,
+        grad_x,
+        grad_n,
+        value,
+        other,
+        cot,
+        half_a,
+        half_b,
+        half_c,
+        half_d,
+        left,
+        turned_q,
+        turned_g,
+        chosen_t,
+        spread,
+        smalls,
+        gains,
+        gain_grad,
+        small_grads,
+        landing,
+        send_sems,
+        recv_sems,
+        local_sems,
+        line_send,
+        line_recv,
+        load_sems,
+        stage_sems,
+        out_sem,
+    ) = refs
     rank, core, along_x, along_y, depth = place()
-    reduce = Reduce(grads, outs, buffers, loads, send_sems, recv_sems, local_sems)
+    reduce = Reduce(pieces, buffers, loads, send_sems, recv_sems, local_sems)
     column = column_partners(rank, depth)
     greet([reduce.to_x, reduce.to_y, reduce.to_core] + column)
-    line = []
-    for number, back in enumerate(backs):
-        for step, (unused, partner) in enumerate(column):
-            send = remote(
-                back.at[partner],
-                landing.at[number, step],
-                line_send.at[number, step],
-                line_recv.at[number, step],
-                (rank, partner),
-            )
-            send.start()
-            line.append(send)
-    for step in range(count + reduce.levels - 1):
+    ticks = iter(range(count + reduce.levels - 1))
+
+    def tick():
+        step = next(ticks)
         for level in range(reduce.levels):
             if 0 <= step - level < count:
                 reduce.stage(step - level, level)
-    for copy in line:
-        copy.wait_recv()
-        copy.wait_send()
-    rows = backs[0].shape[1]
-    chunk = math.gcd(rows, 32)
-    for number, back in enumerate(backs):
-
-        def one(index, unused):
-            at = pl.ds(index * chunk, chunk)
-            total = back[depth, at, :].astype(jnp.float32)
+
+    def fetch(*pairs):
+        copies = [
+            pltpu.make_async_copy(source, target, load_sems.at[i])
+            for i, (source, target) in enumerate(pairs)
+        ]
+        for copy in copies:
+            copy.start()
+        for copy in copies:
+            copy.wait()
+
+    def staged(buffers_of, target_of, values, tiles):
+        def copy(index):
+            slot = lax.rem(index, 2)
+            return pltpu.make_async_copy(buffers_of.at[slot], target_of(index), stage_sems.at[slot])
+
+        def one(index):
+            @pl.when(index >= 2)
+            def _():
+                copy(index - 2).wait()
+
+            buffers_of[lax.rem(index, 2)] = values(tile(index))
+            copy(index).start()
+
+        each(tiles, one)
+        for index in range(max(0, tiles - 2), tiles):
+            copy(jnp.int32(index)).wait()
+
+    def weight_grad(number, right, start=0, width=None, flipped=False):
+        width = grads[number].shape[2] if width is None else width
+
+        def values(at):
+            if flipped:
+                result = product_right(left[...], right[at, :])
+            else:
+                result = product(left[:, 0 : right.shape[0]], right[:, at])
+            return result.astype(jnp.bfloat16).reshape(stage.shape[1:])
+
+        def target(index):
+            column_start = pl.multiple_of(start + index * 256, 256)
+            return grads[number].at[:, :, pl.ds(column_start, 256)]
+
+        staged(stage, target, values, width // 256)
+
+    def send_back(number, rows):
+        def write(index):
+            at = tile(index)
+            result = product(chosen_t[...], rows[:, at]).astype(jnp.bfloat16)
+            backs[number, :, :, at] = result.reshape(backs.shape[1:3] + (256,))
+
+        each(rows.shape[1] // 256, write)
+        for step, (unused, partner) in enumerate(column):
+            back_copy(number, step, partner).start()
+
+    def back_copy(number, step, partner):
+        return remote(
+            backs.at[number, partner],
+            landing.at[number, step],
+            line_send.at[number, step],
+            line_recv.at[number, step],
+            (rank, partner),
+        )
+
+    def receive_back(number, out):
+        for step, (unused, partner) in enumerate(column):
+            copy = back_copy(number, step, partner)
+            copy.wait_recv()
+            copy.wait_send()
+
+        def one(index):
+            at = tile(index, 32)
+            total = backs[number, depth, at, :].astype(jnp.float32)
             for step in range(DOCS - 1):
                 total = total + landing[number, step, at, :].astype(jnp.float32)
-            back_outs[number][at, :] = total.astype(jnp.bfloat16)
-            return unused
-
-        lax.fori_loop(0, rows // chunk, one, 0)
+            out[at, :] = total.astype(jnp.bfloat16)
+
+        each(out.shape[0] // 32, one)
+
+    def norm_grad(values, gain, carry, out):
+        rms_back(values, grad_n, gains[gain : gain + 1, :], carry, out, gain_grad)
+        for slot in range(8):
+            small_grads[slot, gain : gain + 1, :] = gain_grad[:, 128 * slot : 128 * slot + 128]
+
+    def round_rows(source, target):
+        def one(index):
+            at = tile(index, 32)
+            target[at, :] = source[at, :].astype(jnp.bfloat16)
+
+        each(source.shape[0] // 32, one)
+
+    def through(right_rows, weights, write):
+        def one(index):
+            at = tile(index)
+            write(at, product_right(right_rows[...], weights[at, :]))
+
+        each(weights.shape[0] // 256, one)
+
+    def head_grads(weights):
+        through(half_a, weights, store_as(half_b))
+
+        def one(index):
+            at = tile(index)
+            turned_g[at, :] = product_right(weights[at, :], half_a[...]).astype(jnp.bfloat16)
+
+        each(weights.shape[0] // 256, one)
+
+    tick()
+    fetch(
+        (given[Given.cot], cot),
+        (given[Given.normed3_t], left),
+        (given[Given.chosen_t], chosen_t),
+        (given[Given.spread], spread),
+        (given[Given.smalls], smalls),
+    )
+    for slot in range(8):
+        gains[0:3, 128 * slot : 128 * slot + 128] = smalls[16 * slot : 16 * slot + 3, :]
+    small_grads[...] = jnp.zeros_like(small_grads)
+    tick()
+    for start, width in pieces_of(given[Given.w].shape[1]):
+        at = pl.ds(start, width)
+        down, gate, up = one_w.at[0:width], two_w.at[:, 0:width], three_w.at[:, 0:width]
+        part = half_a.at[:, 0:width]
+        slope, gelu = value.at[:, 0:width], other.at[:, 0:width]
+        gate_grad, up_grad = half_b.at[:, 0:width], half_c.at[:, 0:width]
+        fetch(
+            (given[Given.w_fd].at[at], down),
+            (given[Given.w_fg].at[:, at], gate),
+            (given[Given.w_fu].at[:, at], up),
+            (given[Given.w].at[:, at], part),
+            (given[Given.slope].at[:, at], slope),
+            (given[Given.gelu].at[:, at], gelu),
+        )
+
+        def split(at, grad_w):
+            gate_grad[:, at] = (grad_w * slope[:, at]).astype(jnp.bfloat16)
+            up_grad[:, at] = (grad_w * gelu[:, at]).astype(jnp.bfloat16)
+
+        through(cot, down, split)
+        weight_grad(1, gate_grad, start, width)
+        weight_grad(2, up_grad, start, width)
+
+        def add(index):
+            at = tile(index)
+            forward = product(part[...], down[:, at])
+            back = product_right(gate_grad[...], gate[at, :]) + product_right(up_grad[...], up[at, :])
+            if start:
+                forward, back = forward + grad_x[:, at], back + grad_n[:, at]
+            grad_x[:, at] = forward
+            grad_n[:, at] = back
+
+        each(grad_x.shape[1] // 256, add)
+        tick()
+
+    fetch(
+        (given[Given.after2], value),
+        (given[Given.o2_t], left),
+        (given[Given.w_co], one_w),
+        (given[Given.cq], half_c),
+        (given[Given.cq_t], turned_q),
+        (given[Given.ck], two_w.at[0:512]),
+        (given[Given.cv], two_w.at[512:1024]),
+    )
+
+    def layer(index):
+        at = tile(index, 32)
+        half_a[at, :] = (value[at, :] + grad_x[at, :]).astype(jnp.bfloat16)
+
+    each(value.shape[0] // 32, layer)
+    send_back(0, half_a)
+    norm_grad(value, 2, cot, grad_x)
+    round_rows(grad_x, half_a)
+    weight_grad(3, half_a)
+    head_grads(one_w)
+    tick()
+    keys_grad, values_grad = three_w.at[:, 0:512], three_w.at[:, 512:1024]
+
+    def cross(first, last):
+        attend_back_heads(
+            first,
+            last,
+            half_c,
+            turned_q,
+            two_w.at[0:512],
+            two_w.at[512:1024],
+            half_b,
+            turned_g,
+            half_d,
+            keys_grad,
+            values_grad,
+            None,
+            None,
+        )
+
+    cross(0, 4)
+    tick()
+    cross(4, 8)
+    tick()
+    states = one_w.at[:, 0:512]
+    fetch((given[Given.states_t], states))
+
+    def state_grad(number, right):
+        def values(at):
+            result = product_right(states[...], right[at, :])
+            return result.astype(jnp.bfloat16).reshape(stage.shape[1:])
+
+        def target(index):
+            return grads[number].at[:, :, tile(index)]
+
+        staged(stage, target, values, 4)
+
+    state_grad(4, keys_grad)
+    state_grad(5, values_grad)
+    turn(keys_grad, two_w.at[0:512])
+    turn(values_grad, two_w.at[512:1024])
+    fetch((given[Given.w_ck], one_w), (given[Given.w_cv], three_w), (given[Given.normed2_t], left))
+    tick()
+    staged(
+        state_stage,
+        lambda index: encoder_out.at[:, tile(index)],
+        lambda at: product_right(two_w[0:512], one_w[at, :])
+        + product_right(two_w[512:1024], three_w[at, :]),
+        4,
+    )
+    fetch(
+        (given[Given.w_cq], one_w),
+        (given[Given.w_so], three_w),
+        (given[Given.after], value),
+        (given[Given.q], half_c),
+        (given[Given.q_t], turned_q),
+        (given[Given.k], two_w.at[0:256]),
+        (given[Given.u], two_w.at[256:512]),
+    )
+    tick()
+    weight_grad(6, half_d)
+    through(half_d, one_w, store_as(grad_n))
+    norm_grad(value, 1, grad_x, grad_x)
+    round_rows(grad_x, half_a)
+    fetch((given[Given.o1_t], left))
+    weight_grad(7, half_a)
+    head_grads(three_w)
+    tick()
+
+    def table_grad(index, half, grad_s):
+        line = jnp.broadcast_to(diagonal_sums(grad_s), (8, grad_s.shape[1]))
+        table = lax.dot_general(
+            line,
+            spread[half].astype(jnp.float32),
+            (((1,), (1,)), ((), ())),
+            precision=highest,
+            preferred_element_type=jnp.float32,
+        )
+        small_grads[index, 3:4, :] = small_grads[index, 3:4, :] + table[0:1]
+
+    keys_grad, values_grad = three_w.at[:, 0:256], three_w.at[:, 256:512]
+
+    def own(first, last):
+        attend_back_heads(
+            first,
+            last,
+            half_c,
+            turned_q,
+            two_w.at[0:256],
+            two_w.at[256:512],
+            half_b,
+            turned_g,
+            half_d,
+            keys_grad,
+            values_grad,
+            functools.partial(causal_bias, smalls, spread),
+            table_grad,
+        )
+
+    own(0, 4)
+    tick()
+    own(4, 8)
+    turn(keys_grad, half_a)
+    turn(values_grad, half_b)
+    tick()
+    fetch(
+        (given[Given.normed_t], left),
+        (given[Given.inputs], value),
+        (given[Given.w_sq], one_w),
+        (given[Given.w_sk], two_w),
+        (given[Given.w_sv], three_w),
+    )
+    weight_grad(8, half_d)
+    weight_grad(9, half_a)
+    weight_grad(10, half_b)
+    tick()
+
+    def sum_three(index):
+        at = tile(index)
+        grad_n[:, at] = (
+            product_right(half_d[...], one_w[at, :])
+            + product_right(half_a[...], two_w[at, :])
+            + product_right(half_b[...], three_w[at, :])
+        )
+
+    each(grad_n.shape[1] // 256, sum_three)
+    norm_grad(value, 0, grad_x, half_c)
+    small_copy = pltpu.make_async_copy(small_grads, grads[11], out_sem)
+    small_copy.start()
+    small_copy.wait()
+    send_back(1, half_c)
+    for unused in range(count + reduce.levels):
+        try:
+            tick()
+        except StopIteration:
+            break
+    receive_back(0, layer_out)
+    receive_back(1, hidden_out)
     for number in range(count):
         reduce.write(number).wait()
 
 
-def reduce_call(grads, backs):
-    count = len(grads)
+def thirds(width):
+    return [(0, 384), (384, 384), (768, width - 768)]
+
+
+def piece_order(count):
+    return [0, 1, 2, 3, 6, 4, 7, 5, 8] + list(range(9, count))
+
+
+def backward_call(operands, rows):
+    count = Given.count
+    anywhere = pl.BlockSpec(memory_space=pl.ANY)
     vmem = pl.BlockSpec(memory_space=pltpu.VMEM)
-    anywhere = pl.BlockSpec(memory_space=pl.ANY)
-    scratch, load_shapes, shared = [], [], []
-    for grad in grads:
-        scratch += buffer_shapes(grad.shape[1], grad.shape[2], grad.dtype)
-        shape = ((4,) + grad.shape[1:], grad.dtype)
-        held = [i for i, s in enumerate(load_shapes) if s == shape]
+    grad_fd = operands[Given.grad_fd]
+    width, wide = operands[Given.w_fg].shape
+    square = jax.ShapeDtypeStruct((8, width // 8, width), jnp.bfloat16)
+    broad = jax.ShapeDtypeStruct((8, width // 8, wide), jnp.bfloat16)
+    small = jax.ShapeDtypeStruct((8, 16, 128), jnp.float32)
+    full = [jax.ShapeDtypeStruct(grad_fd.shape, grad_fd.dtype), broad, broad] + [square] * 8 + [small]
+    outs = [jax.ShapeDtypeStruct(g.shape[1:], g.dtype) for g in full]
+    most = operands[Given.inputs].shape[0]
+    states = operands[Given.ck].shape[0]
+    total = operands[Given.chosen_t].shape[0]
+    tail = [
+        jax.ShapeDtypeStruct((states, width), jnp.float32),
+        jax.ShapeDtypeStruct((rows, width), jnp.bfloat16),
+        jax.ShapeDtypeStruct((rows, width), jnp.bfloat16),
+    ]
+    shapes = []
+    for grad in full:
+        for start, part in pieces_of(grad.shape[2]) if grad.shape[1] < 256 else thirds(grad.shape[2]):
+            shapes.append(((grad.shape[1], part), grad.dtype))
+    shapes = [shapes[i] for i in piece_order(len(shapes))]
+    scratch, load_shapes, shared, turns = [], [], [], []
+    for shape, dtype in shapes:
+        scratch += buffer_shapes(shape[0], shape[1], dtype)
+        key = ((2,) + shape, dtype)
+        held = [i for i, s in enumerate(load_shapes) if s == key]
         if len(held) < 2:
             shared.append(len(load_shapes))
-            load_shapes.append(shape)
+            load_shapes.append(key)
         else:
-            turns = [i for i in shared if load_shapes[i] == shape]
-            shared.append(held[0] if turns[-1] == held[1] else held[1])
-    scratch += [pltpu.VMEM(*shape) for shape in load_shapes]
+            last = [i for i in shared if i in held][-1]
+            shared.append(held[0] if last == held[1] else held[1])
+    scratch += [pltpu.VMEM(*s) for s in load_shapes]
+    pieces = len(shapes)
+    bf16, f32 = jnp.bfloat16, jnp.float32
+    scratch += [pltpu.VMEM((width, width), bf16)] * 3
+    scratch += [
+        pltpu.VMEM((2, DOCS, total // DOCS, width), bf16),
+        pltpu.VMEM((2, 8, width // 8, 256), bf16),
+        pltpu.VMEM((2, states, 256), f32),
+    ]
+    scratch += [pltpu.VMEM((most, width), f32)] * 4
+    scratch += [pltpu.VMEM((most, width), bf16)] * 5
+    scratch += [pltpu.VMEM((width, most), bf16)] * 3
+    scratch += [
+        pltpu.VMEM((total, most), bf16),
+        pltpu.VMEM((2, 128, most), bf16),
+        pltpu.VMEM((128, 128), f32),
+        pltpu.VMEM((8, width), f32),
+        pltpu.VMEM((1, width), f32),
+        pltpu.VMEM((8, 16, 128), f32),
+        pltpu.VMEM((2, DOCS - 1, rows, width), bf16),
+        pltpu.SemaphoreType.DMA((pieces, 12)),
+        pltpu.SemaphoreType.DMA((pieces, 12)),
+        pltpu.SemaphoreType.DMA((pieces, 5)),
+        pltpu.SemaphoreType.DMA((2, DOCS - 1)),
+        pltpu.SemaphoreType.DMA((2, DOCS - 1)),
+        pltpu.SemaphoreType.DMA((8,)),
+        pltpu.SemaphoreType.DMA((2,)),
+        pltpu.SemaphoreType.DMA,
+    ]
     return pl.pallas_call(
-        functools.partial(reduce_kernel, count, shared),
-        out_shape=[jax.ShapeDtypeStruct(g.shape[1:], g.dtype) for g in grads]
-        + [jax.ShapeDtypeStruct(b.shape[1:], b.dtype) for b in backs],
-        in_specs=[anywhere] * count + [vmem] * 2,
-        out_specs=[anywhere] * count + [vmem] * 2,
-        scratch_shapes=scratch
-        + [
-            pltpu.VMEM((2, DOCS - 1) + backs[0].shape[1:], jnp.bfloat16),
-            pltpu.SemaphoreType.DMA((count, 12)),
-            pltpu.SemaphoreType.DMA((count, 12)),
-            pltpu.SemaphoreType.DMA((count, 5)),
-            pltpu.SemaphoreType.DMA((2, DOCS - 1)),
-            pltpu.SemaphoreType.DMA((2, DOCS - 1)),
-        ],
+        functools.partial(backward_kernel, range(12), shared),
+        out_shape=full[1:] + outs + tail,
+        in_specs=[anywhere] * count,
+        out_specs=[anywhere] * (len(full) - 1 + len(outs) + 1) + [vmem] * 2,
+        scratch_shapes=scratch,
         compiler_params=pltpu.CompilerParams(
-            collective_id=2, has_side_effects=True, vmem_limit_bytes=60 * 2**20
+            collective_id=2, has_side_effects=True, vmem_limit_bytes=67043328
         ),
-        name="reduce_all",
-    )(*grads, *backs)
+        name="backward",
+    )(*operands)
 
 
 def pack_small(norms, table):
@@ -1029,7 +1762,23 @@
     most = total // 2
     encoded = encoder_states[0]
     small = pack_small((norm_self, norm_cross, norm_feed), bias_table)
-    gathered = gather_call(
+    document = lax.dynamic_slice_in_dim(
+        encoder_docs[0], lax.axis_index("ctx") * encoded.shape[0], 1, 0
+    )
+    segments = segment_ids[0]
+    start = jnp.sum((segments < document).astype(jnp.int32))
+    length = jnp.sum((segments == document).astype(jnp.int32))
+    row = lax.broadcasted_iota(jnp.int32, (most, total), 0)
+    column = lax.broadcasted_iota(jnp.int32, (most, total), 1)
+    chosen = ((row + start == column) & (row < length)).astype(jnp.bfloat16)
+
+    slot = jnp.arange(2 * HD, dtype=jnp.int32)
+    position = jnp.arange(most, dtype=jnp.int32)
+    bucket = bucket_of(lax.rem(most - position, most))
+    spread = jnp.stack(
+        [(slot[:, None] == bucket[None] + BUCKETS * half) for half in range(2)]
+    ).astype(jnp.bfloat16)
+    results = forward_call(
         (
             small,
             cross_key,
@@ -1046,158 +1795,46 @@
         ),
         hidden_in[0],
         out_grad[0],
-    )
-    smalls = gathered[0]
-    w_ck, w_cv, w_sq, w_sk, w_sv, w_so, w_cq, w_co, w_fg, w_fu, w_fd = (
-        w.reshape(-1, w.shape[2]) for w in gathered[1:12]
-    )
-    all_tokens = gathered[12].reshape(total, width)
-    all_cotangent = gathered[13].reshape(total, width)
-    gain_self, gain_cross, gain_feed = (smalls[:, i].reshape(-1) for i in range(3))
-    table = smalls[:, 3, : bias_table.shape[0]].reshape(H, BUCKETS).astype(jnp.bfloat16)
-
-    document = lax.dynamic_slice_in_dim(
-        encoder_docs[0], lax.axis_index("ctx") * encoded.shape[0], 1, 0
-    )
-    segments = segment_ids[0]
-    start = jnp.sum((segments < document).astype(jnp.int32))
-    length = jnp.sum((segments == document).astype(jnp.int32))
-    row = lax.broadcasted_iota(jnp.int32, (most, total), 0)
-    column = lax.broadcasted_iota(jnp.int32, (most, total), 1)
-    chosen = ((row + start == column) & (row < length)).astype(jnp.bfloat16)
-
-    inputs = product(chosen, all_tokens)
-    grad_after = product(chosen, all_cotangent)
-    grad_round = grad_after.astype(jnp.bfloat16)
-
-    position = jnp.arange(most, dtype=jnp.int32)
-    distance = position[:, None] - position[None, :]
-    causal = (distance >= 0)[None]
-    onehot = bucket_onehot(jnp.maximum(distance, 0))
-
-    def heads(values):
-        return values.reshape(values.shape[0], H, HD)
-
-    def flat(values):
-        return values.reshape(values.shape[0], H * HD).astype(jnp.bfloat16)
-
-    def attend(q, k, v, bias, allowed):
-        scores = jnp.einsum("qhd,khd->hqk", q, k, preferred_element_type=jnp.float32)
-        if bias is not None:
-            scores = jnp.where(allowed, scores + bias, masked_value)
-        p = jax.nn.softmax(scores, axis=-1)
-        out = jnp.einsum(
-            "hqk,khd->qhd", p.astype(jnp.bfloat16), v, preferred_element_type=jnp.float32
+        chosen,
+        encoded,
+        spread,
+    )
+    kept = results[12:]
+    grad_fd = results[-1].reshape(8, -1, width)
+    forward_side = [
+        kept[i]
+        for i in (
+            Kept.inputs,
+            Kept.normed_t,
+            Kept.q,
+            Kept.q_t,
+            Kept.k,
+            Kept.u,
+            Kept.o1_t,
+            Kept.after,
+            Kept.normed2_t,
+            Kept.cq,
+            Kept.cq_t,
+            Kept.ck,
+            Kept.cv,
+            Kept.o2_t,
+            Kept.after2,
+            Kept.normed3_t,
+            Kept.w,
+            Kept.slope,
+            Kept.gelu,
+            Kept.cot,
+            Kept.states_t,
         )
-        return (p, out)
-
-    def attend_back(q, k, v, p, grad):
-        grad_p = jnp.einsum("qhd,khd->hqk", grad, v, preferred_element_type=jnp.float32)
-        grad_s = p * (grad_p - jnp.sum(p * grad_p, axis=-1, keepdims=True))
-        rounded = grad_s.astype(jnp.bfloat16)
-        grad_q = jnp.einsum("hqk,khd->qhd", rounded, k, preferred_element_type=jnp.float32)
-        grad_k = jnp.einsum("hqk,qhd->khd", rounded, q, preferred_element_type=jnp.float32)
-        grad_v = jnp.einsum(
-            "hqk,qhd->khd", p.astype(jnp.bfloat16), grad, preferred_element_type=jnp.float32
-        )
-        return (grad_s, flat(grad_q), flat(grad_k), flat(grad_v))
-
-    self_normed = normalize(inputs, gain_self).astype(jnp.bfloat16)
-    queries = heads(product(self_normed, w_sq).astype(jnp.bfloat16))
-    keys = heads(product(self_normed, w_sk).astype(jnp.bfloat16))
-    values = heads(product(self_normed, w_sv).astype(jnp.bfloat16))
-    bias = jnp.einsum("qkb,hb->hqk", onehot, table, preferred_element_type=jnp.float32)
-    self_p, self_heads = attend(queries, keys, values, bias, causal)
-    self_attended = flat(self_heads)
-    after_self = inputs + product(self_attended, w_so)
-    cross_normed = normalize(after_self, gain_cross).astype(jnp.bfloat16)
-    cross_q = heads(product(cross_normed, w_cq).astype(jnp.bfloat16))
-    cross_k = heads(product(encoded, w_ck).astype(jnp.bfloat16))
-    cross_v = heads(product(encoded, w_cv).astype(jnp.bfloat16))
-    cross_p, cross_heads = attend(cross_q, cross_k, cross_v, None, None)
-    cross_attended = flat(cross_heads)
-    after_cross = after_self + product(cross_attended, w_co)
-    feed_normed = normalize(after_cross, gain_feed).astype(jnp.bfloat16)
-    gate_value = product(feed_normed, w_fg)
-    up_value = product(feed_normed, w_fu)
-
-    def gated(gate_in, up_in):
-        return jax.nn.gelu(gate_in, approximate=True) * up_in
-
-    hidden_units, pullback = jax.vjp(gated, gate_value, up_value)
-    hidden_units = hidden_units.astype(jnp.bfloat16)
-    layer_out = (after_cross + product(hidden_units, w_fd)).astype(jnp.bfloat16)
-
-    grad_fd = product_left(hidden_units, grad_round)
-    grad_gate, grad_up = pullback(product_right(grad_round, w_fd))
-    gate_round = grad_gate.astype(jnp.bfloat16)
-    up_round = grad_up.astype(jnp.bfloat16)
-    grad_fg = product_left(feed_normed, gate_round)
-    grad_fu = product_left(feed_normed, up_round)
-    grad_normed = product_right(gate_round, w_fg) + product_right(up_round, w_fu)
-    side, grad_gain_feed = norm_back(after_cross, gain_feed, grad_normed)
-    grad_after_cross = grad_after + side
-    cross_round = grad_after_cross.astype(jnp.bfloat16)
-    grad_co = product_left(cross_attended, cross_round)
-    grad_heads = heads(product_right(cross_round, w_co).astype(jnp.bfloat16))
-    unused, grad_q, grad_k, grad_v = attend_back(cross_q, cross_k, cross_v, cross_p, grad_heads)
-    grad_ck = product_left(encoded, grad_k)
-    grad_cv = product_left(encoded, grad_v)
-    encoder_grad = product_right(grad_k, w_ck) + product_right(grad_v, w_cv)
-    grad_cq = product_left(cross_normed, grad_q)
-    side, grad_gain_cross = norm_back(after_self, gain_cross, product_right(grad_q, w_cq))
-    grad_after_self = grad_after_cross + side
-    self_round = grad_after_self.astype(jnp.bfloat16)
-    grad_so = product_left(self_attended, self_round)
-    grad_heads = heads(product_right(self_round, w_so).astype(jnp.bfloat16))
-    grad_s, grad_q, grad_k, grad_v = attend_back(queries, keys, values, self_p, grad_heads)
-    grad_table = jnp.einsum(
-        "hqk,qkb->hb", grad_s, onehot.astype(jnp.float32), precision=highest
-    )
-    grad_sq = product_left(self_normed, grad_q)
-    grad_sk = product_left(self_normed, grad_k)
-    grad_sv = product_left(self_normed, grad_v)
-    grad_normed = (
-        product_right(grad_q, w_sq) + product_right(grad_k, w_sk) + product_right(grad_v, w_sv)
-    )
-    side, grad_gain_self = norm_back(inputs, gain_self, grad_normed)
-    hidden_grad = (grad_after_self + side).astype(jnp.bfloat16)
-
-    def back(values):
-        return product_left(chosen, values).astype(jnp.bfloat16).reshape(DOCS, -1, width)
-
-    table_rows = jnp.pad(grad_table.reshape(8, -1), ((0, 0), (0, 64)))
-    small_grads = jnp.stack(
-        [g.reshape(8, 128) for g in (grad_gain_self, grad_gain_cross, grad_gain_feed)]
-        + [table_rows],
-        axis=1,
-    )
-    small_grads = jnp.pad(small_grads, ((0, 0), (0, 12), (0, 0)))
-
-    def shards(grad):
-        return grad.astype(jnp.bfloat16).reshape(8, -1, grad.shape[1])
-
-    names = (
-        grad_fd,
-        grad_fg,
-        grad_fu,
-        grad_co,
-        grad_ck,
-        grad_cv,
-        grad_cq,
-        grad_so,
-        grad_sq,
-        grad_sk,
-        grad_sv,
-    )
-    reduced = reduce_call(
-        tuple(shards(g) for g in names) + (small_grads,), (back(layer_out), back(hidden_grad))
-    )
-    fd, fg, fu, co, ck, cv, cq, so, sq, sk, sv = (r.astype(jnp.float32) for r in reduced[:11])
-    smalls = reduced[11]
+    ]
+    results = backward_call(
+        forward_side + [chosen.T, spread] + list(results[:12]) + [grad_fd], hidden_in.shape[1]
+    )[11:]
+    fd, fg, fu, co, ck, cv, cq, so, sq, sk, sv = (r.astype(jnp.float32) for r in results[:11])
+    smalls, encoder_grad, layer_out, hidden_grad = results[11:]
     return (
-        reduced[12][None],
-        reduced[13].astype(jnp.float32)[None],
+        layer_out[None],
+        hidden_grad.astype(jnp.float32)[None],
         encoder_grad[None],
         sq,
         sk,

time: 582 us -> 444 us (0.76)
  matrix products: 158 us -> 0 us
  Pallas kernels: 347 us -> 414 us
  local copies, waits for them, and re-layouts: 43.9 us -> 6.55 us
    dot_general x49 -> x0, matrix products: 151 us -> none  [the longest x13 40 us: product_left(): lax.dot_general(left_side, right_side, (((0,), (0,)), ((), ())), preferre...]
    pallas_call x2, Pallas kernels: 347 us -> 414 us  [the longest x1 248 us: backward_call(): pl.pallas_call(functools.partial(backward_kernel, range(12), shared), out...]
    eq x1 -> x0, local copies, waits for them, and re-layouts: 11.8 us -> none  [bucket_onehot(): bucket_index[:, :, None] == jnp.arange(BUCKETS, dtype=jnp.int32)]
    unnamed x145 -> x24, local copies, waits for them, and re-layouts: 11.3 us -> 2.06 us
    convert_element_type x7 -> x0, local copies, waits for them, and re-layouts: 8.65 us -> none  [the longest x1 2.04 us: by_document(): cross_q = heads(product(cross_normed, w_cq).astype(jnp.bfloat16))]
    sub x1 -> x0, matrix products: 6.81 us -> none  [attend(): p = jax.nn.softmax(scores, axis=-1)]
where the time goes in v2:
time: 444 us; the launch traced here: 443 us
  Pallas kernels  414 us (93%)
  other arithmetic  21.1 us (5%)
  local copies, waits for them, and re-layouts  6.55 us (1%)
    pallas_call x1, Pallas kernels, backward_call(): pl.pallas_call(functools.partial(backward_kernel, range(12), shared), out...  248 us
    pallas_call x1, Pallas kernels, forward_call(): pl.pallas_call(functools.partial(forward_kernel, count), out_shape=shapes...  166 us
    convert_element_type x11, other arithmetic, by_document(): r.astype(jnp.float32)  12.4 us

profile of v2, /device:TPU:0, one launch (start us, length us, event | category | flops | bytes accessed | tf_op | source)
XLA Modules:
  0.0 442.8 jit_solution(14560450870497246113)
XLA Ops:
  0.7 1.2 constant_dynamic-slice_fusion
  2.6 2.0 fusion.13
  5.9 1.3 fusion.11.refs_0_
  7.2 0.7 add_convert_fusion.refs_16_.refs_22_
  7.9 0.8 fusion.3.refs_21_
  8.7 0.9 fusion.1.refs_14_
  9.6 166.2 %forward.1 = (f32[128,128]{1,0:T(8,128)}, bf16[1024,1024]{1,0:T(8,128)(2,1)}, bf16[1024,1024]{1,0:T(8,128)(2,1)}, bf16[1024,1024]{1,0:T(8,128)(2,1)}, bf16[1024,...) custom-call(f32[16,128]{1,0:T(8,128)} %fusion.11.refs_0_, ...), custom_call_target="tpu_custom_call" | custom-call | tf_op jit(solution)/shard_map/forward/pallas_call | solution.py:913
  175.8 248.1 %backward.1 = (bf16[8,128,2816]{2,1,0:T(8,128)(2,1)}, bf16[8,128,2816]{2,1,0:T(8,128)(2,1)}, bf16[8,128,1024]{2,1,0:T(8,128)(2,1)}, bf16[8,128,1024]{2,1,0:T(8,1...) custom-call(f32[256,1024]{1,0:T(8,128)} %get-tuple-element.67.refs_0, ...), custom_call_target="tpu_custom_call" | custom-call | tf_op jit(solution)/shard_map/backward/pallas_call | solution.py:1719
  423.9 1.3 slice_bitcast_fusion
  425.2 1.3 slice_bitcast_fusion.1
  426.5 1.8 bitcast_convert_fusion
  428.3 1.8 convert_element_type.258
  430.2 1.8 convert_element_type.259
  432.0 0.8 convert_element_type.260
  432.9 0.8 convert_element_type.261
  433.7 0.8 convert_element_type.262
  434.5 0.8 convert_element_type.263
  435.4 0.8 convert_element_type.264
  436.2 0.8 convert_element_type.265
  437.1 1.2 convert_element_type.266
  438.3 1.2 convert_element_type.267
  439.5 1.3 convert_element_type.268
  440.7 0.7 copy.40
  441.4 1.3 copy.41
  (28 shorter events, 2.1 us)
Async XLA Ops:
  423.9 8.1 %copy-start.9 = (bf16[128,1024]{1,0:T(8,128)(2,1)S(1)}, bf16[128,1024]{1,0:T(8,128)(2,1)}, u32[]{:S(2)}) copy-start(bf16[128,1024]{1,0:T(8,128)(2,1)} %get-tuple-element.106) | copy-start | bytes 786436
  423.9 8.9 %copy-start.8 = (bf16[128,1024]{1,0:T(8,128)(2,1)S(1)}, bf16[128,1024]{1,0:T(8,128)(2,1)}, u32[]{:S(2)}) copy-start(bf16[128,1024]{1,0:T(8,128)(2,1)} %get-tuple-element.107) | copy-start | bytes 786436
  423.9 9.8 %copy-start.7 = (bf16[128,1024]{1,0:T(8,128)(2,1)S(1)}, bf16[128,1024]{1,0:T(8,128)(2,1)}, u32[]{:S(2)}) copy-start(bf16[128,1024]{1,0:T(8,128)(2,1)} %get-tuple-element.108) | copy-start | bytes 786436
  428.3 6.2 %copy-start.6 = (bf16[128,1024]{1,0:T(8,128)(2,1)S(1)}, bf16[128,1024]{1,0:T(8,128)(2,1)}, u32[]{:S(2)}) copy-start(bf16[128,1024]{1,0:T(8,128)(2,1)} %get-tuple-element.109) | copy-start | bytes 786436
  430.2 5.2 %copy-start.5 = (bf16[128,1024]{1,0:T(8,128)(2,1)S(1)}, bf16[128,1024]{1,0:T(8,128)(2,1)}, u32[]{:S(2)}) copy-start(bf16[128,1024]{1,0:T(8,128)(2,1)} %get-tuple-element.110) | copy-start | bytes 786436
  432.0 4.2 copy-start.4
  432.9 4.2 copy-start.3
  434.5 3.7 copy-start.2
  437.1 2.4 copy-start.1
  438.3 2.5 copy-start.10
  438.3 3.2 copy-start

commit v3 on v2

--- a/solution.py
+++ b/solution.py
@@ -855,7 +855,9 @@
             keep[Kept.slope][:, at] = slope * b
             w = (gelu * b).astype(jnp.bfloat16)
             keep[Kept.w][:, at] = w
-            grad_fd[at, :] = product_left(w, keep[Kept.cot][...]).astype(jnp.bfloat16)
+            grad = product_left(w, keep[Kept.cot][...]).astype(jnp.bfloat16)
+            for part in range(grad_fd.shape[0]):
+                grad_fd[part, at, :] = grad[:, 256 * part : 256 * part + 256]
 
         by_columns(keep[Kept.normed3], wide, write)
         for name in (Kept.gelu, Kept.slope, Kept.w):
@@ -909,6 +911,7 @@
         saved.append(((rows, width), jnp.float32 if name in Kept.exact else jnp.bfloat16))
     shapes += [jax.ShapeDtypeStruct(*s) for s in saved]
     down = shapes[count - 1]
+    down = jax.ShapeDtypeStruct((down.shape[1] // 256, down.shape[0], 256), down.dtype)
     square = shards[1].shape[1]
     return pl.pallas_call(
         functools.partial(forward_kernel, count),
@@ -941,15 +944,14 @@
 
 
 def add_rows(target, source):
-    rows = target.shape[-2]
-    step = math.gcd(rows, 32)
-
-    def one(index, unused):
-        at = pl.ds(index * step, step)
-        target[at, :] = target[at, :] + source[at, :]
-        return unused
-
-    lax.fori_loop(0, rows // step, one, 0)
+    rows = target.shape[1]
+    step = math.gcd(rows, 64)
+
+    def one(index):
+        at = pl.ds(pl.multiple_of(index * step, step), step)
+        target[:, at, :] = target[:, at, :] + source[:, at, :]
+
+    each(rows // step, one)
 
 
 class Reduce:
@@ -1003,7 +1005,7 @@
                 self.copy(
                     number,
                     4 + other,
-                    both.at[2 * other + 1 - self.along_x, low],
+                    both.at[2 * other + 1 - self.along_x, :, low],
                     from_x.at[other],
                     self.to_x,
                 )
@@ -1013,7 +1015,7 @@
                 self.copy(
                     number,
                     6 + other,
-                    both.at[2 * (1 - self.along_y) + other, high],
+                    both.at[2 * (1 - self.along_y) + other, :, high],
                     from_y.at[other],
                     self.to_y,
                 )
@@ -1027,14 +1029,14 @@
             self.copy(
                 number,
                 8,
-                both.at[2 * (1 - self.along_y) + self.along_x, low],
+                both.at[2 * (1 - self.along_y) + self.along_x, :, low],
                 late_y,
                 self.to_y,
             ),
             self.copy(
                 number,
                 9,
-                both.at[2 * self.along_y + 1 - self.along_x, high],
+                both.at[2 * self.along_y + 1 - self.along_x, :, high],
                 late_x,
                 self.to_x,
             ),
@@ -1070,7 +1072,7 @@
     def write(self, number):
         return pltpu.make_async_copy(
             self.buffers[number][5],
-            self.pieces[number].out.at[:, self.pieces[number].columns],
+            self.pieces[number].out.at[self.pieces[number].tiles],
             self.local_sems.at[number, 4],
         )
 
@@ -1096,19 +1098,19 @@
             for other in range(2):
                 copies[other].wait_recv()
                 copies[other].wait_send()
-                add_rows(both.at[2 * other + self.along_x, low], from_x.at[other])
+                add_rows(both.at[2 * other + self.along_x, :, low], from_x.at[other])
             for other in range(2):
                 copies[2 + other].wait_recv()
                 copies[2 + other].wait_send()
-                add_rows(both.at[2 * self.along_y + other, high], from_y.at[other])
+                add_rows(both.at[2 * self.along_y + other, :, high], from_y.at[other])
             for copy in self.second_copies(number):
                 copy.start()
         elif level == 3:
             to_y, to_x = self.second_copies(number)
             to_y.wait_recv()
-            add_rows(both.at[self.block, low], late_y)
+            add_rows(both.at[self.block, :, low], late_y)
             to_x.wait_recv()
-            add_rows(both.at[self.block, high], late_x)
+            add_rows(both.at[self.block, :, high], late_x)
             to_y.wait_send()
             to_x.wait_send()
 
@@ -1128,15 +1130,14 @@
             def _():
                 middle = self.middle_copy(number)
                 middle.wait_recv()
-                rows = on_line.shape[0]
-                step = math.gcd(rows, 32)
-
-                def one(index, unused):
-                    at = pl.ds(index * step, step)
-                    on_line[at, :] = both[self.block, at, :] + on_middle[at, :]
-                    return unused
-
-                lax.fori_loop(0, rows // step, one, 0)
+                rows = on_line.shape[1]
+                step = math.gcd(rows, 64)
+
+                def one(index):
+                    at = pl.ds(pl.multiple_of(index * step, step), step)
+                    on_line[:, at, :] = both[self.block, :, at, :] + on_middle[:, at, :]
+
+                each(rows // step, one)
                 middle.wait_send()
                 self.return_copy(number).start()
         else:
@@ -1158,30 +1159,59 @@
     levels = 7
 
 
-def buffer_shapes(rows, width, dtype):
+def buffer_shapes(tiles, rows, width, dtype):
     return [
-        pltpu.VMEM((4, rows, width), dtype),
-        pltpu.VMEM((2, rows // 2, width), dtype),
-        pltpu.VMEM((2, rows // 2, width), dtype),
-        pltpu.VMEM((rows // 2, width), dtype),
-        pltpu.VMEM((rows // 2, width), dtype),
-        pltpu.VMEM((rows, width), dtype),
-        pltpu.VMEM((rows, width), dtype),
+        pltpu.VMEM((4, tiles, rows, width), dtype),
+        pltpu.VMEM((2, tiles, rows // 2, width), dtype),
+        pltpu.VMEM((2, tiles, rows // 2, width), dtype),
+        pltpu.VMEM((tiles, rows // 2, width), dtype),
+        pltpu.VMEM((tiles, rows // 2, width), dtype),
+        pltpu.VMEM((tiles, rows, width), dtype),
+        pltpu.VMEM((tiles, rows, width), dtype),
     ]
 
 
 class Piece:
-    def __init__(self, grad, out, start, width):
+    def __init__(self, grad, out, start, tiles):
         self.grad, self.out = grad, out
-        self.columns = pl.ds(start, width)
-        self.rows, self.width = grad.shape[1], width
+        self.tiles = pl.ds(start, tiles)
+        self.rows = grad.shape[2]
 
     def slot(self, index):
-        return self.grad.at[index, :, self.columns]
-
-
-def pieces_of(width):
-    return [(start, min(1024, width - start)) for start in range(0, width, 1024)]
+        return self.grad.at[self.tiles, index]
+
+
+def pieces_of(shape):
+    most = 1 if shape[2] > 256 else 4
+    return [(start, min(most, shape[0] - start)) for start in range(0, shape[0], most)]
+
+
+def piece_order(shapes):
+    parts = [[(number,) + p for p in pieces_of(shape)] for number, shape in enumerate(shapes)]
+    turns = [p for both in zip(parts[1], parts[2]) for p in both]
+    return parts[0] + turns + [p for part in parts[3:] for p in part]
+
+
+class Pipeline:
+    gaps = (0, 1, 2, 2, 2, 2, 2)
+
+    def __init__(self, reduce, count):
+        self.reduce, self.count = reduce, count
+        self.done, self.ready = [0] * reduce.levels, 0
+
+    def tick(self):
+        before = [self.ready] + list(self.done)
+        for level, gap in enumerate(self.gaps):
+            limit = before[level]
+            if level and limit < self.count:
+                limit = limit - gap + 1
+            if self.done[level] < limit:
+                self.reduce.stage(self.done[level], level)
+                self.done[level] += 1
+
+    def drain(self):
+        while self.done[-1] < self.count:
+            self.tick()
 
 
 def rms_back(values, cotangent, gain, carry, out, gain_grad):
@@ -1267,18 +1297,14 @@
     count = 36
 
 
-def backward_kernel(names, shared, *refs):
+def backward_kernel(shared, *refs):
     given, refs = refs[: Given.count], refs[Given.count :]
-    n = len(names)
-    grads, refs = (given[Given.grad_fd],) + refs[: n - 1], refs[n - 1 :]
-    outs, refs = refs[:n], refs[n:]
+    grads, refs = (given[Given.grad_fd],) + refs[:11], refs[11:]
+    kept_states, refs = refs[0], refs[1:]
+    outs, refs = refs[:12], refs[12:]
     (encoder_out, layer_out, hidden_out), refs = refs[:3], refs[3:]
-    pieces = []
-    for grad, out in zip(grads, outs):
-        for start, width in pieces_of(grad.shape[2]) if grad.shape[1] < 256 else thirds(grad.shape[2]):
-            pieces.append(Piece(grad, out, start, width))
-    order = piece_order(len(pieces))
-    pieces = [pieces[i] for i in order]
+    order = piece_order([g.shape for g in grads])
+    pieces = [Piece(grads[n], outs[n], start, tiles) for n, start, tiles in order]
     count = len(pieces)
     buffers, refs = [refs[7 * i : 7 * i + 7] for i in range(count)], refs[7 * count :]
     loads = [refs[shared[i]] for i in range(count)]
@@ -1316,62 +1342,56 @@
         line_recv,
         load_sems,
         stage_sems,
-        out_sem,
+        out_sems,
     ) = refs
     rank, core, along_x, along_y, depth = place()
     reduce = Reduce(pieces, buffers, loads, send_sems, recv_sems, local_sems)
     column = column_partners(rank, depth)
     greet([reduce.to_x, reduce.to_y, reduce.to_core] + column)
-    ticks = iter(range(count + reduce.levels - 1))
-
-    def tick():
-        step = next(ticks)
-        for level in range(reduce.levels):
-            if 0 <= step - level < count:
-                reduce.stage(step - level, level)
-
-    def fetch(*pairs):
-        copies = [
-            pltpu.make_async_copy(source, target, load_sems.at[i])
-            for i, (source, target) in enumerate(pairs)
-        ]
-        for copy in copies:
-            copy.start()
+    pipeline = Pipeline(reduce, count)
+    tick = pipeline.tick
+    numbers = [n for n, unused_start, unused_tiles in order]
+    pipeline.ready = numbers.count(0)
+    turn_of = iter(range(1 << 20))
+
+    def begin(*pairs):
+        copies = []
+        for source, target in pairs:
+            sem = load_sems.at[next(turn_of) % load_sems.shape[0]]
+            copies.append(pltpu.make_async_copy(source, target, sem))
+            copies[-1].start()
+        return copies
+
+    def end(copies):
         for copy in copies:
             copy.wait()
 
     def staged(buffers_of, target_of, values, tiles):
+        slots = buffers_of.shape[0]
+
         def copy(index):
-            slot = lax.rem(index, 2)
+            slot = lax.rem(index, slots)
             return pltpu.make_async_copy(buffers_of.at[slot], target_of(index), stage_sems.at[slot])
 
         def one(index):
-            @pl.when(index >= 2)
+            @pl.when(index >= slots)
             def _():
-                copy(index - 2).wait()
-
-            buffers_of[lax.rem(index, 2)] = values(tile(index))
+                copy(index - slots).wait()
+
+            buffers_of[lax.rem(index, slots)] = values(tile(index))
             copy(index).start()
 
         each(tiles, one)
-        for index in range(max(0, tiles - 2), tiles):
+        for index in range(max(0, tiles - slots), tiles):
             copy(jnp.int32(index)).wait()
 
-    def weight_grad(number, right, start=0, width=None, flipped=False):
-        width = grads[number].shape[2] if width is None else width
-
+    def weight_grad(number, right, start=0):
         def values(at):
-            if flipped:
-                result = product_right(left[...], right[at, :])
-            else:
-                result = product(left[:, 0 : right.shape[0]], right[:, at])
+            result = product(left[...], right[:, at])
             return result.astype(jnp.bfloat16).reshape(stage.shape[1:])
 
-        def target(index):
-            column_start = pl.multiple_of(start + index * 256, 256)
-            return grads[number].at[:, :, pl.ds(column_start, 256)]
-
-        staged(stage, target, values, width // 256)
+        staged(stage, lambda index: grads[number].at[start + index], values, right.shape[1] // 256)
+        pipeline.ready += 1
 
     def send_back(number, rows):
         def write(index):
@@ -1410,7 +1430,7 @@
     def norm_grad(values, gain, carry, out):
         rms_back(values, grad_n, gains[gain : gain + 1, :], carry, out, gain_grad)
         for slot in range(8):
-            small_grads[slot, gain : gain + 1, :] = gain_grad[:, 128 * slot : 128 * slot + 128]
+            small_grads[0, slot, gain : gain + 1, :] = gain_grad[:, 128 * slot : 128 * slot + 128]
 
     def round_rows(source, target):
         def one(index):
@@ -1435,40 +1455,46 @@
 
         each(weights.shape[0] // 256, one)
 
+    def feed_loads(start, tiles):
+        at = pl.ds(256 * start, 256 * tiles)
+        width = 256 * tiles
+        return begin(
+            (given[Given.w_fd].at[at], one_w.at[0:width]),
+            (given[Given.slope].at[:, at], value.at[:, 0:width]),
+            (given[Given.gelu].at[:, at], other.at[:, 0:width]),
+            (given[Given.w].at[:, at], half_a.at[:, 0:width]),
+            (given[Given.w_fg].at[:, at], two_w.at[:, 0:width]),
+            (given[Given.w_fu].at[:, at], three_w.at[:, 0:width]),
+        )
+
     tick()
-    fetch(
+    first = begin(
         (given[Given.cot], cot),
-        (given[Given.normed3_t], left),
+        (given[Given.smalls], smalls),
         (given[Given.chosen_t], chosen_t),
         (given[Given.spread], spread),
-        (given[Given.smalls], smalls),
-    )
+        (given[Given.normed3_t], left),
+    )
+    feeds = pieces_of(grads[1].shape)
+    loaded = feed_loads(*feeds[0])
+    tick()
+    end(first)
     for slot in range(8):
         gains[0:3, 128 * slot : 128 * slot + 128] = smalls[16 * slot : 16 * slot + 3, :]
     small_grads[...] = jnp.zeros_like(small_grads)
-    tick()
-    for start, width in pieces_of(given[Given.w].shape[1]):
-        at = pl.ds(start, width)
+    for turn_number, (start, tiles) in enumerate(feeds):
+        width = 256 * tiles
         down, gate, up = one_w.at[0:width], two_w.at[:, 0:width], three_w.at[:, 0:width]
         part = half_a.at[:, 0:width]
         slope, gelu = value.at[:, 0:width], other.at[:, 0:width]
         gate_grad, up_grad = half_b.at[:, 0:width], half_c.at[:, 0:width]
-        fetch(
-            (given[Given.w_fd].at[at], down),
-            (given[Given.w_fg].at[:, at], gate),
-            (given[Given.w_fu].at[:, at], up),
-            (given[Given.w].at[:, at], part),
-            (given[Given.slope].at[:, at], slope),
-            (given[Given.gelu].at[:, at], gelu),
-        )
+        end(loaded)
 
         def split(at, grad_w):
             gate_grad[:, at] = (grad_w * slope[:, at]).astype(jnp.bfloat16)
             up_grad[:, at] = (grad_w * gelu[:, at]).astype(jnp.bfloat16)
 
         through(cot, down, split)
-        weight_grad(1, gate_grad, start, width)
-        weight_grad(2, up_grad, start, width)
 
         def add(index):
             at = tile(index)
@@ -1480,30 +1506,41 @@
             grad_n[:, at] = back
 
         each(grad_x.shape[1] // 256, add)
+        if turn_number + 1 < len(feeds):
+            loaded = feed_loads(*feeds[turn_number + 1])
+        else:
+            loaded = begin(
+                (given[Given.after2], value),
+                (given[Given.w_co], one_w),
+                (given[Given.cq_t], turned_q),
+                (given[Given.ck], two_w.at[0:512]),
+                (given[Given.cv], two_w.at[512:1024]),
+            )
         tick()
-
-    fetch(
-        (given[Given.after2], value),
-        (given[Given.o2_t], left),
-        (given[Given.w_co], one_w),
-        (given[Given.cq], half_c),
-        (given[Given.cq_t], turned_q),
-        (given[Given.ck], two_w.at[0:512]),
-        (given[Given.cv], two_w.at[512:1024]),
-    )
-
-    def layer(index):
+        weight_grad(1, gate_grad, start)
+        weight_grad(2, up_grad, start)
+        tick()
+
+    loaded += begin((given[Given.o2_t], left), (given[Given.cq], half_c))
+    end(loaded)
+
+    def last(index):
         at = tile(index, 32)
         half_a[at, :] = (value[at, :] + grad_x[at, :]).astype(jnp.bfloat16)
 
-    each(value.shape[0] // 32, layer)
+    each(value.shape[0] // 32, last)
     send_back(0, half_a)
     norm_grad(value, 2, cot, grad_x)
     round_rows(grad_x, half_a)
+    tick()
     weight_grad(3, half_a)
     head_grads(one_w)
     tick()
     keys_grad, values_grad = three_w.at[:, 0:512], three_w.at[:, 512:1024]
+    states = one_w.at[:, 0:512]
+    loaded = begin(
+        (given[Given.states_t], states), (given[Given.normed2_t], left), (given[Given.after], value)
+    )
 
     def cross(first, last):
         attend_back_heads(
@@ -1522,53 +1559,48 @@
             None,
         )
 
-    cross(0, 4)
+    cross(0, 3)
     tick()
-    cross(4, 8)
+    cross(3, 6)
     tick()
-    states = one_w.at[:, 0:512]
-    fetch((given[Given.states_t], states))
+    cross(6, 8)
+    end(loaded)
 
     def state_grad(number, right):
         def values(at):
             result = product_right(states[...], right[at, :])
             return result.astype(jnp.bfloat16).reshape(stage.shape[1:])
 
-        def target(index):
-            return grads[number].at[:, :, tile(index)]
-
-        staged(stage, target, values, 4)
+        staged(stage, lambda index: grads[number].at[index], values, 4)
+        pipeline.ready += 1
 
     state_grad(4, keys_grad)
     state_grad(5, values_grad)
+    tick()
     turn(keys_grad, two_w.at[0:512])
     turn(values_grad, two_w.at[512:1024])
-    fetch((given[Given.w_ck], one_w), (given[Given.w_cv], three_w), (given[Given.normed2_t], left))
-    tick()
-    staged(
-        state_stage,
-        lambda index: encoder_out.at[:, tile(index)],
-        lambda at: product_right(two_w[0:512], one_w[at, :])
-        + product_right(two_w[512:1024], three_w[at, :]),
-        4,
-    )
-    fetch(
+    kept = pltpu.make_async_copy(two_w, kept_states, out_sems.at[0])
+    kept.start()
+    loaded = begin(
         (given[Given.w_cq], one_w),
         (given[Given.w_so], three_w),
-        (given[Given.after], value),
         (given[Given.q], half_c),
         (given[Given.q_t], turned_q),
-        (given[Given.k], two_w.at[0:256]),
-        (given[Given.u], two_w.at[256:512]),
-    )
-    tick()
+    )
     weight_grad(6, half_d)
+    kept.wait()
+    end(loaded)
+    loaded = begin((given[Given.k], two_w.at[0:256]), (given[Given.u], two_w.at[256:512]))
     through(half_d, one_w, store_as(grad_n))
+    loaded += begin((given[Given.o1_t], left))
     norm_grad(value, 1, grad_x, grad_x)
     round_rows(grad_x, half_a)
-    fetch((given[Given.o1_t], left))
+    end(loaded)
+    loaded = begin((given[Given.inputs], value), (given[Given.w_sq], one_w))
+    tick()
     weight_grad(7, half_a)
     head_grads(three_w)
+    loaded += begin((given[Given.normed_t], left))
     tick()
 
     def table_grad(index, half, grad_s):
@@ -1580,7 +1612,7 @@
             precision=highest,
             preferred_element_type=jnp.float32,
         )
-        small_grads[index, 3:4, :] = small_grads[index, 3:4, :] + table[0:1]
+        small_grads[0, index, 3:4, :] = small_grads[0, index, 3:4, :] + table[0:1]
 
     keys_grad, values_grad = three_w.at[:, 0:256], three_w.at[:, 256:512]
 
@@ -1606,18 +1638,14 @@
     own(4, 8)
     turn(keys_grad, half_a)
     turn(values_grad, half_b)
+    end(loaded)
+    loaded = begin((given[Given.w_sk], two_w), (given[Given.w_sv], three_w))
     tick()
-    fetch(
-        (given[Given.normed_t], left),
-        (given[Given.inputs], value),
-        (given[Given.w_sq], one_w),
-        (given[Given.w_sk], two_w),
-        (given[Given.w_sv], three_w),
-    )
     weight_grad(8, half_d)
     weight_grad(9, half_a)
     weight_grad(10, half_b)
     tick()
+    end(loaded)
 
     def sum_three(index):
         at = tile(index)
@@ -1628,58 +1656,57 @@
         )
 
     each(grad_n.shape[1] // 256, sum_three)
+    loaded = begin((given[Given.w_ck], one_w), (given[Given.w_cv], three_w), (kept_states, two_w))
     norm_grad(value, 0, grad_x, half_c)
-    small_copy = pltpu.make_async_copy(small_grads, grads[11], out_sem)
+    small_copy = pltpu.make_async_copy(small_grads, grads[11], out_sems.at[1])
     small_copy.start()
     small_copy.wait()
+    pipeline.ready += 1
+    tick()
     send_back(1, half_c)
-    for unused in range(count + reduce.levels):
-        try:
-            tick()
-        except StopIteration:
-            break
+    tick()
+    end(loaded)
+    staged(
+        state_stage,
+        lambda index: encoder_out.at[:, tile(index)],
+        lambda at: product_right(two_w[0:512], one_w[at, :])
+        + product_right(two_w[512:1024], three_w[at, :]),
+        4,
+    )
     receive_back(0, layer_out)
+    pipeline.drain()
     receive_back(1, hidden_out)
     for number in range(count):
         reduce.write(number).wait()
-
-
-def thirds(width):
-    return [(0, 384), (384, 384), (768, width - 768)]
-
-
-def piece_order(count):
-    return [0, 1, 2, 3, 6, 4, 7, 5, 8] + list(range(9, count))
 
 
 def backward_call(operands, rows):
     count = Given.count
     anywhere = pl.BlockSpec(memory_space=pl.ANY)
     vmem = pl.BlockSpec(memory_space=pltpu.VMEM)
+    bf16, f32 = jnp.bfloat16, jnp.float32
     grad_fd = operands[Given.grad_fd]
     width, wide = operands[Given.w_fg].shape
-    square = jax.ShapeDtypeStruct((8, width // 8, width), jnp.bfloat16)
-    broad = jax.ShapeDtypeStruct((8, width // 8, wide), jnp.bfloat16)
-    small = jax.ShapeDtypeStruct((8, 16, 128), jnp.float32)
+    square = jax.ShapeDtypeStruct((width // 256, 8, width // 8, 256), bf16)
+    broad = jax.ShapeDtypeStruct((wide // 256, 8, width // 8, 256), bf16)
+    small = jax.ShapeDtypeStruct((1, 8, 16, 128), f32)
     full = [jax.ShapeDtypeStruct(grad_fd.shape, grad_fd.dtype), broad, broad] + [square] * 8 + [small]
-    outs = [jax.ShapeDtypeStruct(g.shape[1:], g.dtype) for g in full]
+    outs = [jax.ShapeDtypeStruct(g.shape[:1] + g.shape[2:], g.dtype) for g in full]
     most = operands[Given.inputs].shape[0]
     states = operands[Given.ck].shape[0]
     total = operands[Given.chosen_t].shape[0]
+    kept_states = jax.ShapeDtypeStruct((2 * states, width), bf16)
     tail = [
-        jax.ShapeDtypeStruct((states, width), jnp.float32),
-        jax.ShapeDtypeStruct((rows, width), jnp.bfloat16),
-        jax.ShapeDtypeStruct((rows, width), jnp.bfloat16),
+        jax.ShapeDtypeStruct((states, width), f32),
+        jax.ShapeDtypeStruct((rows, width), bf16),
+        jax.ShapeDtypeStruct((rows, width), bf16),
     ]
-    shapes = []
-    for grad in full:
-        for start, part in pieces_of(grad.shape[2]) if grad.shape[1] < 256 else thirds(grad.shape[2]):
-            shapes.append(((grad.shape[1], part), grad.dtype))
-    shapes = [shapes[i] for i in piece_order(len(shapes))]
-    scratch, load_shapes, shared, turns = [], [], [], []
-    for shape, dtype in shapes:
-        scratch += buffer_shapes(shape[0], shape[1], dtype)
-        key = ((2,) + shape, dtype)
+    scratch, load_shapes, shared = [], [], []
+    order = piece_order([g.shape for g in full])
+    for number, unused, tiles in order:
+        shape = (tiles,) + full[number].shape[2:]
+        scratch += buffer_shapes(*shape, full[number].dtype)
+        key = ((2,) + shape, full[number].dtype)
         held = [i for i, s in enumerate(load_shapes) if s == key]
         if len(held) < 2:
             shared.append(len(load_shapes))
@@ -1688,12 +1715,11 @@
             last = [i for i in shared if i in held][-1]
             shared.append(held[0] if last == held[1] else held[1])
     scratch += [pltpu.VMEM(*s) for s in load_shapes]
-    pieces = len(shapes)
-    bf16, f32 = jnp.bfloat16, jnp.float32
+    pieces = len(order)
     scratch += [pltpu.VMEM((width, width), bf16)] * 3
     scratch += [
         pltpu.VMEM((2, DOCS, total // DOCS, width), bf16),
-        pltpu.VMEM((2, 8, width // 8, 256), bf16),
+        pltpu.VMEM((3, 8, width // 8, 256), bf16),
         pltpu.VMEM((2, states, 256), f32),
     ]
     scratch += [pltpu.VMEM((most, width), f32)] * 4
@@ -1705,27 +1731,53 @@
         pltpu.VMEM((128, 128), f32),
         pltpu.VMEM((8, width), f32),
         pltpu.VMEM((1, width), f32),
-        pltpu.VMEM((8, 16, 128), f32),
+        pltpu.VMEM((1, 8, 16, 128), f32),
         pltpu.VMEM((2, DOCS - 1, rows, width), bf16),
         pltpu.SemaphoreType.DMA((pieces, 12)),
         pltpu.SemaphoreType.DMA((pieces, 12)),
         pltpu.SemaphoreType.DMA((pieces, 5)),
         pltpu.SemaphoreType.DMA((2, DOCS - 1)),
         pltpu.SemaphoreType.DMA((2, DOCS - 1)),
-        pltpu.SemaphoreType.DMA((8,)),
+        pltpu.SemaphoreType.DMA((16,)),
+        pltpu.SemaphoreType.DMA((3,)),
         pltpu.SemaphoreType.DMA((2,)),
-        pltpu.SemaphoreType.DMA,
     ]
-    return pl.pallas_call(
-        functools.partial(backward_kernel, range(12), shared),
-        out_shape=full[1:] + outs + tail,
+    results = pl.pallas_call(
+        functools.partial(backward_kernel, shared),
+        out_shape=full[1:] + [kept_states] + outs + tail,
         in_specs=[anywhere] * count,
-        out_specs=[anywhere] * (len(full) - 1 + len(outs) + 1) + [vmem] * 2,
+        out_specs=[anywhere] * (len(full) + len(outs) + 1) + [vmem] * 2,
         scratch_shapes=scratch,
         compiler_params=pltpu.CompilerParams(
             collective_id=2, has_side_effects=True, vmem_limit_bytes=67043328
         ),
         name="backward",
+    )(*operands)
+    return results[len(full) :]
+
+
+def widen_kernel(*refs):
+    half = len(refs) // 2
+    for source, target in zip(refs[:half], refs[half:]):
+        if len(source.shape) == 2:
+            target[...] = source[...].astype(target.dtype)
+            continue
+        for part in range(source.shape[0]):
+            target[:, 256 * part : 256 * part + 256] = source[part].astype(target.dtype)
+
+
+def widen_call(sums, layer_out, hidden_grad):
+    operands = list(sums) + [layer_out, hidden_grad]
+    shapes = [jax.ShapeDtypeStruct((s.shape[1], s.shape[0] * s.shape[2]), jnp.float32) for s in sums]
+    shapes.append(jax.ShapeDtypeStruct(layer_out.shape, layer_out.dtype))
+    shapes.append(jax.ShapeDtypeStruct(hidden_grad.shape, jnp.float32))
+    vmem = pl.BlockSpec(memory_space=pltpu.VMEM)
+    return pl.pallas_call(
+        widen_kernel,
+        out_shape=shapes,
+        in_specs=[vmem] * len(operands),
+        out_specs=[vmem] * len(operands),
+        name="widen",
     )(*operands)
 
 
@@ -1800,7 +1852,7 @@
         spread,
     )
     kept = results[12:]
-    grad_fd = results[-1].reshape(8, -1, width)
+    grad_fd = results[-1].reshape(width // 256, 8, -1, 256)
     forward_side = [
         kept[i]
         for i in (
@@ -1829,12 +1881,15 @@
     ]
     results = backward_call(
         forward_side + [chosen.T, spread] + list(results[:12]) + [grad_fd], hidden_in.shape[1]
-    )[11:]
-    fd, fg, fu, co, ck, cv, cq, so, sq, sk, sv = (r.astype(jnp.float32) for r in results[:11])
+    )
     smalls, encoder_grad, layer_out, hidden_grad = results[11:]
+    fd, fg, fu, co, ck, cv, cq, so, sq, sk, sv, layer_out, hidden_grad = widen_call(
+        results[:11], layer_out, hidden_grad
+    )
+    smalls = smalls[0]
     return (
         layer_out[None],
-        hidden_grad.astype(jnp.float32)[None],
+        hidden_grad[None],
         encoder_grad[None],
         sq,
         sk,

time: 444 us -> 412 us (0.928)
  Pallas kernels: 414 us -> 398 us
  other arithmetic: 21.1 us -> 6.98 us
    pallas_call x1 -> x2, Pallas kernels: 248 us -> 232 us  [the longest x1 226 us: backward_call(): pl.pallas_call(functools.partial(backward_kernel, shared), out_shape=full...]
    convert_element_type x11 -> x0, other arithmetic: 12.4 us -> none  [by_document(): r.astype(jnp.float32)]
where the time goes in v3:
time: 412 us; the launch traced here: 411 us
  Pallas kernels  398 us (97%)
  other arithmetic  6.98 us (2%)
  local copies, waits for them, and re-layouts  5.72 us (1%)
    pallas_call x1, Pallas kernels, backward_call(): pl.pallas_call(functools.partial(backward_kernel, shared), out_shape=full...  226 us
    pallas_call x1, Pallas kernels, forward_call(): pl.pallas_call(functools.partial(forward_kernel, count), out_shape=shapes...  166 us

profile of v3, /device:TPU:0, one launch (start us, length us, event | category | flops | bytes accessed | tf_op | source)
XLA Modules:
  0.0 411.4 jit_solution(13220268390664716289)
XLA Ops:
  0.7 1.2 constant_dynamic-slice_fusion
  1.9 0.7 pad_bitcast_fusion
  2.6 2.0 fusion.13
  4.5 0.6 iota_compare_fusion.5
  5.2 0.7 iota_add_fusion
  5.9 1.3 fusion.11.refs_0_
  7.2 0.7 add_convert_fusion.refs_16_.refs_22_
  7.9 0.8 fusion.3.refs_21_
  8.7 0.9 fusion.1.refs_14_
  9.6 166.3 %forward.1 = (f32[128,128]{1,0:T(8,128)}, bf16[1024,1024]{1,0:T(8,128)(2,1)}, bf16[1024,1024]{1,0:T(8,128)(2,1)}, bf16[1024,1024]{1,0:T(8,128)(2,1)}, bf16[1024,...) custom-call(f32[16,128]{1,0:T(8,128)} %fusion.11.refs_0_, ...), custom_call_target="tpu_custom_call" | custom-call | tf_op jit(solution)/shard_map/forward/pallas_call | solution.py:916
  175.9 225.6 %backward.1 = (bf16[11,8,128,256]{3,2,1,0:T(8,128)(2,1)}, bf16[11,8,128,256]{3,2,1,0:T(8,128)(2,1)}, bf16[4,8,128,256]{3,2,1,0:T(8,128)(2,1)}, bf16[4,8,128,256]...) custom-call(f32[256,1024]{1,0:T(8,128)} %get-tuple-element.80.refs_0, ...), custom_call_target="tpu_custom_call" | custom-call | tf_op jit(solution)/shard_map/backward/pallas_call | solution.py:1745
  401.4 1.2 slice_bitcast_fusion
  402.6 1.3 slice_bitcast_fusion.1
  403.9 0.0 copy-start
  403.9 6.1 %widen.1 = (f32[352,1024]{1,0:T(8,128)}, f32[128,2816]{1,0:T(8,128)}, f32[128,2816]{1,0:T(8,128)}, f32[128,1024]{1,0:T(8,128)}, f32[128,1024]{1,0:T(8,128)}, /*i...) custom-call(bf16[4,352,256]{2,1,0:T(8,128)(2,1)} %get-tuple-element., ...), custom_call_target="tpu_custom_call" | custom-call | tf_op jit(solution)/shard_map/widen/pallas_call | solution.py:1775
  410.1 0.0 copy-done
  410.1 1.3 copy.39
  (3 shorter events, 0.1 us)
Async XLA Ops:
  403.9 6.1 %copy-start = (f32[512,1024]{1,0:T(8,128)S(1)}, f32[512,1024]{1,0:T(8,128)}, u32[]{:S(2)}) copy-start(f32[512,1024]{1,0:T(8,128)} %get-tuple-element.129) | copy-start | bytes 6291460

commit v4 on v3

--- a/solution.py
+++ b/solution.py
@@ -527,10 +527,28 @@
     )
 
 
+class Unit:
+    def __init__(self, number, start, rows, flat, first, last):
+        self.number, self.start, self.rows = number, start, rows
+        self.flat, self.first, self.last = flat, first, last
+
+
+def units_of(shapes, flat_count):
+    units = []
+    for number, (rows, columns) in enumerate(shapes):
+        parts = max(1, rows * columns // (176 * 1024)) if number < len(shapes) - 1 else 4
+        most = -(-rows // parts // 16) * 16
+        starts = list(range(0, rows, most))
+        for start in starts:
+            size = min(most, rows - start)
+            units.append(Unit(number, start, size, number < flat_count, start == 0, start == starts[-1]))
+    return units
+
+
 class Gather:
-    def __init__(self, owns, fulls, send_sems, recv_sems, local_sems):
+    def __init__(self, units, owns, fulls, send_sems, recv_sems, local_sems):
         rank, core, along_x, along_y, depth = place()
-        self.owns, self.fulls = owns, fulls
+        self.units, self.owns, self.fulls = units, owns, fulls
         self.send_sems, self.recv_sems, self.local_sems = send_sems, recv_sems, local_sems
         self.rank = rank
         self.by_x = rank + 2 - 4 * along_x
@@ -540,27 +558,35 @@
         self.to_y = (self.by_y, depth)
         self.to_core = (rank + 1 - 2 * core, depth)
         self.shift = 1 - 2 * core
-
-    def rows(self, number, slot, half):
-        size = self.owns[number].shape[0]
-        start = pl.multiple_of(slot * size, size)
-        if half is None:
-            return self.fulls[number].at[pl.ds(start, size)]
-        size = size // 2
-        return self.fulls[number].at[pl.ds(pl.multiple_of(start + half * size, size), size)]
-
-    def copy(self, number, kind, slot, half, device, own=False):
-        target = self.rows(number, slot, half)
+        odd = lax.rem(depth, 2)
+        self.odd = odd == 1
+        self.to_pair = (rank, depth + 1 - 2 * odd)
+        self.second = self.by_x + odd * (self.diag - self.by_x)
+        self.third = self.diag + odd * (self.by_x - self.diag)
+
+    def rows(self, index, slot, half):
+        unit = self.units[index]
+        size = self.owns[unit.number].shape[0]
+        start = pl.multiple_of(slot * size + unit.start, math.gcd(size, unit.start))
+        rows = unit.rows
+        if half is not None:
+            rows = rows // 2
+            start = pl.multiple_of(start + half * rows, math.gcd(size, unit.start, rows))
+        return self.fulls[unit.number].at[pl.ds(start, rows)]
+
+    def copy(self, index, kind, slot, half, device, own=False):
+        target = self.rows(index, slot, half)
+        unit = self.units[index]
         return remote(
-            self.owns[number] if own else target,
+            self.owns[unit.number].at[pl.ds(unit.start, unit.rows)] if own else target,
             target,
-            self.send_sems.at[number, kind],
-            self.recv_sems.at[number, kind],
+            self.send_sems.at[index, kind],
+            self.recv_sems.at[index, kind],
             device,
         )
 
-    def sent(self, number, kind):
-        slot, half, device = (
+    def sent(self, index, kind):
+        flat = (
             (self.rank, None, self.to_x),
             (self.rank, None, self.to_y),
             (self.rank, None, self.to_core),
@@ -570,12 +596,23 @@
             (self.by_y, None, self.to_core),
             (self.diag, 0, self.to_core),
             (self.diag, 1, self.to_core),
-        )[kind]
-        return self.copy(number, kind, slot, half, device, kind < 3)
-
-    def landed(self, number, kind):
+        )
+        line = (
+            (self.rank, None, self.to_x),
+            (self.rank, None, self.to_y),
+            (self.rank, None, self.to_core),
+            (self.by_y, None, self.to_x),
+            (self.second, None, self.to_pair),
+            (self.by_y, None, self.to_core),
+            (self.second, None, self.to_core),
+            (self.third, None, self.to_core),
+        )
+        slot, half, device = (flat if self.units[index].flat else line)[kind]
+        return self.copy(index, kind, slot, half, device, kind < 3)
+
+    def landed(self, index, kind):
         shift = self.shift
-        slot, half, device = (
+        flat = (
             (self.by_x, None, self.to_x),
             (self.by_y, None, self.to_y),
             (self.rank + shift, None, self.to_core),
@@ -585,39 +622,87 @@
             (self.by_y + shift, None, self.to_core),
             (self.diag + shift, 0, self.to_core),
             (self.diag + shift, 1, self.to_core),
-        )[kind]
-        return self.copy(number, kind, slot, half, device)
+        )
+        line = (
+            (self.by_x, None, self.to_x),
+            (self.by_y, None, self.to_y),
+            (self.rank + shift, None, self.to_core),
+            (self.diag, None, self.to_x),
+            (self.third, None, self.to_pair),
+            (self.by_y + shift, None, self.to_core),
+            (self.second + shift, None, self.to_core),
+            (self.third + shift, None, self.to_core),
+        )
+        slot, half, device = (flat if self.units[index].flat else line)[kind]
+        return self.copy(index, kind, slot, half, device)
 
     def local(self, number):
-        return pltpu.make_async_copy(
-            self.owns[number], self.rows(number, self.rank, None), self.local_sems.at[number]
+        size = self.owns[number].shape[0]
+        start = pl.multiple_of(self.rank * size, size)
+        target = self.fulls[number].at[pl.ds(start, size)]
+        return pltpu.make_async_copy(self.owns[number], target, self.local_sems.at[number])
+
+    def by_pair(self, even, odd):
+        pl.when(jnp.logical_not(self.odd))(even)
+        pl.when(self.odd)(odd)
+
+    def issue(self, index):
+        unit = self.units[index]
+        self.sent(index, 1).start()
+        if unit.flat:
+            self.sent(index, 0).start()
+        else:
+            pl.when(jnp.logical_not(self.odd))(lambda: self.sent(index, 0).start())
+        self.sent(index, 2).start()
+        if unit.first:
+            self.local(unit.number).start()
+
+    def relay(self, index):
+        if self.units[index].flat:
+            self.landed(index, 0).wait_recv()
+            self.sent(index, 3).start()
+            self.landed(index, 1).wait_recv()
+            self.sent(index, 4).start()
+            self.sent(index, 5).start()
+            self.sent(index, 6).start()
+            return
+        self.landed(index, 1).wait_recv()
+        pl.when(self.odd)(lambda: self.sent(index, 3).start())
+        self.sent(index, 5).start()
+
+    def spread(self, index):
+        if self.units[index].flat:
+            self.landed(index, 3).wait_recv()
+            self.sent(index, 7).start()
+            self.landed(index, 4).wait_recv()
+            self.sent(index, 8).start()
+            return
+        self.by_pair(
+            lambda: self.landed(index, 0).wait_recv(), lambda: self.landed(index, 3).wait_recv()
         )
-
-    def issue(self, number):
-        for kind in range(3):
-            self.sent(number, kind).start()
-        self.local(number).start()
-
-    def relay(self, number):
-        self.landed(number, 0).wait_recv()
-        self.sent(number, 3).start()
-        self.landed(number, 1).wait_recv()
-        self.sent(number, 4).start()
-        self.sent(number, 5).start()
-        self.sent(number, 6).start()
-
-    def spread(self, number):
-        self.landed(number, 3).wait_recv()
-        self.sent(number, 7).start()
-        self.landed(number, 4).wait_recv()
-        self.sent(number, 8).start()
-
-    def finish(self, number):
-        for kind in (2, 5, 6, 7, 8):
-            self.landed(number, kind).wait_recv()
-        for kind in range(9):
-            self.sent(number, kind).wait_send()
-        self.local(number).wait()
+        self.sent(index, 4).start()
+        self.sent(index, 6).start()
+
+    def close(self, index):
+        if not self.units[index].flat:
+            self.landed(index, 4).wait_recv()
+            self.sent(index, 7).start()
+
+    def finish(self, index):
+        unit = self.units[index]
+        for kind in (2, 5, 6, 7, 8) if unit.flat else (2, 5, 6, 7):
+            self.landed(index, kind).wait_recv()
+        if unit.flat:
+            for kind in range(9):
+                self.sent(index, kind).wait_send()
+        else:
+            self.by_pair(
+                lambda: self.sent(index, 0).wait_send(), lambda: self.sent(index, 3).wait_send()
+            )
+            for kind in (1, 2, 4, 5, 6, 7):
+                self.sent(index, kind).wait_send()
+        if unit.last:
+            self.local(unit.number).wait()
 
 
 def column_partners(rank, depth):
@@ -717,7 +802,23 @@
     inside = (1, 5, 7, 11, 13)
 
 
-def forward_kernel(count, *refs):
+class Steps:
+    lags = (0, 3, 5, 7, 8)
+
+    def __init__(self, gather):
+        self.gather, self.step, self.finished = gather, 0, 0
+
+    def advance(self):
+        gather, count = self.gather, len(self.gather.units)
+        stages = (gather.issue, gather.relay, gather.spread, gather.close, gather.finish)
+        for stage, lag in zip(stages, self.lags):
+            if 0 <= self.step - lag < count:
+                stage(self.step - lag)
+        self.step += 1
+        self.finished = min(max(0, self.step - self.lags[-1]), count)
+
+
+def forward_kernel(count, units, *refs):
     owns, refs = refs[:count], refs[count:]
     (tokens, cotangent, chosen, encoded, spread), refs = refs[:5], refs[5:]
     fulls, refs = refs[:count], refs[count:]
@@ -743,7 +844,7 @@
         save_sems,
     ) = refs
     rank, core, along_x, along_y, depth = place()
-    gather = Gather(owns, fulls, send_sems, recv_sems, local_sems)
+    gather = Gather(units, owns, fulls, send_sems, recv_sems, local_sems)
     column = column_partners(rank, depth)
     greet([gather.to_x, gather.to_y, gather.to_core] + column)
 
@@ -769,6 +870,10 @@
         for copy in sends:
             copy.wait_send()
 
+    steps = Steps(gather)
+    advance = steps.advance
+    lasts = [index for index, unit in enumerate(units) if unit.last]
+    advance()
     for number in range(2):
         here, sends, unused = line_copies(number)
         here.start()
@@ -784,37 +889,46 @@
             return
         pltpu.make_async_copy(keep[name], outs[name], save_sems.at[name]).start()
 
-    def load(number, buffer):
-        copy = pltpu.make_async_copy(fulls[number], buffer, load_sems.at[number])
-        copy.start()
+    def load(number):
+        if number == 0:
+            buffer = smalls
+        else:
+            buffer = (square if fulls[number].shape[1] == square.shape[2] else wide).at[number % 2]
+        return (pltpu.make_async_copy(fulls[number], buffer, load_sems.at[number]), buffer)
+
+    def loaded(number):
+        copy, buffer = load(number)
         copy.wait()
+        return buffer
 
     def project(left, number, name):
-        load(number, square)
-        by_columns(left, square, store_as(keep[name]))
+        by_columns(left, loaded(number), store_as(keep[name]))
         save(name)
 
     def residual(before, left, number, name, gain, normed, turned):
-        load(number, square)
+        weight = loaded(number)
 
         def write(at, value):
             keep[name][:, at] = keep[before][:, at] + value
 
-        by_columns(keep[left], square, write)
+        by_columns(keep[left], weight, write)
         save(name)
         rms_rows(keep[name], gains[gain : gain + 1, :], keep[normed])
         flip(keep[normed], turned)
 
     def start():
-        load(0, smalls)
+        loaded(0)
         for slot in range(8):
             gains[0:3, 128 * slot : 128 * slot + 128] = smalls[16 * slot : 16 * slot + 3, :]
+        flip(encoded, Kept.states_t)
+
+    def values_and_tokens():
+        project(encoded, 2, Kept.cv)
         line_finish(0)
         by_columns(chosen, all_tokens, store_as(keep[Kept.inputs]))
         save(Kept.inputs)
         rms_rows(keep[Kept.inputs], gains[0:1, :], keep[Kept.normed])
         flip(keep[Kept.normed], Kept.normed_t)
-        flip(encoded, Kept.states_t)
 
     def keys():
         flip(keep[Kept.q], Kept.q_t)
@@ -822,6 +936,7 @@
 
     def self_heads():
         project(keep[Kept.normed], 5, Kept.u)
+        advance()
         attend_heads(
             keep[Kept.q], keep[Kept.k], keep[Kept.u], keep[Kept.o1], functools.partial(causal_bias, smalls, spread)
         )
@@ -830,6 +945,7 @@
     def cross_heads():
         project(keep[Kept.normed2], 7, Kept.cq)
         flip(keep[Kept.cq], Kept.cq_t)
+        advance()
         attend_heads(keep[Kept.cq], keep[Kept.ck], keep[Kept.cv], keep[Kept.o2], None)
         flip(keep[Kept.o2], Kept.o2_t)
         line_finish(1)
@@ -837,11 +953,10 @@
         save(Kept.cot)
 
     def gate():
-        load(9, wide)
-        by_columns(keep[Kept.normed3], wide, store_as(keep[Kept.slope]))
+        by_columns(keep[Kept.normed3], loaded(9), store_as(keep[Kept.slope]))
 
     def up():
-        load(10, wide)
+        weight = loaded(10)
         scale = math.sqrt(2.0 / math.pi)
 
         def write(at, b):
@@ -859,7 +974,14 @@
             for part in range(grad_fd.shape[0]):
                 grad_fd[part, at, :] = grad[:, 256 * part : 256 * part + 256]
 
-        by_columns(keep[Kept.normed3], wide, write)
+        def one(index):
+            at = tile(index)
+            write(at, product(keep[Kept.normed3][...], weight[:, at]))
+
+        tiles = weight.shape[1] // 256
+        for part in range(0, tiles, 3):
+            lax.fori_loop(part, min(part + 3, tiles), lambda index, unused: one(index), None)
+            advance()
         for name in (Kept.gelu, Kept.slope, Kept.w):
             save(name)
         pltpu.make_async_copy(grad_fd, grad_out, save_sems.at[n]).start()
@@ -867,7 +989,7 @@
     compute = (
         start,
         lambda: project(encoded, 1, Kept.ck),
-        lambda: project(encoded, 2, Kept.cv),
+        values_and_tokens,
         lambda: project(keep[Kept.normed], 3, Kept.q),
         keys,
         self_heads,
@@ -876,18 +998,16 @@
         lambda: residual(Kept.after, Kept.o2, 8, Kept.after2, 2, Kept.normed3, Kept.normed3_t),
         gate,
         up,
-        lambda: None,
-    )
-    for step in range(count + 4):
-        if step < count:
-            gather.issue(step)
-        if 0 <= step - 2 < count:
-            gather.relay(step - 2)
-        if 0 <= step - 3 < count:
-            gather.spread(step - 3)
-        if 0 <= step - 4 < count:
-            gather.finish(step - 4)
-            compute[step - 4]()
+    )
+    for number in range(count - 1):
+        while steps.finished <= lasts[number]:
+            advance()
+        load(number)[0].start()
+        if number:
+            compute[number - 1]()
+    compute[count - 2]()
+    while steps.finished < len(units):
+        advance()
     for name in range(n):
         if name not in Kept.inside:
             pltpu.make_async_copy(keep[name], outs[name], save_sems.at[name]).wait()
@@ -913,8 +1033,9 @@
     down = shapes[count - 1]
     down = jax.ShapeDtypeStruct((down.shape[1] // 256, down.shape[0], 256), down.dtype)
     square = shards[1].shape[1]
+    units = units_of([s.shape for s in shards], 3)
     return pl.pallas_call(
-        functools.partial(forward_kernel, count),
+        functools.partial(forward_kernel, count, units),
         out_shape=shapes + [down],
         in_specs=[vmem] * (count + 5),
         out_specs=[anywhere] * (len(shapes) + 1),
@@ -925,10 +1046,10 @@
             pltpu.VMEM((8, square), jnp.float32),
             pltpu.VMEM((total, square), jnp.bfloat16),
             pltpu.VMEM((total, square), jnp.bfloat16),
-            pltpu.VMEM((square, square), jnp.bfloat16),
-            pltpu.VMEM((square, shards[9].shape[1]), jnp.bfloat16),
-            pltpu.SemaphoreType.DMA((count, 9)),
-            pltpu.SemaphoreType.DMA((count, 9)),
+            pltpu.VMEM((2, square, square), jnp.bfloat16),
+            pltpu.VMEM((2, square, shards[9].shape[1]), jnp.bfloat16),
+            pltpu.SemaphoreType.DMA((len(units), 9)),
+            pltpu.SemaphoreType.DMA((len(units), 9)),
             pltpu.SemaphoreType.DMA((count,)),
             pltpu.SemaphoreType.DMA((2, DOCS - 1)),
             pltpu.SemaphoreType.DMA((2, DOCS - 1)),
@@ -1757,8 +1878,11 @@
 
 
 def widen_kernel(*refs):
-    half = len(refs) // 2
-    for source, target in zip(refs[:half], refs[half:]):
+    half = (len(refs) - 5) // 2
+    smalls, lines = refs[half], refs[-4:]
+    for index, line in enumerate(lines):
+        line[...] = smalls[0, index : index + 1, 0 : line.shape[0]].reshape(line.shape)
+    for source, target in zip(refs[:half], refs[half + 1 : -4]):
         if len(source.shape) == 2:
             target[...] = source[...].astype(target.dtype)
             continue
@@ -1766,25 +1890,68 @@
             target[:, 256 * part : 256 * part + 256] = source[part].astype(target.dtype)
 
 
-def widen_call(sums, layer_out, hidden_grad):
-    operands = list(sums) + [layer_out, hidden_grad]
+def widen_call(sums, layer_out, hidden_grad, smalls, entries):
+    operands = list(sums) + [layer_out, hidden_grad, smalls]
     shapes = [jax.ShapeDtypeStruct((s.shape[1], s.shape[0] * s.shape[2]), jnp.float32) for s in sums]
     shapes.append(jax.ShapeDtypeStruct(layer_out.shape, layer_out.dtype))
     shapes.append(jax.ShapeDtypeStruct(hidden_grad.shape, jnp.float32))
+    shapes += [jax.ShapeDtypeStruct((size,), jnp.float32) for size in (smalls.shape[2],) * 3 + (entries,)]
     vmem = pl.BlockSpec(memory_space=pltpu.VMEM)
     return pl.pallas_call(
         widen_kernel,
         out_shape=shapes,
         in_specs=[vmem] * len(operands),
-        out_specs=[vmem] * len(operands),
+        out_specs=[vmem] * len(shapes),
         name="widen",
     )(*operands)
 
 
-def pack_small(norms, table):
-    rows = [n.astype(jnp.float32) for n in norms]
-    rows.append(jnp.pad(table.astype(jnp.float32), (0, 128 - table.shape[0])))
-    return jnp.pad(jnp.stack(rows), ((0, 12), (0, 0)))
+def prepare_kernel(rows, norms, table, segments, docs, small, chosen, chosen_t, spread):
+    small[...] = jnp.zeros_like(small)
+    for index, norm in enumerate(norms):
+        small[index : index + 1, :] = norm[...].reshape(1, norm.shape[0]).astype(jnp.float32)
+    entries = table.shape[0]
+    small[3:4, 0:entries] = table[...].reshape(1, entries).astype(jnp.float32)
+    first = pl.multiple_of(lax.axis_index("ctx") * rows, rows)
+    document = docs[:, pl.ds(first, 128)][:, 0:1]
+    ids = segments[...]
+    start = jnp.sum((ids < document).astype(jnp.int32), axis=1, keepdims=True)
+    length = jnp.sum((ids == document).astype(jnp.int32), axis=1, keepdims=True)
+    for target, axis in ((chosen, 0), (chosen_t, 1)):
+        row = lax.broadcasted_iota(jnp.int32, target.shape, axis)
+        column = lax.broadcasted_iota(jnp.int32, target.shape, 1 - axis)
+        here = jnp.where(row < length, row + start, -1)
+        target[...] = (here == column).astype(jnp.float32).astype(jnp.bfloat16)
+    most = spread.shape[2]
+    position = lax.broadcasted_iota(jnp.int32, (1, most), 1)
+    bucket = bucket_of(jnp.where(position == 0, 0, most - position))
+    slot = lax.broadcasted_iota(jnp.int32, spread.shape[1:], 0)
+    for half in range(2):
+        found = (slot == bucket + BUCKETS * half).astype(jnp.float32)
+        spread[half] = found.astype(jnp.bfloat16)
+
+
+def prepare_call(norms, table, segment_ids, encoder_docs, rows):
+    total = segment_ids.shape[1]
+    most = total // 2
+    count = len(norms)
+
+    def kernel(*refs):
+        prepare_kernel(rows, refs[:count], *refs[count:])
+
+    vmem = pl.BlockSpec(memory_space=pltpu.VMEM)
+    return pl.pallas_call(
+        kernel,
+        out_shape=[
+            jax.ShapeDtypeStruct((16, norms[0].shape[0]), jnp.float32),
+            jax.ShapeDtypeStruct((most, total), jnp.bfloat16),
+            jax.ShapeDtypeStruct((total, most), jnp.bfloat16),
+            jax.ShapeDtypeStruct((2, 2 * HD, most), jnp.bfloat16),
+        ],
+        in_specs=[vmem] * (count + 3),
+        out_specs=[vmem] * 4,
+        name="prepare",
+    )(*norms, table, segment_ids, encoder_docs)
 
 
 def by_document(
@@ -1810,26 +1977,10 @@
     out_grad,
 ):
     width = hidden_in.shape[2]
-    total = segment_ids.shape[1]
-    most = total // 2
     encoded = encoder_states[0]
-    small = pack_small((norm_self, norm_cross, norm_feed), bias_table)
-    document = lax.dynamic_slice_in_dim(
-        encoder_docs[0], lax.axis_index("ctx") * encoded.shape[0], 1, 0
-    )
-    segments = segment_ids[0]
-    start = jnp.sum((segments < document).astype(jnp.int32))
-    length = jnp.sum((segments == document).astype(jnp.int32))
-    row = lax.broadcasted_iota(jnp.int32, (most, total), 0)
-    column = lax.broadcasted_iota(jnp.int32, (most, total), 1)
-    chosen = ((row + start == column) & (row < length)).astype(jnp.bfloat16)
-
-    slot = jnp.arange(2 * HD, dtype=jnp.int32)
-    position = jnp.arange(most, dtype=jnp.int32)
-    bucket = bucket_of(lax.rem(most - position, most))
-    spread = jnp.stack(
-        [(slot[:, None] == bucket[None] + BUCKETS * half) for half in range(2)]
-    ).astype(jnp.bfloat16)
+    small, chosen, chosen_t, spread = prepare_call(
+        (norm_self, norm_cross, norm_feed), bias_table, segment_ids, encoder_docs, encoded.shape[0]
+    )
     results = forward_call(
         (
             small,
@@ -1880,13 +2031,12 @@
         )
     ]
     results = backward_call(
-        forward_side + [chosen.T, spread] + list(results[:12]) + [grad_fd], hidden_in.shape[1]
+        forward_side + [chosen_t, spread] + list(results[:12]) + [grad_fd], hidden_in.shape[1]
     )
     smalls, encoder_grad, layer_out, hidden_grad = results[11:]
-    fd, fg, fu, co, ck, cv, cq, so, sq, sk, sv, layer_out, hidden_grad = widen_call(
-        results[:11], layer_out, hidden_grad
-    )
-    smalls = smalls[0]
+    fd, fg, fu, co, ck, cv, cq, so, sq, sk, sv, layer_out, hidden_grad, *lines = widen_call(
+        results[:11], layer_out, hidden_grad, smalls, bias_table.shape[0]
+    )
     return (
         layer_out[None],
         hidden_grad[None],
@@ -1902,10 +2052,7 @@
         fg,
         fu,
         fd,
-        smalls[0],
-        smalls[1],
-        smalls[2],
-        smalls[3, : bias_table.shape[0]],
+        *lines,
     )
 
 

time: 412 us -> 373 us (0.905)
  Pallas kernels: 398 us -> 370 us
  other arithmetic: 6.98 us -> 0 us
  local copies, waits for them, and re-layouts: 5.72 us -> 1.33 us
    pallas_call x1 -> x2, Pallas kernels: 166 us -> 146 us  [the longest x1 144 us: forward_call(): pl.pallas_call(functools.partial(forward_kernel, count, units), out_shape...]
    pallas_call x1, Pallas kernels: 226 us -> 218 us  [backward_call(): pl.pallas_call(functools.partial(backward_kernel, shared), out_shape=full...]
where the time goes in v4:
time: 373 us; the launch traced here: 372 us
  Pallas kernels  370 us (99%)
    pallas_call x1, Pallas kernels, backward_call(): pl.pallas_call(functools.partial(backward_kernel, shared), out_shape=full...  218 us
    pallas_call x1, Pallas kernels, forward_call(): pl.pallas_call(functools.partial(forward_kernel, count, units), out_shape...  144 us

profile of v4, /device:TPU:0, one launch (start us, length us, event | category | flops | bytes accessed | tf_op | source)
XLA Modules:
  0.0 372.4 jit_solution(31782102174809730)
XLA Ops:
  0.7 1.9 prepare.1
  2.6 143.9 %forward.1 = (f32[128,128]{1,0:T(8,128)}, bf16[1024,1024]{1,0:T(8,128)(2,1)}, bf16[1024,1024]{1,0:T(8,128)(2,1)}, bf16[1024,1024]{1,0:T(8,128)(2,1)}, bf16[1024,...) custom-call(f32[16,128]{1,0:T(8,128)} %get-tuple-element.88.refs_0_,, ...), custom_call_target="tpu_custom_call" | custom-call | tf_op jit(solution)/shard_map/forward/pallas_call | solution.py:1037
  146.4 218.4 %backward.1 = (bf16[11,8,128,256]{3,2,1,0:T(8,128)(2,1)}, bf16[11,8,128,256]{3,2,1,0:T(8,128)(2,1)}, bf16[4,8,128,256]{3,2,1,0:T(8,128)(2,1)}, bf16[4,8,128,256]...) custom-call(f32[256,1024]{1,0:T(8,128)} %get-tuple-element.91.refs_0, ...), custom_call_target="tpu_custom_call" | custom-call | tf_op jit(solution)/shard_map/backward/pallas_call | solution.py:1866
  364.9 0.0 copy-start
  364.9 6.2 %widen.1 = (f32[352,1024]{1,0:T(8,128)}, f32[128,2816]{1,0:T(8,128)}, f32[128,2816]{1,0:T(8,128)}, f32[128,1024]{1,0:T(8,128)}, f32[128,1024]{1,0:T(8,128)}, /*i...) custom-call(bf16[4,352,256]{2,1,0:T(8,128)(2,1)} %get-tuple-element., ...), custom_call_target="tpu_custom_call" | custom-call | tf_op jit(solution)/shard_map/widen/pallas_call | solution.py:1900
  371.1 0.0 copy-done
  371.1 1.3 copy.39
Async XLA Ops:
  364.9 6.2 %copy-start = (f32[512,1024]{1,0:T(8,128)S(1)}, f32[512,1024]{1,0:T(8,128)}, u32[]{:S(2)}) copy-start(f32[512,1024]{1,0:T(8,128)} %get-tuple-element.142) | copy-start | bytes 6291460

commit v5 on v4

--- a/solution.py
+++ b/solution.py
@@ -1106,7 +1106,7 @@
     def core_copies(self, number):
         piece, both = self.pieces[number], self.buffers[number][0]
         return [
-            self.copy(number, q, piece.slot(2 * q + 1 - self.core), both.at[q], self.to_core)
+            self.copy(number, q, piece.slot(2 * q + 1 - self.core), both.at[q // 2, q % 2], self.to_core)
             for q in range(4)
         ]
 
@@ -1120,28 +1120,10 @@
     def first_copies(self, number):
         both, from_x, from_y = self.buffers[number][:3]
         low, high = self.halves(number)
-        copies = []
-        for other in range(2):
-            copies.append(
-                self.copy(
-                    number,
-                    4 + other,
-                    both.at[2 * other + 1 - self.along_x, :, low],
-                    from_x.at[other],
-                    self.to_x,
-                )
-            )
-        for other in range(2):
-            copies.append(
-                self.copy(
-                    number,
-                    6 + other,
-                    both.at[2 * (1 - self.along_y) + other, :, high],
-                    from_y.at[other],
-                    self.to_y,
-                )
-            )
-        return copies
+        return [
+            self.copy(number, 4, both.at[:, 1 - self.along_x, :, low], from_x, self.to_x),
+            self.copy(number, 6, both.at[1 - self.along_y, :, :, high], from_y, self.to_y),
+        ]
 
     def second_copies(self, number):
         both, unused_x, unused_y, late_x, late_y = self.buffers[number][:5]
@@ -1150,14 +1132,14 @@
             self.copy(
                 number,
                 8,
-                both.at[2 * (1 - self.along_y) + self.along_x, :, low],
+                both.at[1 - self.along_y, self.along_x, :, low],
                 late_y,
                 self.to_y,
             ),
             self.copy(
                 number,
                 9,
-                both.at[2 * self.along_y + 1 - self.along_x, :, high],
+                both.at[self.along_y, 1 - self.along_x, :, high],
                 late_x,
                 self.to_x,
             ),
@@ -1167,7 +1149,7 @@
         return self.copy(
             number,
             10,
-            self.buffers[number][0].at[self.block],
+            self.buffers[number][0].at[self.along_y, self.along_x],
             self.buffers[number][5],
             self.to_line,
         )
@@ -1176,7 +1158,7 @@
         return self.copy(
             number,
             11,
-            self.buffers[number][0].at[self.block],
+            self.buffers[number][0].at[self.along_y, self.along_x],
             self.buffers[number][6],
             self.to_middle,
         )
@@ -1209,29 +1191,28 @@
             for q, copy in enumerate(self.core_copies(number)):
                 copy.wait_recv()
                 self.own_load(number, q).wait()
-                add_rows(both.at[q], self.load[number].at[q % 2])
+                add_rows(both.at[q // 2, q % 2], self.load[number].at[q % 2])
                 if q < 2:
                     self.own_load(number, q + 2).start()
             for copy in self.first_copies(number):
                 copy.start()
         elif level == 2:
             copies = self.first_copies(number)
+            for copy in copies:
+                copy.wait_recv()
+                copy.wait_send()
             for other in range(2):
-                copies[other].wait_recv()
-                copies[other].wait_send()
-                add_rows(both.at[2 * other + self.along_x, :, low], from_x.at[other])
+                add_rows(both.at[other, self.along_x, :, low], from_x.at[other])
             for other in range(2):
-                copies[2 + other].wait_recv()
-                copies[2 + other].wait_send()
-                add_rows(both.at[2 * self.along_y + other, :, high], from_y.at[other])
+                add_rows(both.at[self.along_y, other, :, high], from_y.at[other])
             for copy in self.second_copies(number):
                 copy.start()
         elif level == 3:
             to_y, to_x = self.second_copies(number)
             to_y.wait_recv()
-            add_rows(both.at[self.block, :, low], late_y)
+            add_rows(both.at[self.along_y, self.along_x, :, low], late_y)
             to_x.wait_recv()
-            add_rows(both.at[self.block, :, high], late_x)
+            add_rows(both.at[self.along_y, self.along_x, :, high], late_x)
             to_y.wait_send()
             to_x.wait_send()
 
@@ -1243,7 +1224,7 @@
             @pl.when(self.inner)
             def _():
                 self.line_copy(number).wait_recv()
-                add_rows(both.at[self.block], on_line)
+                add_rows(both.at[self.along_y, self.along_x], on_line)
                 self.middle_copy(number).start()
         elif level == 5:
 
@@ -1256,7 +1237,7 @@
 
                 def one(index):
                     at = pl.ds(pl.multiple_of(index * step, step), step)
-                    on_line[:, at, :] = both[self.block, :, at, :] + on_middle[:, at, :]
+                    on_line[:, at, :] = both[self.along_y, self.along_x, :, at, :] + on_middle[:, at, :]
 
                 each(rows // step, one)
                 middle.wait_send()
@@ -1282,7 +1263,7 @@
 
 def buffer_shapes(tiles, rows, width, dtype):
     return [
-        pltpu.VMEM((4, tiles, rows, width), dtype),
+        pltpu.VMEM((2, 2, tiles, rows, width), dtype),
         pltpu.VMEM((2, tiles, rows // 2, width), dtype),
         pltpu.VMEM((2, tiles, rows // 2, width), dtype),
         pltpu.VMEM((tiles, rows // 2, width), dtype),
@@ -1322,7 +1303,8 @@
 
     def tick(self):
         before = [self.ready] + list(self.done)
-        for level, gap in enumerate(self.gaps):
+        for level in reversed(range(len(self.gaps))):
+            gap = self.gaps[level]
             limit = before[level]
             if level and limit < self.count:
                 limit = limit - gap + 1

time: 373 us -> 371 us (level)
  no operation moved by 1% of the time
where the time goes in v5:
time: 371 us
  Pallas kernels  369 us (99%)
    pallas_call x1, Pallas kernels, backward_call(): pl.pallas_call(functools.partial(backward_kernel, shared), out_shape=full...  217 us
    pallas_call x1, Pallas kernels, forward_call(): pl.pallas_call(functools.partial(forward_kernel, count, units), out_shape...  144 us

profile of v5, /device:TPU:0, one launch (start us, length us, event | category | flops | bytes accessed | tf_op | source)
XLA Modules:
  0.0 370.6 jit_solution(10729353584672991414)
XLA Ops:
  0.7 1.9 prepare.1
  2.6 143.9 %forward.1 = (f32[128,128]{1,0:T(8,128)}, bf16[1024,1024]{1,0:T(8,128)(2,1)}, bf16[1024,1024]{1,0:T(8,128)(2,1)}, bf16[1024,1024]{1,0:T(8,128)(2,1)}, bf16[1024,...) custom-call(f32[16,128]{1,0:T(8,128)} %get-tuple-element.88.refs_0_,, ...), custom_call_target="tpu_custom_call" | custom-call | tf_op jit(solution)/shard_map/forward/pallas_call | solution.py:1037
  146.4 216.6 %backward.1 = (bf16[11,8,128,256]{3,2,1,0:T(8,128)(2,1)}, bf16[11,8,128,256]{3,2,1,0:T(8,128)(2,1)}, bf16[4,8,128,256]{3,2,1,0:T(8,128)(2,1)}, bf16[4,8,128,256]...) custom-call(f32[256,1024]{1,0:T(8,128)} %get-tuple-element.91.refs_0, ...), custom_call_target="tpu_custom_call" | custom-call | tf_op jit(solution)/shard_map/backward/pallas_call | solution.py:1848
  363.0 0.0 copy-start
  363.0 6.2 %widen.1 = (f32[352,1024]{1,0:T(8,128)}, f32[128,2816]{1,0:T(8,128)}, f32[128,2816]{1,0:T(8,128)}, f32[128,1024]{1,0:T(8,128)}, f32[128,1024]{1,0:T(8,128)}, /*i...) custom-call(bf16[4,352,256]{2,1,0:T(8,128)(2,1)} %get-tuple-element., ...), custom_call_target="tpu_custom_call" | custom-call | tf_op jit(solution)/shard_map/widen/pallas_call | solution.py:1882
  369.2 0.0 copy-done
  369.2 1.3 copy.39
Async XLA Ops:
  363.0 6.2 %copy-start = (f32[512,1024]{1,0:T(8,128)S(1)}, f32[512,1024]{1,0:T(8,128)}, u32[]{:S(2)}) copy-start(f32[512,1024]{1,0:T(8,128)} %get-tuple-element.142) | copy-start | bytes 6291460
